TPU v7x, 512 devices: a whole 4x8x8 slice. The times are simulated.
512 devices in a mesh: dp: 8 (over z), section: 4 (over x), patch: 16 (over y, core).
Axes of the slice: x: 4, y: 8, z: 8, core: 2. Of those that a mesh axis runs over, the one named last changes fastest.
Arguments:
- maps: bfloat16 [4, 8, 1536, 256], P(None, 'dp', 'patch'), may hold values from -6 to 6
- upstream: bfloat16 [4, 8, 1536, 256], P(None, 'dp', 'patch'), may hold values from -6 to 6
- weights: bfloat16 [4, 2304, 256], P('section'), may hold values from -0.125 to 0.125
- neighbours: int32 [9, 1536], P(None, 'patch'), may hold values from 0 to 1535, as said below
Outputs:
- input_grads: bfloat16 [4, 4, 8, 1536, 256], P('section', None, 'dp', 'patch')
- weight_grads: bfloat16 [4, 2304, 256], P('section')
Inputs may be any that keep to these rules, and one draw needn't show every extreme that they name: neighbours[0, p] = p; every entry is (p + d) mod 1536 with -32 <= d <= 32, and both d = 32 and d = -32 occur in every draw.
All inputs are finite; a program needn't handle non-finite values.
Results may differ from a plain program's by a relative error of at most 0.0063.
Values may be sent and summed in bfloat16 or wider, within the bound.
No kernel may reach another device: no remote copies, remote signals or barrier semaphores. Data moves between devices by JAX's collectives and lax.ppermute only.
A program may use at most 64 MiB of HBM per device.

v0:
```python
import jax
import jax.numpy as jnp
from jax import lax
from jax.sharding import PartitionSpec as P

HALO = 32


def extended_2(block, sides, width):
    for axis, dim in sides:
        count = lax.axis_size(axis)
        forward = [(i, i + 1) for i in range(count - 1)]
        forward.append((count - 1, 0))
        backward = [(target, source) for source, target in forward]
        low = lax.ppermute(
            lax.slice_in_dim(block, block.shape[dim] - width, None, axis=dim), axis, forward
        )
        high = lax.ppermute(lax.slice_in_dim(block, 0, width, axis=dim), axis, backward)
        block = jnp.concatenate([low, block, high], axis=dim)
    return block


def from_behind(shard, axis, by):
    size = lax.axis_size(axis)
    pairs = [(i, i + by) for i in range(size) if 0 <= i + by < size]
    return lax.ppermute(shard, axis, pairs)


def body(maps, upstream, weights, neighbours):
    micro = maps.shape[0]
    pix = maps.shape[2]
    chans = maps.shape[3]
    taps = neighbours.shape[0]
    sections = lax.axis_size("section")
    patches = lax.axis_size("patch")
    section_id = lax.axis_index("section")
    patch_id = lax.axis_index("patch")
    total = pix * patches
    local = jnp.mod(neighbours - patch_id * pix + HALO, total)
    index_rows = local.T.reshape(-1)
    w_flat = weights[0]
    w_taps = w_flat.reshape((taps, chans, chans))
    width = pix + 2 * HALO
    saved_ext = jnp.zeros((micro, width, chans), jnp.bfloat16)
    saved_tanh = jnp.zeros((micro, pix, chans), jnp.float32)
    incoming = jnp.zeros((pix, chans), jnp.bfloat16)
    for tick in range(micro + sections - 1):
        slot = tick - section_id
        valid = (slot >= 0) & (slot < micro)
        clipped = jnp.clip(slot, 0, micro - 1)
        current = jnp.where(section_id == 0, maps[min(tick, micro - 1), 0], incoming)
        extended = extended_2(current, (("patch", 0),), HALO)
        gathered = extended[index_rows].reshape((pix, taps * chans))
        act = jnp.dot(gathered, w_flat, preferred_element_type=jnp.float32)
        squash = jnp.tanh(act)
        result = (current.astype(jnp.float32) + squash).astype(jnp.bfloat16)
        saved_ext = saved_ext.at[clipped].set(jnp.where(valid, extended, saved_ext[clipped]))
        saved_tanh = saved_tanh.at[clipped].set(jnp.where(valid, squash, saved_tanh[clipped]))
        incoming = from_behind(result, "section", 1)
    grad_in = jnp.zeros((pix, chans), jnp.bfloat16)
    weight_acc = jnp.zeros((taps * chans, chans), jnp.float32)
    grads_out = jnp.zeros((micro, 1, pix, chans), jnp.bfloat16)
    for tick in range(micro + sections - 1):
        slot = tick - (sections - 1 - section_id)
        valid = (slot >= 0) & (slot < micro)
        clipped = jnp.clip(slot, 0, micro - 1)
        grad = jnp.where(section_id == sections - 1, upstream[min(tick, micro - 1), 0], grad_in)
        squash = saved_tanh[clipped]
        pre = (grad.astype(jnp.float32) * (1.0 - squash * squash)).astype(jnp.bfloat16)
        gathered = saved_ext[clipped][index_rows].reshape((pix, taps * chans))
        term = lax.dot_general(
            gathered, pre, (((0,), (0,)), ((), ())), preferred_element_type=jnp.float32
        )
        weight_acc = weight_acc + jnp.where(valid, term, 0.0)
        parts = jnp.einsum("qo,kio->qki", pre, w_taps, preferred_element_type=jnp.float32)
        spread = (
            jnp.zeros((width, chans), jnp.float32)
            .at[index_rows]
            .add(parts.reshape((pix * taps, chans)))
        )
        rims = jnp.concatenate([spread[:HALO], spread[pix + HALO :]], 0)
        returned = extended_2(rims, (("patch", 0),), HALO)
        own = spread[HALO : HALO + pix]
        own = own.at[:HALO].add(returned[:HALO])
        own = own.at[pix - HALO :].add(returned[3 * HALO :])
        dx_level = (grad.astype(jnp.float32) + own).astype(jnp.bfloat16)
        grads_out = grads_out.at[clipped, 0].set(jnp.where(valid, dx_level, grads_out[clipped, 0]))
        grad_in = from_behind(dx_level, "section", -1)
    summed = lax.psum(weight_acc, ("dp", "patch")).astype(jnp.bfloat16)
    return (grads_out[None], summed[None])


def solution(mesh):
    in_specs = (
        P(None, "dp", "patch", None),
        P(None, "dp", "patch", None),
        P("section", None, None),
        P(None, "patch"),
    )
    out_specs = (P("section", None, "dp", "patch", None), P("section", None, None))
    return jax.shard_map(body, mesh=mesh, in_specs=in_specs, out_specs=out_specs, check_vma=False)
```

profile of v0, /device:TPU:1, one launch (start us, length us, event | category | flops | bytes accessed | tf_op | source)
XLA Modules:
  0.0 830.3 jit_solution(4863639710440151621)
XLA Ops:
  4.2 4.2 collective-permute-start.1
  36.8 4.0 collective-permute-start.5
  42.0 4.4 collective-permute-start.7
  52.2 4.0 collective-permute-start.8
  57.4 4.4 collective-permute-start.10
  67.6 4.0 collective-permute-start.11
  72.8 4.4 collective-permute-start.13
  83.0 4.0 collective-permute-start.14
  88.2 4.4 collective-permute-start.16
  98.4 4.4 collective-permute-start.17
  103.6 4.4 collective-permute-start.19
  116.8 6.1 scatter_custom_fusion
  140.3 6.1 scatter_custom_fusion.1
  185.3 6.1 scatter_custom_fusion.2
  209.5 6.6 scatter_custom_fusion.3
  218.6 4.6 collective-permute-start.30
  227.5 3.8 fusion.5
  235.0 6.1 scatter_custom_fusion.4
  241.9 4.6 collective-permute-start.33
  261.3 6.6 scatter_custom_fusion.5
  270.4 4.5 collective-permute-start.36
  290.3 6.6 scatter_custom_fusion.6
  298.4 521.6 %all-reduce.1 = bf16[2304,256]{1,0:T(8,128)(2,1)} all-reduce(f32[2304,256]{1,0:T(8,128)S(1)} %fusion.3), channel_id=1, replica_groups=mesh['dp'=8,'section'=4,'patch'=16] {'dp','patch'}, use_global_device_ids=true, to_apply=%region_21.22 | all-reduce | flops 589824 | bytes 3538944 | tf_op jit(solution)/shard_map/psum | solution.py:89
  820.9 5.7 collective-permute-start.39
  (273 shorter events, 192.5 us)
Async XLA Ops:
  1.6 18.3 %collective-permute-start = (bf16[32,256]{1,0:T(8,128)(2,1)S(1)}, bf16[32,256]{1,0:T(8,128)(2,1)S(1)}, u32[]{:S(2)}, u32[]{:S(2)}) collective-permute-start(bf16[32,256]{1,0:T(8,128)(2,1)S(1)} %get-tuple-element.483), channel_id=1, source_target_pairs={{0,1},{1,2},{2,3},{3,4},{4,5},{5,6},{6,7},{7,8},{8,9},{9,10},{10,1... | collective-permute-start | bytes 49160 | tf_op jit(solution)/shard_map/ppermute | solution.py:15
  4.2 15.6 %collective-permute-start.1 = (bf16[32,256]{1,0:T(8,128)(2,1)S(1)}, bf16[32,256]{1,0:T(8,128)(2,1)S(1)}, u32[]{:S(2)}, u32[]{:S(2)}) collective-permute-start(bf16[32,256]{1,0:T(8,128)(2,1)S(1)} %get-tuple-element.484), channel_id=1, source_target_pairs={{1,0},{2,1},{3,2},{4,3},{5,4},{6,5},{7,6},{8,7},{9,8},{10,9},{11,1... | collective-permute-start | bytes 49160 | tf_op jit(solution)/shard_map/ppermute | solution.py:18
  42.0 5.1 collective-permute-start.6
  42.0 5.2 collective-permute-start.7
  57.4 5.2 collective-permute-start.10
  67.6 5.1 collective-permute-start.11
  72.8 5.2 collective-permute-start.13
  83.0 5.1 collective-permute-start.14
  88.2 5.1 collective-permute-start.15
  88.2 5.2 collective-permute-start.16
  98.4 5.1 collective-permute-start.17
  103.6 5.2 collective-permute-start.19
  129.5 6.1 collective-permute-start.22
  151.3 31.8 %collective-permute-start.25 = (bf16[96,256]{1,0:T(8,128)(2,1)S(1)}, bf16[96,256]{1,0:T(8,128)(2,1)S(1)}, u32[]{:S(2)}, u32[]{:S(2)}) collective-permute-start(bf16[96,256]{1,0:T(8,128)(2,1)S(1)} %get-tuple-element.447), channel_id=1, source_target_pairs={{16,0},{32,16},{48,32},{17,1},{33,17},{49,33},{18,2},{34,18},{50,3... | collective-permute-start | bytes 147464 | tf_op jit(solution)/shard_map/ppermute | solution.py:26
  198.0 6.5 collective-permute-start.28
  216.9 6.3 collective-permute-start.29
  218.6 5.4 collective-permute-start.30
  241.1 5.4 collective-permute-start.32
  241.9 5.4 collective-permute-start.33
  268.7 6.3 collective-permute-start.35
  270.4 5.4 collective-permute-start.36
  278.0 5.2 collective-permute-start.37
  298.4 528.3 %collective-permute-start.38 = (f32[32,256]{1,0:T(8,128)}, f32[32,256]{1,0:T(8,128)}, u32[]{:S(2)}, u32[]{:S(2)}) collective-permute-start(f32[32,256]{1,0:T(8,128)} %get-tuple-element.458), channel_id=1, source_target_pairs={{0,1},{1,2},{2,3},{3,4},{4,5},{5,6},{6,7},{7,8},{8,9},{9,10},{10,1... | collective-permute-start | bytes 98312 | tf_op jit(solution)/shard_map/ppermute | solution.py:15
  820.9 6.8 collective-permute-start.39
  (37 other events, 275.2 us)
where the time goes:
time: 841 us; the launch traced here: 830 us
  blocking collectives  522 us (62%)
  local copies, waits for them, and re-layouts  94.9 us (11%)
  starting transfers between devices  92.5 us (11%)
  other arithmetic  79 us (9%)
  matrix products  24.8 us (3%)
  waiting for transfers between devices  15.1 us (2%)
    psum x1, blocking collectives, body(): summed = lax.psum(weight_acc, ('dp', 'patch')).astype(jnp.bfloat16)  522 us
    ppermute x14, starting transfers between devices, extended_2(): lax.ppermute(lax.slice_in_dim(block, 0, width, axis=dim), axis, backward)  59.4 us
    scatter-add x7, other arithmetic, body(): spread = jnp.zeros((width, chans), jnp.float32).at[index_rows].add(parts....  44.2 us
    ppermute x12, starting transfers between devices, from_behind(): return lax.ppermute(shard, axis, pairs)  30.1 us
    gather x7, local copies, waits for them, and re-layouts, body(): gathered = extended[index_rows].reshape((pix, taps * chans))  24.2 us
    gather x7, local copies, waits for them, and re-layouts, body(): gathered = saved_ext[clipped][index_rows].reshape((pix, taps * chans))  24.2 us
  transfers between devices with their start and end apart: 40, of which 22 were waited for; matrix products, arithmetic and copies ran while one was open for 9% of the time, Pallas kernels for 0%

commit v1 on v0

v1 whole, which is shorter than its diff:
```python
import functools

import jax
import jax.numpy as jnp
from jax import lax
from jax.experimental import pallas as pl
from jax.experimental.pallas import tpu as pltpu
from jax.sharding import Mesh
from jax.sharding import PartitionSpec as P

HALO = 32
TAPS = 9
C = 256
PIX = 96
LEVELS = 4
REACH = 2 * LEVELS * HALO
TILE = 64
PAD = 32
WIN = PIX + 2 * REACH
ROWS = WIN + 2 * PAD
HALF = TAPS * C // 2
BF = jnp.bfloat16
F32 = jnp.float32
NT = (((1,), (1,)), ((), ()))

FWD_TILES = ((0, 9), (1, 9), (1, 8), (2, 8))
PRE_ROWS = ((224, 384), (192, 416), (160, 448), (128, 480))
BWD_TILES = ((4, 6), (3, 6), (3, 7), (2, 7))
OWN = REACH
HROWS, PROWS, GROWS = PIX, PIX + HALO, PIX
MSG = HROWS + PROWS + GROWS


def stack_kernel(core_ref, m3a, m2a, m1a, own, m1b, m2b, m3b, w_mine, w_other, out_ref, offp_ref,
                 w_buf, h_buf, off_buf, s_buf, st_buf, gat, der, pre_buf, g_buf, sems):
    core = core_ref[0]
    copies = []
    for n, (src, half) in enumerate(((w_mine, core), (w_other, 1 - core))):
        row = pl.multiple_of(half * HALF, HALF)
        copies.append(pltpu.make_async_copy(src, w_buf.at[:, pl.ds(row, HALF), :], sems.at[n]))
        copies[-1].start()

    h_buf[...] = jnp.zeros_like(h_buf)
    off_buf[...] = jnp.zeros_like(off_buf)
    pre_buf[...] = jnp.zeros_like(pre_buf)
    g_buf[...] = jnp.zeros_like(g_buf)
    at = PAD
    for piece in (m3a, m2a, m1a, own, m1b, m2b, m3b):
        n = piece.shape[0]
        h_buf[0, at:at + n, :] = piece[:, :C]
        off_buf[at:at + n, :] = piece[:, C:C + 128].astype(F32)
        if piece.shape[1] > C + 128:
            g_buf[at:at + n, :] = piece[:, C + 128:]
        at += n

    rel = (lax.broadcasted_iota(jnp.int32, (TILE, 128), 1)
           - lax.broadcasted_iota(jnp.int32, (TILE, 128), 0) - HALO).astype(F32)

    def build_s(t, carry):
        d = off_buf[pl.ds(pl.multiple_of(t * TILE + PAD, PAD), TILE), :]
        for k in range(1, TAPS):
            hit = rel == d[:, k:k + 1]
            s_buf[t, (k - 1) * TILE:k * TILE, :] = jnp.where(hit, 1.0, 0.0).astype(BF)
        return carry

    lax.fori_loop(0, FWD_TILES[0][1], build_s, 0)

    def build_st(t, carry):
        d = jnp.transpose(off_buf[pl.ds(pl.multiple_of(t * TILE, TILE), 128), :])
        for k in range(1, TAPS):
            hit = -rel == d[k:k + 1, :]
            st_buf[t, (k - 1) * TILE:k * TILE, :] = jnp.where(hit, 1.0, 0.0).astype(BF)
        return carry

    lax.fori_loop(BWD_TILES[3][0], BWD_TILES[3][1], build_st, 0)

    for copy in copies:
        copy.wait()

    for level in range(LEVELS):
        first, last = FWD_TILES[level]

        def gather(t, carry, level=level):
            src = h_buf[level, pl.ds(pl.multiple_of(t * TILE, TILE), 2 * TILE), :]
            dst = pl.ds(pl.multiple_of(t * TILE, TILE), TILE)
            rows = jnp.dot(s_buf[t], src, preferred_element_type=F32).astype(BF)
            gat[dst, :C] = src[PAD:PAD + TILE]
            for k in range(1, TAPS):
                gat[dst, k * C:(k + 1) * C] = rows[(k - 1) * TILE:k * TILE]
            return carry

        lax.fori_loop(first, last, gather, 0)
        lo, hi = first * TILE, last * TILE
        act = jnp.dot(gat[lo:hi, :], w_buf[level], preferred_element_type=F32)
        squash = jnp.tanh(act)
        der[level, lo:hi, :] = 1.0 - squash * squash
        if level + 1 < LEVELS:
            h_buf[level + 1, PAD + lo:PAD + hi, :] = (
                h_buf[level, PAD + lo:PAD + hi, :].astype(F32) + squash).astype(BF)
        out_ref[level, :HROWS, :] = h_buf[level, PAD + OWN:PAD + OWN + PIX, :]

    for level in range(LEVELS - 1, -1, -1):
        lo, hi = PRE_ROWS[level]
        pre_buf[PAD + lo:PAD + hi, :] = (
            g_buf[PAD + lo:PAD + hi, :].astype(F32) * der[level, lo:hi, :]).astype(BF)
        first, last = BWD_TILES[level]

        def spread(t, carry):
            src = pre_buf[pl.ds(pl.multiple_of(t * TILE, TILE), 2 * TILE), :]
            dst = pl.ds(pl.multiple_of(t * TILE, TILE), TILE)
            rows = jnp.dot(st_buf[t], src, preferred_element_type=F32).astype(BF)
            gat[dst, :C] = src[PAD:PAD + TILE]
            for k in range(1, TAPS):
                gat[dst, k * C:(k + 1) * C] = rows[(k - 1) * TILE:k * TILE]
            return carry

        lax.fori_loop(first, last, spread, 0)
        lo, hi = first * TILE, last * TILE
        total = g_buf[PAD + lo:PAD + hi, :].astype(F32)
        for k in range(TAPS):
            total = total + lax.dot_general(gat[lo:hi, k * C:(k + 1) * C],
                                            w_buf[level, k * C:(k + 1) * C, :], NT,
                                            preferred_element_type=F32)
        g_buf[PAD + lo:PAD + hi, :] = total.astype(BF)
        start = pl.multiple_of(PAD + OWN - HALO + HALO * core, HALO)
        out_ref[level, HROWS:HROWS + PROWS, :] = pre_buf[pl.ds(start, PROWS), :]
        out_ref[level, HROWS + PROWS:, :] = g_buf[PAD + OWN:PAD + OWN + PIX, :]

    start = pl.multiple_of(PAD + OWN - HALO - PIX * core, HALO)
    offp_ref[...] = off_buf[pl.ds(start, 2 * PROWS), :]


def grad_kernel(core_ref, mine, other, offp, out_ref, gin_ref, st_buf, p_buf, h_buf, t_buf):
    core = core_ref[0]
    micro = mine.shape[0]
    pair = 2 * PIX
    gin_ref[...] = mine[:, HROWS + PROWS:, :]
    for c in range(2):
        @pl.when(core == c)
        def _(c=c):
            both = (mine, other) if c == 0 else (other, mine)
            for m in range(micro):
                for n, ref in enumerate(both):
                    p_buf[n * PROWS:(n + 1) * PROWS, m * 128:(m + 1) * 128] = (
                        ref[m, HROWS:HROWS + PROWS, c * 128:(c + 1) * 128])
                    h_buf[m * pair + n * PIX:m * pair + (n + 1) * PIX, :] = ref[m, :HROWS, :]
    rel = (lax.broadcasted_iota(jnp.int32, (pair, 2 * PROWS), 0)
           - lax.broadcasted_iota(jnp.int32, (pair, 2 * PROWS), 1) + HALO).astype(F32)
    offt = jnp.transpose(offp[...])
    h_t = jnp.transpose(h_buf[...].astype(F32)).astype(BF)
    pre = p_buf[...]
    for k in range(TAPS):
        if k == 0:
            spread = pre[HALO:HALO + pair]
        else:
            hit = jnp.where(rel == offt[k:k + 1, :], 1.0, 0.0).astype(BF)
            spread = jnp.dot(hit, pre, preferred_element_type=F32).astype(BF)
        for m in range(micro):
            t_buf[m * pair:(m + 1) * pair, :] = spread[:, m * 128:(m + 1) * 128]
        block = jnp.dot(h_t, t_buf[...], preferred_element_type=F32)
        out_ref[k * C:(k + 1) * C, :] = block.astype(BF)
    out_ref[TAPS * C:, :] = jnp.zeros((out_ref.shape[0] - TAPS * C, 128), BF)


def sum_kernel(x_ref, out_ref):
    total = jnp.sum(x_ref[...].astype(F32), axis=0).astype(BF)
    out_ref[...] = jnp.broadcast_to(total[None], out_ref.shape)


def join_kernel(core_ref, mine, other, out_ref):
    for c in range(2):
        @pl.when(core_ref[0] == c)
        def _(c=c):
            rows = out_ref.shape[0]
            out_ref[:, c * 128:(c + 1) * 128] = mine[:rows]
            out_ref[:, (1 - c) * 128:(2 - c) * 128] = other[:rows]


VMEM = pl.BlockSpec(memory_space=pltpu.VMEM)
SMEM = pl.BlockSpec(memory_space=pltpu.SMEM)
ANY = pl.BlockSpec(memory_space=pl.ANY)
INTERPRET = False


def call(kernel, out_shape, in_specs, scratch=(), flops=0, nbytes=0):
    many = isinstance(out_shape, (tuple, list))
    return pl.pallas_call(
        kernel,
        out_shape=out_shape,
        in_specs=in_specs,
        out_specs=[VMEM] * len(out_shape) if many else VMEM,
        scratch_shapes=list(scratch),
        interpret=INTERPRET,
        cost_estimate=pl.CostEstimate(flops=flops, bytes_accessed=nbytes, transcendentals=0),
        compiler_params=pltpu.CompilerParams(vmem_limit_bytes=48 << 20),
    )


def shift(axis_size, by):
    return [(i, (i + by) % axis_size) for i in range(axis_size)]


def body(maps, upstream, weights, neighbours):
    micro = maps.shape[0]
    section = lax.axis_index("section")
    core = lax.axis_index("core")
    patches = lax.axis_size("py") * lax.axis_size("core")
    patch = lax.axis_index("py") * lax.axis_size("core") + core
    npix = PIX * patches
    cores = core.reshape((1,)).astype(jnp.int32)

    half = lax.dynamic_slice_in_dim(weights[0], core * HALF, HALF, axis=0)
    w_mine = lax.all_gather(half, "section")
    w_other = lax.ppermute(w_mine, "core", shift(2, 1))

    place = patch * PIX + jnp.arange(PIX, dtype=jnp.int32)
    offsets = jnp.mod(neighbours - place[None, :] + HALO, npix) - HALO
    offsets = jnp.pad(offsets.astype(BF).T, ((0, 0), (0, 128 - TAPS)))
    start = lax.dynamic_index_in_dim(maps, section, 0, keepdims=False)[0]
    top = lax.dynamic_index_in_dim(upstream, section, 0, keepdims=False)[0]
    own = jnp.concatenate([start, offsets, top], axis=1)
    edge = 2 * HALO
    send = functools.partial(lax.ppermute, axis_name=("py", "core"))
    m1a = send(own, perm=shift(patches, 1))
    m1b = send(own, perm=shift(patches, -1))
    m2a = send(own, perm=shift(patches, 2))
    m2b = send(own, perm=shift(patches, -2))
    m3a = send(own[PIX - edge:, :C + 128], perm=shift(patches, 3))
    m3b = send(own[:edge, :C + 128], perm=shift(patches, -3))

    tiles = FWD_TILES[0][1]
    out, offp = call(
        stack_kernel,
        [jax.ShapeDtypeStruct((LEVELS, MSG, C), BF), jax.ShapeDtypeStruct((2 * PROWS, 128), F32)],
        [SMEM] + [VMEM] * 7 + [ANY] * 2,
        [
            pltpu.VMEM((LEVELS, TAPS * C, C), BF),
            pltpu.VMEM((LEVELS, ROWS, C), BF),
            pltpu.VMEM((ROWS, 128), F32),
            pltpu.VMEM((tiles, (TAPS - 1) * TILE, 2 * TILE), BF),
            pltpu.VMEM((BWD_TILES[3][1], (TAPS - 1) * TILE, 2 * TILE), BF),
            pltpu.VMEM((tiles * TILE, TAPS * C), BF),
            pltpu.VMEM((LEVELS, tiles * TILE, C), F32),
            pltpu.VMEM((ROWS, C), BF),
            pltpu.VMEM((ROWS, C), BF),
            pltpu.SemaphoreType.DMA((2,)),
        ],
        flops=6 * 10**9, nbytes=6 * 10**6,
    )(cores, m3a, m2a, m1a, own, m1b, m2b, m3b, w_mine, w_other)

    mine = lax.all_to_all(out, "section", 0, 0, tiled=True)
    other = lax.ppermute(mine[:, :HROWS + PROWS], "core", shift(2, 1))
    chips = lax.axis_size("dp") * lax.axis_size("py")
    rows = (TAPS + 1) * C
    part, gin = call(
        grad_kernel,
        [jax.ShapeDtypeStruct((rows, 128), BF), jax.ShapeDtypeStruct((micro, PIX, C), BF)],
        [SMEM] + [VMEM] * 3,
        [
            pltpu.VMEM((2 * PIX, 2 * PROWS), BF),
            pltpu.VMEM((2 * PROWS, micro * 128), BF),
            pltpu.VMEM((micro * 2 * PIX, C), BF),
            pltpu.VMEM((micro * 2 * PIX, 128), BF),
        ],
        flops=10**9, nbytes=2 * 10**6,
    )(cores, mine, other, offp)
    pieces = lax.all_to_all(part.reshape((chips, rows // chips, 128)), ("dp", "py"), 0, 0, tiled=True)
    total = call(
        sum_kernel, jax.ShapeDtypeStruct(pieces.shape, BF), [VMEM], nbytes=10**6,
    )(pieces)
    full = lax.all_to_all(total, ("dp", "py"), 0, 0, tiled=True).reshape((rows, 128))
    swapped = lax.ppermute(full, "core", shift(2, 1))
    summed = call(
        join_kernel, jax.ShapeDtypeStruct((TAPS * C, C), BF), [SMEM, VMEM, VMEM], nbytes=2 * 10**6,
    )(cores, full, swapped)
    return (gin[None, :, None], summed[None])


def solution(mesh):
    size = dict(mesh.shape)
    grid = (size["dp"], size["section"], size["patch"] // 2, 2)
    fine = Mesh(mesh.devices.reshape(grid), ("dp", "section", "py", "core"))
    patch = ("py", "core")
    in_specs = (
        P(None, "dp", patch, None),
        P(None, "dp", patch, None),
        P("section", None, None),
        P(None, patch),
    )
    out_specs = (P("section", None, "dp", patch, None), P("section", None, None))
    return jax.shard_map(body, mesh=fine, in_specs=in_specs, out_specs=out_specs, check_vma=False)
```

time: 841 us -> 194 us (0.23); the launches traced: 830 us -> 193 us
  blocking collectives: 522 us -> 67.9 us
  local copies, waits for them, and re-layouts: 94.9 us -> 6.11 us
  other arithmetic: 79 us -> 0.87 us
  starting transfers between devices: 92.5 us -> 28.6 us
  waiting for transfers between devices: 15.1 us -> 54.3 us
  matrix products: 24.8 us -> 0 us
  Pallas kernels: 0 us -> 20.9 us
  between operations: 2.33 us -> 14.2 us
    psum x1 -> x0, blocking collectives: 522 us -> none  [body(): summed = lax.psum(weight_acc, ('dp', 'patch')).astype(jnp.bfloat16)]
    all_to_all x0 -> x3, blocking collectives: none -> 67.9 us  [the longest x1 29.8 us: body(): lax.all_to_all(part.reshape((chips, rows // chips, 128)), ('dp', 'py'), 0...]
    ppermute x40 -> x9, starting transfers between devices: 92.5 us -> 28.6 us  [the longest x1 6.33 us: body(): swapped = lax.ppermute(full, 'core', shift(2, 1))]
    gather x14 -> x0, local copies, waits for them, and re-layouts: 48.4 us -> none  [the longest x7 24.2 us: body(): gathered = extended[index_rows].reshape((pix, taps * chans))]
    scatter-add x21 -> x0, other arithmetic: 46.5 us -> none  [the longest x7 44.2 us: body(): spread = jnp.zeros((width, chans), jnp.float32).at[index_rows].add(parts....]
    all_gather x0 -> x1, waiting for transfers between devices: none -> 45 us  [body(): w_mine = lax.all_gather(half, 'section')]
    reshape x22 -> x0, local copies, waits for them, and re-layouts: 25.4 us -> none  [the longest x7 13 us: body(): parts.reshape((pix * taps, chans))]
    dot_general x21 -> x0, matrix products: 24.8 us -> none  [the longest x7 13.5 us: body(): lax.dot_general(gathered, pre, (((0,), (0,)), ((), ())), preferred_elemen...]
  transfers between devices with their start and end apart: 40 -> 10, of which waited for: 22 -> 5; matrix products, arithmetic and copies ran while one was open for 9% -> 2% of each run, Pallas kernels for 0% -> 0%
where the time goes in v1:
time: 194 us; the launch traced here: 193 us
  blocking collectives  67.9 us (35%)
  waiting for transfers between devices  54.3 us (28%)
  starting transfers between devices  28.6 us (15%)
  Pallas kernels  20.9 us (11%)
  between operations  14.2 us (7%)
  local copies, waits for them, and re-layouts  6.11 us (3%)
    all_gather x1, waiting for transfers between devices, body(): w_mine = lax.all_gather(half, 'section')  45 us
    all_to_all x1, blocking collectives, body(): lax.all_to_all(part.reshape((chips, rows // chips, 128)), ('dp', 'py'), 0...  29.8 us
    all_to_all x1, blocking collectives, body(): lax.all_to_all(total, ('dp', 'py'), 0, 0, tiled=True).reshape((rows, 128))  25.5 us
    pallas_call x1, Pallas kernels, body(): call(stack_kernel, [jax.ShapeDtypeStruct((LEVELS, MSG, C), BF), jax.Shape...  16.8 us
    all_to_all x1, blocking collectives, body(): mine = lax.all_to_all(out, 'section', 0, 0, tiled=True)  12.6 us
    ppermute x1, starting transfers between devices, body(): swapped = lax.ppermute(full, 'core', shift(2, 1))  6.33 us
    ppermute x1, starting transfers between devices, body(): m2b = send(own, perm=shift(patches, -2))  5.67 us
    ppermute x1, waiting for transfers between devices, body(): m2a = send(own, perm=shift(patches, 2))  5.59 us
  transfers between devices with their start and end apart: 10, of which 5 were waited for; matrix products, arithmetic and copies ran while one was open for 2% of the time, Pallas kernels for 0%

profile of v1, /device:TPU:1, one launch (start us, length us, event | category | flops | bytes accessed | tf_op | source)
XLA Modules:
  0.0 192.9 jit_solution(7128914884893814008)
XLA Ops:
  7.2 1.2 copy-done
  8.4 0.9 constant_dynamic-slice_fusion
  9.3 45.0 %all-gather.2.cloned.1.call-done.w_mine = bf16[4,1152,256]{2,1,0:T(8,128)(2,1)} async-done(((bf16[1,1152,256]{2,1,0:T(8,128)(2,1)}), bf16[4,1152,256]{2,1,0:T(8,128)(2,1)}) %all-gather.2.cloned.1.call-update) | async-done | bytes 2359312 | tf_op jit(solution)/shard_map/all_gather | solution.py:213
  54.3 2.7 %collective-permute-start.6 = (bf16[4,1152,256]{2,1,0:T(8,128)(2,1)}, bf16[4,1152,256]{2,1,0:T(8,128)(2,1)S(1)}, u32[]{:S(2)}, u32[]{:S(2)}) collective-permute-start(bf16[4,1152,256]{2,1,0:T(8,128)(2,1)} %all-gather.2.cloned.1.call-done.w_mine), channel_id=1, source_target_pairs={{0,1},{1,0},{2,3},{3,2},{4,5},{5,4},{6,7},{7,6},{8,9},{9,8},{10,11... | collective-permute-start | bytes 7077896 | tf_op jit(solution)/shard_map/ppermute | solution.py:214
  57.8 0.8 fusion.3
  58.6 0.8 dynamic-slice_bitcast_fusion.1
  59.5 4.4 %collective-permute-start.5 = (bf16[64,384]{1,0:T(8,128)(2,1)S(1)}, bf16[64,384]{1,0:T(8,128)(2,1)S(1)}, u32[]{:S(2)}, u32[]{:S(2)}) collective-permute-start(bf16[64,384]{1,0:T(8,128)(2,1)S(1)} %get-tuple-element.16), channel_id=1, source_target_pairs={{0,13},{1,14},{2,15},{3,0},{4,1},{5,2},{6,3},{7,4},{8,5},{9,6},{10... | collective-permute-start | bytes 147464 | tf_op jit(solution)/shard_map/ppermute | solution.py:229
  63.8 2.1 %collective-permute-start = (bf16[64,384]{1,0:T(8,128)(2,1)S(1)}, bf16[64,384]{1,0:T(8,128)(2,1)S(1)}, u32[]{:S(2)}, u32[]{:S(2)}) collective-permute-start(bf16[64,384]{1,0:T(8,128)(2,1)S(1)} %get-tuple-element.17), channel_id=1, source_target_pairs={{0,3},{1,4},{2,5},{3,6},{4,7},{5,8},{6,9},{7,10},{8,11},{9,12},{10... | collective-permute-start | bytes 147464 | tf_op jit(solution)/shard_map/ppermute | solution.py:228
  65.9 0.8 dynamic-slice_bitcast_fusion
  66.8 5.7 %collective-permute-start.4 = (bf16[96,640]{1,0:T(8,128)(2,1)S(1)}, bf16[96,640]{1,0:T(8,128)(2,1)S(1)}, u32[]{:S(2)}, u32[]{:S(2)}) collective-permute-start(bf16[96,640]{1,0:T(8,128)(2,1)S(1)} %pad_maximum_fusion.own), channel_id=1, source_target_pairs={{0,14},{1,15},{2,0},{3,1},{4,2},{5,3},{6,4},{7,5},{8,6},{9,7},{10,... | collective-permute-start | bytes 368648 | tf_op jit(solution)/shard_map/ppermute | solution.py:227
  72.5 1.7 collective-permute-start.2
  74.2 1.9 collective-permute-start.1
  76.8 5.6 %collective-permute-done.1.m2a = bf16[96,640]{1,0:T(8,128)(2,1)S(1)} collective-permute-done((bf16[96,640]{1,0:T(8,128)(2,1)S(1)}, bf16[96,640]{1,0:T(8,128)(2,1)S(1)}, u32[]{:S(2)}, u32[]{:S(2)}) %collective-permute-start.1) | collective-permute-done | bytes 122912 | tf_op jit(solution)/shard_map/ppermute | solution.py:226
  82.4 1.7 copy-done.1
  84.0 16.8 %shard_map.59 = (bf16[4,320,256]{2,1,0:T(8,128)(2,1)S(1)}, f32[256,128]{1,0:T(8,128)S(1)}) custom-call(s32[1]{0:T(128)} %bitcast.core_ref, bf16[64,384]{1,0:T(8,128)(2,1)S(1)} %collective-permute-done.m3a, bf16[96,640]{1,0:T(8,128)(2,1)S(1)} %collective-permute-done.1.m2a, bf16[96,640]{1,0:T(8,128)(2,1)S(1)} %collective-permute-done.2.m1a, ...), custom_call_target="tpu_custom_call" | custom-call | flops 6000000000 | bytes 6000000 | tf_op jit(solution)/shard_map/pallas_call | solution.py:232
  100.9 12.6 %all_to_all.15.mine = bf16[4,320,256]{2,1,0:T(8,128)(2,1)S(1)} all-to-all(bf16[4,320,256]{2,1,0:T(8,128)(2,1)S(1)} %get-tuple-element.6), channel_id=1, replica_groups=mesh['dp'=8,'section'=4,'py'=8,'core'=2] {'section'}, dimensions={0} | all-to-all | bytes 1310720 | tf_op jit(solution)/shard_map/all_to_all | solution.py:251
  113.5 3.7 %collective-permute-start.7 = (bf16[4,224,256]{2,1,0:T(8,128)(2,1)S(1)}, bf16[4,224,256]{2,1,0:T(8,128)(2,1)S(1)}, u32[]{:S(2)}, u32[]{:S(2)}) collective-permute-start(bf16[4,224,256]{2,1,0:T(8,128)(2,1)S(1)} %slice.16), channel_id=1, source_target_pairs={{0,1},{1,0},{2,3},{3,2},{4,5},{5,4},{6,7},{7,6},{8,9},{9,8},{10,11... | collective-permute-start | bytes 1376264 | tf_op jit(solution)/shard_map/ppermute | solution.py:252
  117.2 1.4 collective-permute-done.7.other
  118.7 2.7 %shard_map.60 = (bf16[2560,128]{1,0:T(8,128)(2,1)S(1)}, bf16[4,96,256]{2,1,0:T(8,128)(2,1)}) custom-call(s32[1]{0:T(128)} %bitcast.core_ref, bf16[4,320,256]{2,1,0:T(8,128)(2,1)S(1)} %all_to_all.15.mine, bf16[4,224,256]{2,1,0:T(8,128)(2,1)S(1)} %collective-permute-done.7.other, f32[256,128]{1,0:T(8,128)S(1)} %get-tuple-element.7.offp), custom_call_target="tpu_custom_call" | custom-call | flops 1000000000 | bytes 2000000 | tf_op jit(solution)/shard_map/pallas_call | solution.py:255
  121.4 29.8 %all_to_all.16.x_ref = bf16[64,40,128]{2,1,0:T(8,128)(2,1)S(1)} all-to-all(bf16[64,40,128]{2,1,0:T(8,128)(2,1)S(1)} %bitcast.15), channel_id=1, replica_groups=mesh['dp'=8,'section'=4,'py'=8,'core'=2] {'dp','py'}, dimensions={0} | all-to-all | bytes 1310720 | tf_op jit(solution)/shard_map/all_to_all | solution.py:267
  151.3 25.5 %all_to_all.17 = bf16[64,40,128]{2,1,0:T(8,128)(2,1)S(1)} all-to-all(bf16[64,40,128]{2,1,0:T(8,128)(2,1)S(1)} %shard_map.61), channel_id=1, replica_groups=mesh['dp'=8,'section'=4,'py'=8,'core'=2] {'dp','py'}, dimensions={0} | all-to-all | bytes 1310720 | tf_op jit(solution)/shard_map/all_to_all | solution.py:271
  176.8 6.3 %collective-permute-start.8 = (bf16[2560,128]{1,0:T(8,128)(2,1)S(1)}, bf16[2560,128]{1,0:T(8,128)(2,1)S(1)}, u32[]{:S(2)}, u32[]{:S(2)}) collective-permute-start(bf16[2560,128]{1,0:T(8,128)(2,1)S(1)} %bitcast.13), channel_id=1, source_target_pairs={{0,1},{1,0},{2,3},{3,2},{4,5},{5,4},{6,7},{7,6},{8,9},{9,8},{10,11... | collective-permute-start | bytes 1966088 | tf_op jit(solution)/shard_map/ppermute | solution.py:272
  183.2 1.7 collective-permute-done.8.other
  184.9 1.2 shard_map.62
  (21 shorter events, 1.7 us)
Async XLA Ops:
  7.2 1.3 copy-start
  7.2 49.9 %copy-start.2 = (s32[9,96]{1,0:T(8,128)S(1)}, s32[9,96]{1,0:T(8,128)}, u32[]{:S(2)}) copy-start(s32[9,96]{1,0:T(8,128)} %param.7) | copy-start | bytes 10372
  7.2 47.1 %all-gather.2.cloned.1.call-start = ((), (), s32[]{:S(2)}) async-start(), calls=%async_computation.3 | async-start | bytes 2949120 | tf_op jit(solution)/shard_map/all_gather | solution.py:213
  54.3 28.1 %collective-permute-start.6 = (bf16[4,1152,256]{2,1,0:T(8,128)(2,1)}, bf16[4,1152,256]{2,1,0:T(8,128)(2,1)S(1)}, u32[]{:S(2)}, u32[]{:S(2)}) collective-permute-start(bf16[4,1152,256]{2,1,0:T(8,128)(2,1)} %all-gather.2.cloned.1.call-done.w_mine), channel_id=1, source_target_pairs={{0,1},{1,0},{2,3},{3,2},{4,5},{5,4},{6,7},{7,6},{8,9},{9,8},{10,11... | collective-permute-start | bytes 7077896 | tf_op jit(solution)/shard_map/ppermute | solution.py:214
  59.5 13.0 %collective-permute-start.5 = (bf16[64,384]{1,0:T(8,128)(2,1)S(1)}, bf16[64,384]{1,0:T(8,128)(2,1)S(1)}, u32[]{:S(2)}, u32[]{:S(2)}) collective-permute-start(bf16[64,384]{1,0:T(8,128)(2,1)S(1)} %get-tuple-element.16), channel_id=1, source_target_pairs={{0,13},{1,14},{2,15},{3,0},{4,1},{5,2},{6,3},{7,4},{8,5},{9,6},{10... | collective-permute-start | bytes 147464 | tf_op jit(solution)/shard_map/ppermute | solution.py:229
  63.8 10.4 %collective-permute-start = (bf16[64,384]{1,0:T(8,128)(2,1)S(1)}, bf16[64,384]{1,0:T(8,128)(2,1)S(1)}, u32[]{:S(2)}, u32[]{:S(2)}) collective-permute-start(bf16[64,384]{1,0:T(8,128)(2,1)S(1)} %get-tuple-element.17), channel_id=1, source_target_pairs={{0,3},{1,4},{2,5},{3,6},{4,7},{5,8},{6,9},{7,10},{8,11},{9,12},{10... | collective-permute-start | bytes 147464 | tf_op jit(solution)/shard_map/ppermute | solution.py:228
  66.8 9.4 %collective-permute-start.4 = (bf16[96,640]{1,0:T(8,128)(2,1)S(1)}, bf16[96,640]{1,0:T(8,128)(2,1)S(1)}, u32[]{:S(2)}, u32[]{:S(2)}) collective-permute-start(bf16[96,640]{1,0:T(8,128)(2,1)S(1)} %pad_maximum_fusion.own), channel_id=1, source_target_pairs={{0,14},{1,15},{2,0},{3,1},{4,2},{5,3},{6,4},{7,5},{8,6},{9,7},{10,... | collective-permute-start | bytes 368648 | tf_op jit(solution)/shard_map/ppermute | solution.py:227
  72.5 4.3 %collective-permute-start.3 = (bf16[96,640]{1,0:T(8,128)(2,1)S(1)}, bf16[96,640]{1,0:T(8,128)(2,1)S(1)}, u32[]{:S(2)}, u32[]{:S(2)}) collective-permute-start(bf16[96,640]{1,0:T(8,128)(2,1)S(1)} %pad_maximum_fusion.own), channel_id=1, source_target_pairs={{0,15},{1,0},{2,1},{3,2},{4,3},{5,4},{6,5},{7,6},{8,7},{9,8},{10,9... | collective-permute-start | bytes 368648 | tf_op jit(solution)/shard_map/ppermute | solution.py:225
  72.5 4.3 %collective-permute-start.2 = (bf16[96,640]{1,0:T(8,128)(2,1)S(1)}, bf16[96,640]{1,0:T(8,128)(2,1)S(1)}, u32[]{:S(2)}, u32[]{:S(2)}) collective-permute-start(bf16[96,640]{1,0:T(8,128)(2,1)S(1)} %pad_maximum_fusion.own), channel_id=1, source_target_pairs={{0,1},{1,2},{2,3},{3,4},{4,5},{5,6},{6,7},{7,8},{8,9},{9,10},{10,1... | collective-permute-start | bytes 368648 | tf_op jit(solution)/shard_map/ppermute | solution.py:224
  74.2 8.2 %collective-permute-start.1 = (bf16[96,640]{1,0:T(8,128)(2,1)S(1)}, bf16[96,640]{1,0:T(8,128)(2,1)S(1)}, u32[]{:S(2)}, u32[]{:S(2)}) collective-permute-start(bf16[96,640]{1,0:T(8,128)(2,1)S(1)} %pad_maximum_fusion.own), channel_id=1, source_target_pairs={{0,2},{1,3},{2,4},{3,5},{4,6},{5,7},{6,8},{7,9},{8,10},{9,11},{10,... | collective-permute-start | bytes 368648 | tf_op jit(solution)/shard_map/ppermute | solution.py:226
  82.4 1.7 copy-start.1
  113.5 5.2 %collective-permute-start.7 = (bf16[4,224,256]{2,1,0:T(8,128)(2,1)S(1)}, bf16[4,224,256]{2,1,0:T(8,128)(2,1)S(1)}, u32[]{:S(2)}, u32[]{:S(2)}) collective-permute-start(bf16[4,224,256]{2,1,0:T(8,128)(2,1)S(1)} %slice.16), channel_id=1, source_target_pairs={{0,1},{1,0},{2,3},{3,2},{4,5},{5,4},{6,7},{7,6},{8,9},{9,8},{10,11... | collective-permute-start | bytes 1376264 | tf_op jit(solution)/shard_map/ppermute | solution.py:252
  176.8 8.0 %collective-permute-start.8 = (bf16[2560,128]{1,0:T(8,128)(2,1)S(1)}, bf16[2560,128]{1,0:T(8,128)(2,1)S(1)}, u32[]{:S(2)}, u32[]{:S(2)}) collective-permute-start(bf16[2560,128]{1,0:T(8,128)(2,1)S(1)} %bitcast.13), channel_id=1, source_target_pairs={{0,1},{1,0},{2,3},{3,2},{4,5},{5,4},{6,7},{7,6},{8,9},{9,8},{10,11... | collective-permute-start | bytes 1966088 | tf_op jit(solution)/shard_map/ppermute | solution.py:272
Sparse Core Ops, SparseCore 0:
  10.7 43.5 all-gather.1

commit v2 on v1

--- a/solution.py
+++ b/solution.py
@@ -7,6 +7,7 @@
 from jax.experimental.pallas import tpu as pltpu
 from jax.sharding import Mesh
 from jax.sharding import PartitionSpec as P
+
 
 HALO = 32
 TAPS = 9
@@ -31,14 +32,19 @@
 MSG = HROWS + PROWS + GROWS
 
 
-def stack_kernel(core_ref, m3a, m2a, m1a, own, m1b, m2b, m3b, w_mine, w_other, out_ref, offp_ref,
-                 w_buf, h_buf, off_buf, s_buf, st_buf, gat, der, pre_buf, g_buf, sems):
-    core = core_ref[0]
-    copies = []
-    for n, (src, half) in enumerate(((w_mine, core), (w_other, 1 - core))):
-        row = pl.multiple_of(half * HALF, HALF)
-        copies.append(pltpu.make_async_copy(src, w_buf.at[:, pl.ds(row, HALF), :], sems.at[n]))
-        copies[-1].start()
+def stack_kernel(ids_ref, m3a, m2a, m1a, own, m1b, m2b, m3b, w_own, *refs):
+    parts, refs = refs[:8], refs[8:]
+    out_ref, offp_ref, w_buf, h_buf, off_buf, s_buf, st_buf, gat, der, pre_buf, g_buf, sems = refs
+    core, section = ids_ref[0], ids_ref[1]
+    copies = [pltpu.make_async_copy(w_own, w_buf.at[section], sems.at[0])]
+    for n, (hop, first) in enumerate(((3, 0), (1, 0), (2, 0), (2, HALF // 2))):
+        for side in range(2):
+            src = parts[2 * n + side]
+            row = pl.multiple_of(jnp.abs(core - side) * HALF + first, HALF // 2)
+            dst = w_buf.at[lax.rem(section + hop, LEVELS), pl.ds(row, src.shape[0]), :]
+            copies.append(pltpu.make_async_copy(src, dst, sems.at[2 * n + side + 1]))
+    for copy in copies:
+        copy.start()
 
     h_buf[...] = jnp.zeros_like(h_buf)
     off_buf[...] = jnp.zeros_like(off_buf)
@@ -200,18 +206,24 @@
     return [(i, (i + by) % axis_size) for i in range(axis_size)]
 
 
-def body(maps, upstream, weights, neighbours):
+def step(maps, upstream, weights, neighbours):
     micro = maps.shape[0]
     section = lax.axis_index("section")
     core = lax.axis_index("core")
     patches = lax.axis_size("py") * lax.axis_size("core")
     patch = lax.axis_index("py") * lax.axis_size("core") + core
     npix = PIX * patches
-    cores = core.reshape((1,)).astype(jnp.int32)
-
+    cores = jnp.stack([core, section]).astype(jnp.int32)
+
+    sections = lax.axis_size("section")
     half = lax.dynamic_slice_in_dim(weights[0], core * HALF, HALF, axis=0)
-    w_mine = lax.all_gather(half, "section")
-    w_other = lax.ppermute(w_mine, "core", shift(2, 1))
+    left = lax.ppermute(half, "section", shift(sections, 1))
+    right = lax.ppermute(half, "section", shift(sections, -1))
+    far_top = lax.ppermute(left[:HALF // 2], "section", shift(sections, 1))
+    far_bottom = lax.ppermute(right[HALF // 2:], "section", shift(sections, -1))
+    parts = []
+    for block in (left, right, far_top, far_bottom):
+        parts += [block, lax.ppermute(block, "core", shift(2, 1))]
 
     place = patch * PIX + jnp.arange(PIX, dtype=jnp.int32)
     offsets = jnp.mod(neighbours - place[None, :] + HALO, npix) - HALO
@@ -232,7 +244,7 @@
     out, offp = call(
         stack_kernel,
         [jax.ShapeDtypeStruct((LEVELS, MSG, C), BF), jax.ShapeDtypeStruct((2 * PROWS, 128), F32)],
-        [SMEM] + [VMEM] * 7 + [ANY] * 2,
+        [SMEM] + [VMEM] * 7 + [ANY] * 9,
         [
             pltpu.VMEM((LEVELS, TAPS * C, C), BF),
             pltpu.VMEM((LEVELS, ROWS, C), BF),
@@ -243,10 +255,10 @@
             pltpu.VMEM((LEVELS, tiles * TILE, C), F32),
             pltpu.VMEM((ROWS, C), BF),
             pltpu.VMEM((ROWS, C), BF),
-            pltpu.SemaphoreType.DMA((2,)),
+            pltpu.SemaphoreType.DMA((9,)),
         ],
         flops=6 * 10**9, nbytes=6 * 10**6,
-    )(cores, m3a, m2a, m1a, own, m1b, m2b, m3b, w_mine, w_other)
+    )(cores, m3a, m2a, m1a, own, m1b, m2b, m3b, weights[0], *parts)
 
     mine = lax.all_to_all(out, "section", 0, 0, tiled=True)
     other = lax.ppermute(mine[:, :HROWS + PROWS], "core", shift(2, 1))
@@ -288,4 +300,4 @@
         P(None, patch),
     )
     out_specs = (P("section", None, "dp", patch, None), P("section", None, None))
-    return jax.shard_map(body, mesh=fine, in_specs=in_specs, out_specs=out_specs, check_vma=False)
+    return jax.shard_map(step, mesh=fine, in_specs=in_specs, out_specs=out_specs, check_vma=False)

time: 194 us -> 168 us (0.87)
  waiting for transfers between devices: 54.3 us -> 12.4 us
  starting transfers between devices: 28.6 us -> 58.3 us
  between operations: 14.2 us -> 0.96 us
  local copies, waits for them, and re-layouts: 6.11 us -> 2.17 us
  Pallas kernels: 20.9 us -> 23.3 us
  blocking collectives: 67.9 us -> 70.2 us
    all_gather x1 -> x0, waiting for transfers between devices: 45 us -> none  [body(): w_mine = lax.all_gather(half, 'section')]
    ppermute x9 -> x16, starting transfers between devices: 28.6 us -> 58.3 us  [the longest x4 13.5 us: step(): parts += [block, lax.ppermute(block, 'core', shift(2, 1))]]
    ppermute x9 -> x16, waiting for transfers between devices: 9.35 us -> 12.4 us  [the longest x1 5.22 us: step(): m2a = send(own, perm=shift(patches, 2))]
    unnamed x6, local copies, waits for them, and re-layouts: 2.88 us -> 0.02 us
    pallas_call x4, Pallas kernels: 20.9 us -> 23.3 us  [the longest x1 18.1 us: step(): call(stack_kernel, [jax.ShapeDtypeStruct((LEVELS, MSG, C), BF), jax.Shape...]
    all_to_all x3, blocking collectives: 67.9 us -> 70.2 us  [the longest x1 33 us: step(): lax.all_to_all(part.reshape((chips, rows // chips, 128)), ('dp', 'py'), 0...]
  transfers between devices with their start and end apart: 10 -> 16, of which waited for: 5 -> 5; matrix products, arithmetic and copies ran while one was open for 2% -> 1% of each run, Pallas kernels for 0% -> 0%
where the time goes in v2:
time: 168 us; the launch traced here: 167 us
  blocking collectives  70.2 us (42%)
  starting transfers between devices  58.3 us (35%)
  Pallas kernels  23.3 us (14%)
  waiting for transfers between devices  12.4 us (7%)
  local copies, waits for them, and re-layouts  2.17 us (1%)
    all_to_all x1, blocking collectives, step(): lax.all_to_all(part.reshape((chips, rows // chips, 128)), ('dp', 'py'), 0...  33 us
    all_to_all x1, blocking collectives, step(): lax.all_to_all(total, ('dp', 'py'), 0, 0, tiled=True).reshape((rows, 128))  25.5 us
    pallas_call x1, Pallas kernels, step(): call(stack_kernel, [jax.ShapeDtypeStruct((LEVELS, MSG, C), BF), jax.Shape...  18.1 us
    ppermute x4, starting transfers between devices, step(): parts += [block, lax.ppermute(block, 'core', shift(2, 1))]  13.5 us
    all_to_all x1, blocking collectives, step(): mine = lax.all_to_all(out, 'section', 0, 0, tiled=True)  11.6 us
    ppermute x1, starting transfers between devices, step(): other = lax.ppermute(mine[:, :HROWS + PROWS], 'core', shift(2, 1))  8.22 us
    ppermute x1, starting transfers between devices, step(): swapped = lax.ppermute(full, 'core', shift(2, 1))  6.34 us
    ppermute x1, starting transfers between devices, step(): m3b = send(own[:edge, :C + 128], perm=shift(patches, -3))  5.94 us
  transfers between devices with their start and end apart: 16, of which 5 were waited for; matrix products, arithmetic and copies ran while one was open for 1% of the time, Pallas kernels for 0%

profile of v2, /device:TPU:1, one launch (start us, length us, event | category | flops | bytes accessed | tf_op | source)
XLA Modules:
  0.0 167.4 jit_solution(9928824287624886900)
XLA Ops:
  1.8 5.3 %collective-permute-start.8 = (bf16[1152,256]{1,0:T(8,128)(2,1)S(1)}, bf16[1152,256]{1,0:T(8,128)(2,1)S(1)}, u32[]{:S(2)}, u32[]{:S(2)}) collective-permute-start(bf16[1152,256]{1,0:T(8,128)(2,1)S(1)} %dynamic-slice_bitcast_fusion), channel_id=1, source_target_pairs={{0,48},{16,0},{32,16},{48,32},{1,49},{17,1},{33,17},{49,33},{2,50}... | collective-permute-start | bytes 1769480 | tf_op jit(solution)/shard_map/ppermute | solution.py:221
  7.2 1.9 %collective-permute-start.6 = (bf16[1152,256]{1,0:T(8,128)(2,1)S(1)}, bf16[1152,256]{1,0:T(8,128)(2,1)S(1)}, u32[]{:S(2)}, u32[]{:S(2)}) collective-permute-start(bf16[1152,256]{1,0:T(8,128)(2,1)S(1)} %dynamic-slice_bitcast_fusion), channel_id=1, source_target_pairs={{0,16},{16,32},{32,48},{48,0},{1,17},{17,33},{33,49},{49,1},{2,18}... | collective-permute-start | bytes 1769480 | tf_op jit(solution)/shard_map/ppermute | solution.py:220
  9.3 5.9 %collective-permute-start.5 = (bf16[64,384]{1,0:T(8,128)(2,1)S(1)}, bf16[64,384]{1,0:T(8,128)(2,1)S(1)}, u32[]{:S(2)}, u32[]{:S(2)}) collective-permute-start(bf16[64,384]{1,0:T(8,128)(2,1)S(1)} %get-tuple-element.14), channel_id=1, source_target_pairs={{0,13},{1,14},{2,15},{3,0},{4,1},{5,2},{6,3},{7,4},{8,5},{9,6},{10... | collective-permute-start | bytes 147464 | tf_op jit(solution)/shard_map/ppermute | solution.py:241
  15.3 1.9 %collective-permute-start = (bf16[64,384]{1,0:T(8,128)(2,1)S(1)}, bf16[64,384]{1,0:T(8,128)(2,1)S(1)}, u32[]{:S(2)}, u32[]{:S(2)}) collective-permute-start(bf16[64,384]{1,0:T(8,128)(2,1)S(1)} %get-tuple-element.15), channel_id=1, source_target_pairs={{0,3},{1,4},{2,5},{3,6},{4,7},{5,8},{6,9},{7,10},{8,11},{9,12},{10... | collective-permute-start | bytes 147464 | tf_op jit(solution)/shard_map/ppermute | solution.py:240
  18.1 4.9 %collective-permute-start.12 = (bf16[576,256]{1,0:T(8,128)(2,1)S(1)}, bf16[576,256]{1,0:T(8,128)(2,1)S(1)}, u32[]{:S(2)}, u32[]{:S(2)}) collective-permute-start(bf16[576,256]{1,0:T(8,128)(2,1)S(1)} %slice.25), channel_id=1, source_target_pairs={{0,48},{16,0},{32,16},{48,32},{1,49},{17,1},{33,17},{49,33},{2,50}... | collective-permute-start | bytes 884744 | tf_op jit(solution)/shard_map/ppermute | solution.py:223
  23.0 1.9 %collective-permute-start.10 = (bf16[576,256]{1,0:T(8,128)(2,1)S(1)}, bf16[576,256]{1,0:T(8,128)(2,1)S(1)}, u32[]{:S(2)}, u32[]{:S(2)}) collective-permute-start(bf16[576,256]{1,0:T(8,128)(2,1)S(1)} %slice.24), channel_id=1, source_target_pairs={{0,16},{16,32},{32,48},{48,0},{1,17},{17,33},{33,49},{49,1},{2,18}... | collective-permute-start | bytes 884744 | tf_op jit(solution)/shard_map/ppermute | solution.py:222
  24.9 5.3 %collective-permute-start.9 = (bf16[1152,256]{1,0:T(8,128)(2,1)S(1)}, bf16[1152,256]{1,0:T(8,128)(2,1)S(1)}, u32[]{:S(2)}, u32[]{:S(2)}) collective-permute-start(bf16[1152,256]{1,0:T(8,128)(2,1)S(1)} %collective-permute-done.8.refs_2_), channel_id=1, source_target_pairs={{0,1},{1,0},{2,3},{3,2},{4,5},{5,4},{6,7},{7,6},{8,9},{9,8},{10,11... | collective-permute-start | bytes 1769480 | tf_op jit(solution)/shard_map/ppermute | solution.py:226
  30.2 1.9 %collective-permute-start.7 = (bf16[1152,256]{1,0:T(8,128)(2,1)S(1)}, bf16[1152,256]{1,0:T(8,128)(2,1)S(1)}, u32[]{:S(2)}, u32[]{:S(2)}) collective-permute-start(bf16[1152,256]{1,0:T(8,128)(2,1)S(1)} %collective-permute-done.6.refs_0_), channel_id=1, source_target_pairs={{0,1},{1,0},{2,3},{3,2},{4,5},{5,4},{6,7},{7,6},{8,9},{9,8},{10,11... | collective-permute-start | bytes 1769480 | tf_op jit(solution)/shard_map/ppermute | solution.py:226
  32.2 5.1 %collective-permute-start.4 = (bf16[96,640]{1,0:T(8,128)(2,1)S(1)}, bf16[96,640]{1,0:T(8,128)(2,1)S(1)}, u32[]{:S(2)}, u32[]{:S(2)}) collective-permute-start(bf16[96,640]{1,0:T(8,128)(2,1)S(1)} %pad_maximum_fusion.own), channel_id=1, source_target_pairs={{0,14},{1,15},{2,0},{3,1},{4,2},{5,3},{6,4},{7,5},{8,6},{9,7},{10,... | collective-permute-start | bytes 368648 | tf_op jit(solution)/shard_map/ppermute | solution.py:239
  37.3 2.2 %collective-permute-done.4.m2b = bf16[96,640]{1,0:T(8,128)(2,1)S(1)} collective-permute-done((bf16[96,640]{1,0:T(8,128)(2,1)S(1)}, bf16[96,640]{1,0:T(8,128)(2,1)S(1)}, u32[]{:S(2)}, u32[]{:S(2)}) %collective-permute-start.4) | collective-permute-done | bytes 122912 | tf_op jit(solution)/shard_map/ppermute | solution.py:239
  40.8 4.3 %collective-permute-start.13 = (bf16[576,256]{1,0:T(8,128)(2,1)S(1)}, bf16[576,256]{1,0:T(8,128)(2,1)S(1)}, u32[]{:S(2)}, u32[]{:S(2)}) collective-permute-start(bf16[576,256]{1,0:T(8,128)(2,1)S(1)} %collective-permute-done.12.refs_6_), channel_id=1, source_target_pairs={{0,1},{1,0},{2,3},{3,2},{4,5},{5,4},{6,7},{7,6},{8,9},{9,8},{10,11... | collective-permute-start | bytes 884744 | tf_op jit(solution)/shard_map/ppermute | solution.py:226
  45.2 1.9 %collective-permute-start.11 = (bf16[576,256]{1,0:T(8,128)(2,1)S(1)}, bf16[576,256]{1,0:T(8,128)(2,1)S(1)}, u32[]{:S(2)}, u32[]{:S(2)}) collective-permute-start(bf16[576,256]{1,0:T(8,128)(2,1)S(1)} %collective-permute-done.10.refs_4_), channel_id=1, source_target_pairs={{0,1},{1,0},{2,3},{3,2},{4,5},{5,4},{6,7},{7,6},{8,9},{9,8},{10,11... | collective-permute-start | bytes 884744 | tf_op jit(solution)/shard_map/ppermute | solution.py:226
  47.1 1.9 %collective-permute-done.2.m1a = bf16[96,640]{1,0:T(8,128)(2,1)S(1)} collective-permute-done((bf16[96,640]{1,0:T(8,128)(2,1)S(1)}, bf16[96,640]{1,0:T(8,128)(2,1)S(1)}, u32[]{:S(2)}, u32[]{:S(2)}) %collective-permute-start.2) | collective-permute-done | bytes 122912 | tf_op jit(solution)/shard_map/ppermute | solution.py:236
  49.0 1.9 %collective-permute-start.1 = (bf16[96,640]{1,0:T(8,128)(2,1)S(1)}, bf16[96,640]{1,0:T(8,128)(2,1)S(1)}, u32[]{:S(2)}, u32[]{:S(2)}) collective-permute-start(bf16[96,640]{1,0:T(8,128)(2,1)S(1)} %pad_maximum_fusion.own), channel_id=1, source_target_pairs={{0,2},{1,3},{2,4},{3,5},{4,6},{5,7},{6,8},{7,9},{8,10},{9,11},{10,... | collective-permute-start | bytes 368648 | tf_op jit(solution)/shard_map/ppermute | solution.py:238
  51.0 5.2 %collective-permute-done.1.m2a = bf16[96,640]{1,0:T(8,128)(2,1)S(1)} collective-permute-done((bf16[96,640]{1,0:T(8,128)(2,1)S(1)}, bf16[96,640]{1,0:T(8,128)(2,1)S(1)}, u32[]{:S(2)}, u32[]{:S(2)}) %collective-permute-start.1) | collective-permute-done | bytes 122912 | tf_op jit(solution)/shard_map/ppermute | solution.py:238
  56.2 18.1 %shard_map.59 = (bf16[4,320,256]{2,1,0:T(8,128)(2,1)S(1)}, f32[256,128]{1,0:T(8,128)S(1)}) custom-call(s32[2]{0:T(128)S(1)} %pad_add_fusion.ids_ref.core_ref, bf16[64,384]{1,0:T(8,128)(2,1)S(1)} %collective-permute-done.m3a, bf16[96,640]{1,0:T(8,128)(2,1)S(1)} %collective-permute-done.1.m2a, bf16[96,640]{1,0:T(8,128)(2,1)S(1)} %collective-permute-done.2.m1a, ...), custom_call_target="tpu_custom_call" | custom-call | flops 6000000000 | bytes 6000000 | tf_op jit(solution)/shard_map/pallas_call | solution.py:244
  74.4 11.6 %all_to_all.15.mine = bf16[4,320,256]{2,1,0:T(8,128)(2,1)S(1)} all-to-all(bf16[4,320,256]{2,1,0:T(8,128)(2,1)S(1)} %get-tuple-element.6), channel_id=1, replica_groups=mesh['dp'=8,'section'=4,'py'=8,'core'=2] {'section'}, dimensions={0} | all-to-all | bytes 1310720 | tf_op jit(solution)/shard_map/all_to_all | solution.py:263
  86.0 8.2 %collective-permute-start.14 = (bf16[4,224,256]{2,1,0:T(8,128)(2,1)S(1)}, bf16[4,224,256]{2,1,0:T(8,128)(2,1)S(1)}, u32[]{:S(2)}, u32[]{:S(2)}) collective-permute-start(bf16[4,224,256]{2,1,0:T(8,128)(2,1)S(1)} %slice.26), channel_id=1, source_target_pairs={{0,1},{1,0},{2,3},{3,2},{4,5},{5,4},{6,7},{7,6},{8,9},{9,8},{10,11... | collective-permute-start | bytes 1376264 | tf_op jit(solution)/shard_map/ppermute | solution.py:264
  95.7 3.3 %shard_map.60 = (bf16[2560,128]{1,0:T(8,128)(2,1)S(1)}, bf16[4,96,256]{2,1,0:T(8,128)(2,1)}) custom-call(s32[2]{0:T(128)S(1)} %pad_add_fusion.ids_ref.core_ref, bf16[4,320,256]{2,1,0:T(8,128)(2,1)S(1)} %all_to_all.15.mine, bf16[4,224,256]{2,1,0:T(8,128)(2,1)S(1)} %collective-permute-done.14.other, f32[256,128]{1,0:T(8,128)S(1)} %get-tuple-element.7.offp), custom_call_target="tpu_custom_call" | custom-call | flops 1000000000 | bytes 2000000 | tf_op jit(solution)/shard_map/pallas_call | solution.py:267
  99.0 33.0 %all_to_all.16.x_ref = bf16[64,40,128]{2,1,0:T(8,128)(2,1)S(1)} all-to-all(bf16[64,40,128]{2,1,0:T(8,128)(2,1)S(1)} %bitcast.19), channel_id=1, replica_groups=mesh['dp'=8,'section'=4,'py'=8,'core'=2] {'dp','py'}, dimensions={0} | all-to-all | bytes 1310720 | tf_op jit(solution)/shard_map/all_to_all | solution.py:279
  132.1 25.5 %all_to_all.17 = bf16[64,40,128]{2,1,0:T(8,128)(2,1)S(1)} all-to-all(bf16[64,40,128]{2,1,0:T(8,128)(2,1)S(1)} %shard_map.61), channel_id=1, replica_groups=mesh['dp'=8,'section'=4,'py'=8,'core'=2] {'dp','py'}, dimensions={0} | all-to-all | bytes 1310720 | tf_op jit(solution)/shard_map/all_to_all | solution.py:283
  157.6 6.3 %collective-permute-start.15 = (bf16[2560,128]{1,0:T(8,128)(2,1)S(1)}, bf16[2560,128]{1,0:T(8,128)(2,1)S(1)}, u32[]{:S(2)}, u32[]{:S(2)}) collective-permute-start(bf16[2560,128]{1,0:T(8,128)(2,1)S(1)} %bitcast.17), channel_id=1, source_target_pairs={{0,1},{1,0},{2,3},{3,2},{4,5},{5,4},{6,7},{7,6},{8,9},{9,8},{10,11... | collective-permute-start | bytes 1966088 | tf_op jit(solution)/shard_map/ppermute | solution.py:284
  164.0 1.7 %collective-permute-done.15.other = bf16[2560,128]{1,0:T(8,128)(2,1)S(1)} collective-permute-done((bf16[2560,128]{1,0:T(8,128)(2,1)S(1)}, bf16[2560,128]{1,0:T(8,128)(2,1)S(1)}, u32[]{:S(2)}, u32[]{:S(2)}) %collective-permute-start.15) | collective-permute-done | bytes 655392 | tf_op jit(solution)/shard_map/ppermute | solution.py:284
  165.7 1.8 %shard_map.62 = bf16[2304,256]{1,0:T(8,128)(2,1)} custom-call(s32[2]{0:T(128)S(1)} %pad_add_fusion.ids_ref.core_ref, bf16[2560,128]{1,0:T(8,128)(2,1)S(1)} %bitcast.18, bf16[2560,128]{1,0:T(8,128)(2,1)S(1)} %collective-permute-done.15.other), custom_call_target="tpu_custom_call" | custom-call | bytes 2000000 | tf_op jit(solution)/shard_map/pallas_call | solution.py:285
  (35 shorter events, 5.3 us)
Async XLA Ops:
  0.6 8.7 %copy-start = (bf16[4,1,96,256]{3,2,1,0:T(8,128)(2,1)S(1)}, bf16[4,1,96,256]{3,2,1,0:T(8,128)(2,1)}, u32[]{:S(2)}) copy-start(bf16[4,1,96,256]{3,2,1,0:T(8,128)(2,1)} %param.4) | copy-start | bytes 589828
  0.6 8.5 %copy-start.2 = (s32[9,96]{1,0:T(8,128)S(1)}, s32[9,96]{1,0:T(8,128)}, u32[]{:S(2)}) copy-start(s32[9,96]{1,0:T(8,128)} %param.7) | copy-start | bytes 10372
  1.8 54.4 %copy-start.1 = (bf16[1,2304,256]{2,1,0:T(8,128)(2,1)S(1)}, bf16[1,2304,256]{2,1,0:T(8,128)(2,1)}, u32[]{:S(2)}) copy-start(bf16[1,2304,256]{2,1,0:T(8,128)(2,1)} %param.6) | copy-start | bytes 3538948
  1.8 16.2 %collective-permute-start.8 = (bf16[1152,256]{1,0:T(8,128)(2,1)S(1)}, bf16[1152,256]{1,0:T(8,128)(2,1)S(1)}, u32[]{:S(2)}, u32[]{:S(2)}) collective-permute-start(bf16[1152,256]{1,0:T(8,128)(2,1)S(1)} %dynamic-slice_bitcast_fusion), channel_id=1, source_target_pairs={{0,48},{16,0},{32,16},{48,32},{1,49},{17,1},{33,17},{49,33},{2,50}... | collective-permute-start | bytes 1769480 | tf_op jit(solution)/shard_map/ppermute | solution.py:221
  7.2 15.8 %collective-permute-start.6 = (bf16[1152,256]{1,0:T(8,128)(2,1)S(1)}, bf16[1152,256]{1,0:T(8,128)(2,1)S(1)}, u32[]{:S(2)}, u32[]{:S(2)}) collective-permute-start(bf16[1152,256]{1,0:T(8,128)(2,1)S(1)} %dynamic-slice_bitcast_fusion), channel_id=1, source_target_pairs={{0,16},{16,32},{32,48},{48,0},{1,17},{17,33},{33,49},{49,1},{2,18}... | collective-permute-start | bytes 1769480 | tf_op jit(solution)/shard_map/ppermute | solution.py:220
  9.3 20.9 %collective-permute-start.5 = (bf16[64,384]{1,0:T(8,128)(2,1)S(1)}, bf16[64,384]{1,0:T(8,128)(2,1)S(1)}, u32[]{:S(2)}, u32[]{:S(2)}) collective-permute-start(bf16[64,384]{1,0:T(8,128)(2,1)S(1)} %get-tuple-element.14), channel_id=1, source_target_pairs={{0,13},{1,14},{2,15},{3,0},{4,1},{5,2},{6,3},{7,4},{8,5},{9,6},{10... | collective-permute-start | bytes 147464 | tf_op jit(solution)/shard_map/ppermute | solution.py:241
  15.3 16.9 %collective-permute-start = (bf16[64,384]{1,0:T(8,128)(2,1)S(1)}, bf16[64,384]{1,0:T(8,128)(2,1)S(1)}, u32[]{:S(2)}, u32[]{:S(2)}) collective-permute-start(bf16[64,384]{1,0:T(8,128)(2,1)S(1)} %get-tuple-element.15), channel_id=1, source_target_pairs={{0,3},{1,4},{2,5},{3,6},{4,7},{5,8},{6,9},{7,10},{8,11},{9,12},{10... | collective-permute-start | bytes 147464 | tf_op jit(solution)/shard_map/ppermute | solution.py:240
  18.1 22.7 %collective-permute-start.12 = (bf16[576,256]{1,0:T(8,128)(2,1)S(1)}, bf16[576,256]{1,0:T(8,128)(2,1)S(1)}, u32[]{:S(2)}, u32[]{:S(2)}) collective-permute-start(bf16[576,256]{1,0:T(8,128)(2,1)S(1)} %slice.25), channel_id=1, source_target_pairs={{0,48},{16,0},{32,16},{48,32},{1,49},{17,1},{33,17},{49,33},{2,50}... | collective-permute-start | bytes 884744 | tf_op jit(solution)/shard_map/ppermute | solution.py:223
  23.0 22.2 %collective-permute-start.10 = (bf16[576,256]{1,0:T(8,128)(2,1)S(1)}, bf16[576,256]{1,0:T(8,128)(2,1)S(1)}, u32[]{:S(2)}, u32[]{:S(2)}) collective-permute-start(bf16[576,256]{1,0:T(8,128)(2,1)S(1)} %slice.24), channel_id=1, source_target_pairs={{0,16},{16,32},{32,48},{48,0},{1,17},{17,33},{33,49},{49,1},{2,18}... | collective-permute-start | bytes 884744 | tf_op jit(solution)/shard_map/ppermute | solution.py:222
  24.9 31.3 %collective-permute-start.9 = (bf16[1152,256]{1,0:T(8,128)(2,1)S(1)}, bf16[1152,256]{1,0:T(8,128)(2,1)S(1)}, u32[]{:S(2)}, u32[]{:S(2)}) collective-permute-start(bf16[1152,256]{1,0:T(8,128)(2,1)S(1)} %collective-permute-done.8.refs_2_), channel_id=1, source_target_pairs={{0,1},{1,0},{2,3},{3,2},{4,5},{5,4},{6,7},{7,6},{8,9},{9,8},{10,11... | collective-permute-start | bytes 1769480 | tf_op jit(solution)/shard_map/ppermute | solution.py:226
  30.2 26.0 %collective-permute-start.7 = (bf16[1152,256]{1,0:T(8,128)(2,1)S(1)}, bf16[1152,256]{1,0:T(8,128)(2,1)S(1)}, u32[]{:S(2)}, u32[]{:S(2)}) collective-permute-start(bf16[1152,256]{1,0:T(8,128)(2,1)S(1)} %collective-permute-done.6.refs_0_), channel_id=1, source_target_pairs={{0,1},{1,0},{2,3},{3,2},{4,5},{5,4},{6,7},{7,6},{8,9},{9,8},{10,11... | collective-permute-start | bytes 1769480 | tf_op jit(solution)/shard_map/ppermute | solution.py:226
  32.2 7.3 %collective-permute-start.4 = (bf16[96,640]{1,0:T(8,128)(2,1)S(1)}, bf16[96,640]{1,0:T(8,128)(2,1)S(1)}, u32[]{:S(2)}, u32[]{:S(2)}) collective-permute-start(bf16[96,640]{1,0:T(8,128)(2,1)S(1)} %pad_maximum_fusion.own), channel_id=1, source_target_pairs={{0,14},{1,15},{2,0},{3,1},{4,2},{5,3},{6,4},{7,5},{8,6},{9,7},{10,... | collective-permute-start | bytes 368648 | tf_op jit(solution)/shard_map/ppermute | solution.py:239
  39.4 7.7 %collective-permute-start.3 = (bf16[96,640]{1,0:T(8,128)(2,1)S(1)}, bf16[96,640]{1,0:T(8,128)(2,1)S(1)}, u32[]{:S(2)}, u32[]{:S(2)}) collective-permute-start(bf16[96,640]{1,0:T(8,128)(2,1)S(1)} %pad_maximum_fusion.own), channel_id=1, source_target_pairs={{0,15},{1,0},{2,1},{3,2},{4,3},{5,4},{6,5},{7,6},{8,7},{9,8},{10,9... | collective-permute-start | bytes 368648 | tf_op jit(solution)/shard_map/ppermute | solution.py:237
  40.8 15.4 %collective-permute-start.13 = (bf16[576,256]{1,0:T(8,128)(2,1)S(1)}, bf16[576,256]{1,0:T(8,128)(2,1)S(1)}, u32[]{:S(2)}, u32[]{:S(2)}) collective-permute-start(bf16[576,256]{1,0:T(8,128)(2,1)S(1)} %collective-permute-done.12.refs_6_), channel_id=1, source_target_pairs={{0,1},{1,0},{2,3},{3,2},{4,5},{5,4},{6,7},{7,6},{8,9},{9,8},{10,11... | collective-permute-start | bytes 884744 | tf_op jit(solution)/shard_map/ppermute | solution.py:226
  45.2 11.1 %collective-permute-start.11 = (bf16[576,256]{1,0:T(8,128)(2,1)S(1)}, bf16[576,256]{1,0:T(8,128)(2,1)S(1)}, u32[]{:S(2)}, u32[]{:S(2)}) collective-permute-start(bf16[576,256]{1,0:T(8,128)(2,1)S(1)} %collective-permute-done.10.refs_4_), channel_id=1, source_target_pairs={{0,1},{1,0},{2,3},{3,2},{4,5},{5,4},{6,7},{7,6},{8,9},{9,8},{10,11... | collective-permute-start | bytes 884744 | tf_op jit(solution)/shard_map/ppermute | solution.py:226
  47.1 1.9 %collective-permute-start.2 = (bf16[96,640]{1,0:T(8,128)(2,1)S(1)}, bf16[96,640]{1,0:T(8,128)(2,1)S(1)}, u32[]{:S(2)}, u32[]{:S(2)}) collective-permute-start(bf16[96,640]{1,0:T(8,128)(2,1)S(1)} %pad_maximum_fusion.own), channel_id=1, source_target_pairs={{0,1},{1,2},{2,3},{3,4},{4,5},{5,6},{6,7},{7,8},{8,9},{9,10},{10,1... | collective-permute-start | bytes 368648 | tf_op jit(solution)/shard_map/ppermute | solution.py:236
  49.0 7.2 %collective-permute-start.1 = (bf16[96,640]{1,0:T(8,128)(2,1)S(1)}, bf16[96,640]{1,0:T(8,128)(2,1)S(1)}, u32[]{:S(2)}, u32[]{:S(2)}) collective-permute-start(bf16[96,640]{1,0:T(8,128)(2,1)S(1)} %pad_maximum_fusion.own), channel_id=1, source_target_pairs={{0,2},{1,3},{2,4},{3,5},{4,6},{5,7},{6,8},{7,9},{8,10},{9,11},{10,... | collective-permute-start | bytes 368648 | tf_op jit(solution)/shard_map/ppermute | solution.py:238
  86.0 9.7 %collective-permute-start.14 = (bf16[4,224,256]{2,1,0:T(8,128)(2,1)S(1)}, bf16[4,224,256]{2,1,0:T(8,128)(2,1)S(1)}, u32[]{:S(2)}, u32[]{:S(2)}) collective-permute-start(bf16[4,224,256]{2,1,0:T(8,128)(2,1)S(1)} %slice.26), channel_id=1, source_target_pairs={{0,1},{1,0},{2,3},{3,2},{4,5},{5,4},{6,7},{7,6},{8,9},{9,8},{10,11... | collective-permute-start | bytes 1376264 | tf_op jit(solution)/shard_map/ppermute | solution.py:264
  157.6 8.1 %collective-permute-start.15 = (bf16[2560,128]{1,0:T(8,128)(2,1)S(1)}, bf16[2560,128]{1,0:T(8,128)(2,1)S(1)}, u32[]{:S(2)}, u32[]{:S(2)}) collective-permute-start(bf16[2560,128]{1,0:T(8,128)(2,1)S(1)} %bitcast.17), channel_id=1, source_target_pairs={{0,1},{1,0},{2,3},{3,2},{4,5},{5,4},{6,7},{7,6},{8,9},{9,8},{10,11... | collective-permute-start | bytes 1966088 | tf_op jit(solution)/shard_map/ppermute | solution.py:284

commit v3 on v1

--- a/solution.py
+++ b/solution.py
@@ -7,6 +7,7 @@
 from jax.experimental.pallas import tpu as pltpu
 from jax.sharding import Mesh
 from jax.sharding import PartitionSpec as P
+
 
 HALO = 32
 TAPS = 9
@@ -31,13 +32,46 @@
 MSG = HROWS + PROWS + GROWS
 
 
-def stack_kernel(core_ref, m3a, m2a, m1a, own, m1b, m2b, m3b, w_mine, w_other, out_ref, offp_ref,
-                 w_buf, h_buf, off_buf, s_buf, st_buf, gat, der, pre_buf, g_buf, sems):
-    core = core_ref[0]
+def expand(gat, t, src, hot):
+    rows = jnp.dot(hot, src, preferred_element_type=F32).astype(BF)
+    dst = pl.ds(pl.multiple_of(t * TILE, TILE), TILE)
+    gat[dst, :C] = src[PAD:PAD + TILE]
+    for k in range(1, TAPS):
+        gat[dst, k * C:(k + 1) * C] = rows[(k - 1) * TILE:k * TILE]
+
+
+def expand_all(gat, first, last, src_ref, hot_ref, group):
+    def one(t):
+        expand(gat, t, src_ref[pl.ds(pl.multiple_of(t * TILE, TILE), 2 * TILE), :], hot_ref[t])
+
+    def some(i, carry):
+        for j in range(group):
+            one(first + i * group + j)
+        return carry
+
+    whole = (last - first) // group
+    if whole:
+        lax.fori_loop(0, whole, some, 0)
+    for t in range(first + whole * group, last):
+        one(t)
+
+
+def stack_kernel(ids_ref, m3a, m2a, m1a, own, m1b, m2b, m3b, w_own, near_mine, near_other, far_mine, far_other,
+                 out_ref, offp_ref, w_buf, h_buf, off_buf, s_buf, st_buf, gat, der, pre_buf, g_buf, sems):
+    core, section = ids_ref[0], ids_ref[1]
+    left, right = lax.rem(section + 3, LEVELS), lax.rem(section + 1, LEVELS)
+    far = w_buf.at[lax.rem(section + 2, LEVELS)]
+    row_mine = pl.multiple_of(core * HALF, HALF)
+    row_other = pl.multiple_of((1 - core) * HALF, HALF)
     copies = []
-    for n, (src, half) in enumerate(((w_mine, core), (w_other, 1 - core))):
-        row = pl.multiple_of(half * HALF, HALF)
-        copies.append(pltpu.make_async_copy(src, w_buf.at[:, pl.ds(row, HALF), :], sems.at[n]))
+    for n, (src, dst) in enumerate((
+        (w_own, w_buf.at[section]),
+        (near_mine, w_buf.at[jnp.where(core == 0, left, right)]),
+        (near_other, w_buf.at[jnp.where(core == 0, right, left)]),
+        (far_mine, far.at[pl.ds(row_mine, HALF), :]),
+        (far_other, far.at[pl.ds(row_other, HALF), :]),
+    )):
+        copies.append(pltpu.make_async_copy(src, dst, sems.at[n]))
         copies[-1].start()
 
     h_buf[...] = jnp.zeros_like(h_buf)
@@ -80,16 +114,7 @@
     for level in range(LEVELS):
         first, last = FWD_TILES[level]
 
-        def gather(t, carry, level=level):
-            src = h_buf[level, pl.ds(pl.multiple_of(t * TILE, TILE), 2 * TILE), :]
-            dst = pl.ds(pl.multiple_of(t * TILE, TILE), TILE)
-            rows = jnp.dot(s_buf[t], src, preferred_element_type=F32).astype(BF)
-            gat[dst, :C] = src[PAD:PAD + TILE]
-            for k in range(1, TAPS):
-                gat[dst, k * C:(k + 1) * C] = rows[(k - 1) * TILE:k * TILE]
-            return carry
-
-        lax.fori_loop(first, last, gather, 0)
+        expand_all(gat, first, last, h_buf.at[level], s_buf, 3)
         lo, hi = first * TILE, last * TILE
         act = jnp.dot(gat[lo:hi, :], w_buf[level], preferred_element_type=F32)
         squash = jnp.tanh(act)
@@ -105,16 +130,7 @@
             g_buf[PAD + lo:PAD + hi, :].astype(F32) * der[level, lo:hi, :]).astype(BF)
         first, last = BWD_TILES[level]
 
-        def spread(t, carry):
-            src = pre_buf[pl.ds(pl.multiple_of(t * TILE, TILE), 2 * TILE), :]
-            dst = pl.ds(pl.multiple_of(t * TILE, TILE), TILE)
-            rows = jnp.dot(st_buf[t], src, preferred_element_type=F32).astype(BF)
-            gat[dst, :C] = src[PAD:PAD + TILE]
-            for k in range(1, TAPS):
-                gat[dst, k * C:(k + 1) * C] = rows[(k - 1) * TILE:k * TILE]
-            return carry
-
-        lax.fori_loop(first, last, spread, 0)
+        expand_all(gat, first, last, pre_buf, st_buf, 3)
         lo, hi = first * TILE, last * TILE
         total = g_buf[PAD + lo:PAD + hi, :].astype(F32)
         for k in range(TAPS):
@@ -178,7 +194,7 @@
 
 VMEM = pl.BlockSpec(memory_space=pltpu.VMEM)
 SMEM = pl.BlockSpec(memory_space=pltpu.SMEM)
-ANY = pl.BlockSpec(memory_space=pl.ANY)
+HBM = pl.BlockSpec(memory_space=pltpu.HBM)
 INTERPRET = False
 
 
@@ -196,22 +212,48 @@
     )
 
 
+def stack_call(*operands):
+    tiles = FWD_TILES[0][1]
+    return call(
+        stack_kernel,
+        [jax.ShapeDtypeStruct((LEVELS, MSG, C), BF), jax.ShapeDtypeStruct((2 * PROWS, 128), F32)],
+        [SMEM] + [VMEM] * 7 + [HBM] * 5,
+        [
+            pltpu.VMEM((LEVELS, TAPS * C, C), BF),
+            pltpu.VMEM((LEVELS, ROWS, C), BF),
+            pltpu.VMEM((ROWS, 128), F32),
+            pltpu.VMEM((tiles, (TAPS - 1) * TILE, 2 * TILE), BF),
+            pltpu.VMEM((BWD_TILES[3][1], (TAPS - 1) * TILE, 2 * TILE), BF),
+            pltpu.VMEM((tiles * TILE, TAPS * C), BF),
+            pltpu.VMEM((LEVELS, tiles * TILE, C), F32),
+            pltpu.VMEM((ROWS, C), BF),
+            pltpu.VMEM((ROWS, C), BF),
+            pltpu.SemaphoreType.DMA((5,)),
+        ],
+        flops=6 * 10**9, nbytes=6 * 10**6,
+    )(*operands)
+
+
 def shift(axis_size, by):
     return [(i, (i + by) % axis_size) for i in range(axis_size)]
 
 
-def body(maps, upstream, weights, neighbours):
+def step(maps, upstream, weights, neighbours):
     micro = maps.shape[0]
     section = lax.axis_index("section")
     core = lax.axis_index("core")
     patches = lax.axis_size("py") * lax.axis_size("core")
     patch = lax.axis_index("py") * lax.axis_size("core") + core
     npix = PIX * patches
-    cores = core.reshape((1,)).astype(jnp.int32)
-
-    half = lax.dynamic_slice_in_dim(weights[0], core * HALF, HALF, axis=0)
-    w_mine = lax.all_gather(half, "section")
-    w_other = lax.ppermute(w_mine, "core", shift(2, 1))
+    cores = jnp.stack([core, section]).astype(jnp.int32)
+
+    sections = lax.axis_size("section")
+    ways = [(2 * i + c, 2 * ((i + (1, -1)[c]) % sections) + c) for i in range(sections) for c in range(2)]
+    near = lax.ppermute(weights[0], ("section", "core"), ways)
+    half = lax.dynamic_slice_in_dim(near, core * HALF, HALF, axis=0)
+    far = lax.ppermute(half, ("section", "core"), ways)
+    near_other = lax.ppermute(near, "core", shift(2, 1))
+    far_other = lax.ppermute(far, "core", shift(2, 1))
 
     place = patch * PIX + jnp.arange(PIX, dtype=jnp.int32)
     offsets = jnp.mod(neighbours - place[None, :] + HALO, npix) - HALO
@@ -228,25 +270,7 @@
     m3a = send(own[PIX - edge:, :C + 128], perm=shift(patches, 3))
     m3b = send(own[:edge, :C + 128], perm=shift(patches, -3))
 
-    tiles = FWD_TILES[0][1]
-    out, offp = call(
-        stack_kernel,
-        [jax.ShapeDtypeStruct((LEVELS, MSG, C), BF), jax.ShapeDtypeStruct((2 * PROWS, 128), F32)],
-        [SMEM] + [VMEM] * 7 + [ANY] * 2,
-        [
-            pltpu.VMEM((LEVELS, TAPS * C, C), BF),
-            pltpu.VMEM((LEVELS, ROWS, C), BF),
-            pltpu.VMEM((ROWS, 128), F32),
-            pltpu.VMEM((tiles, (TAPS - 1) * TILE, 2 * TILE), BF),
-            pltpu.VMEM((BWD_TILES[3][1], (TAPS - 1) * TILE, 2 * TILE), BF),
-            pltpu.VMEM((tiles * TILE, TAPS * C), BF),
-            pltpu.VMEM((LEVELS, tiles * TILE, C), F32),
-            pltpu.VMEM((ROWS, C), BF),
-            pltpu.VMEM((ROWS, C), BF),
-            pltpu.SemaphoreType.DMA((2,)),
-        ],
-        flops=6 * 10**9, nbytes=6 * 10**6,
-    )(cores, m3a, m2a, m1a, own, m1b, m2b, m3b, w_mine, w_other)
+    out, offp = stack_call(cores, m3a, m2a, m1a, own, m1b, m2b, m3b, weights[0], near, near_other, far, far_other)
 
     mine = lax.all_to_all(out, "section", 0, 0, tiled=True)
     other = lax.ppermute(mine[:, :HROWS + PROWS], "core", shift(2, 1))
@@ -288,4 +312,4 @@
         P(None, patch),
     )
     out_specs = (P("section", None, "dp", patch, None), P("section", None, None))
-    return jax.shard_map(body, mesh=fine, in_specs=in_specs, out_specs=out_specs, check_vma=False)
+    return jax.shard_map(step, mesh=fine, in_specs=in_specs, out_specs=out_specs, check_vma=False)

time: 194 us -> 168 us (0.87)
  waiting for transfers between devices: 54.3 us -> 24.9 us
  starting transfers between devices: 28.6 us -> 48.8 us
  between operations: 14.2 us -> 0.85 us
  local copies, waits for them, and re-layouts: 6.11 us -> 1.83 us
  blocking collectives: 67.9 us -> 70.4 us
    all_gather x1 -> x0, waiting for transfers between devices: 45 us -> none  [body(): w_mine = lax.all_gather(half, 'section')]
    ppermute x9 -> x12, starting transfers between devices: 28.6 us -> 48.8 us  [the longest x1 10.7 us: step(): far_other = lax.ppermute(far, 'core', shift(2, 1))]
    ppermute x9 -> x12, waiting for transfers between devices: 9.35 us -> 24.9 us  [the longest x1 13.4 us: step(): near = lax.ppermute(weights[0], ('section', 'core'), ways)]
    unnamed x6, local copies, waits for them, and re-layouts: 2.88 us -> 0.02 us
    all_to_all x3, blocking collectives: 67.9 us -> 70.4 us  [the longest x1 31.3 us: step(): lax.all_to_all(part.reshape((chips, rows // chips, 128)), ('dp', 'py'), 0...]
  transfers between devices with their start and end apart: 10 -> 12, of which waited for: 5 -> 7; matrix products, arithmetic and copies ran while one was open for 2% -> 1% of each run, Pallas kernels for 0% -> 0%
where the time goes in v3:
time: 168 us; the launch traced here: 167 us
  blocking collectives  70.4 us (42%)
  starting transfers between devices  48.8 us (29%)
  waiting for transfers between devices  24.9 us (15%)
  Pallas kernels  20 us (12%)
  local copies, waits for them, and re-layouts  1.83 us (1%)
    all_to_all x1, blocking collectives, step(): lax.all_to_all(part.reshape((chips, rows // chips, 128)), ('dp', 'py'), 0...  31.3 us
    all_to_all x1, blocking collectives, step(): lax.all_to_all(total, ('dp', 'py'), 0, 0, tiled=True).reshape((rows, 128))  25.5 us
    pallas_call x1, Pallas kernels, stack_call(): call(stack_kernel, [jax.ShapeDtypeStruct((LEVELS, MSG, C), BF), jax.Shape...  14.8 us
    all_to_all x1, blocking collectives, step(): mine = lax.all_to_all(out, 'section', 0, 0, tiled=True)  13.6 us
    ppermute x1, waiting for transfers between devices, step(): near = lax.ppermute(weights[0], ('section', 'core'), ways)  13.4 us
    ppermute x1, starting transfers between devices, step(): far_other = lax.ppermute(far, 'core', shift(2, 1))  10.7 us
    ppermute x1, starting transfers between devices, step(): near_other = lax.ppermute(near, 'core', shift(2, 1))  6.61 us
    ppermute x1, starting transfers between devices, step(): swapped = lax.ppermute(full, 'core', shift(2, 1))  6.34 us
  transfers between devices with their start and end apart: 12, of which 7 were waited for; matrix products, arithmetic and copies ran while one was open for 1% of the time, Pallas kernels for 0%

profile of v3, /device:TPU:1, one launch (start us, length us, event | category | flops | bytes accessed | tf_op | source)
XLA Modules:
  0.0 167.0 jit_solution(16453778023691104428)
XLA Ops:
  0.7 5.3 %collective-permute-start.6 = (bf16[2304,256]{1,0:T(8,128)(2,1)}, bf16[2304,256]{1,0:T(8,128)(2,1)S(1)}, u32[]{:S(2)}, u32[]{:S(2)}) collective-permute-start(bf16[2304,256]{1,0:T(8,128)(2,1)} %bitcast.18), channel_id=1, source_target_pairs={{0,16},{1,49},{16,32},{17,1},{32,48},{33,17},{48,0},{49,33},{2,18}... | collective-permute-start | bytes 3538952 | tf_op jit(solution)/shard_map/ppermute | solution.py:252
  6.0 13.4 %collective-permute-done.6.near_mine = bf16[2304,256]{1,0:T(8,128)(2,1)S(1)} collective-permute-done((bf16[2304,256]{1,0:T(8,128)(2,1)}, bf16[2304,256]{1,0:T(8,128)(2,1)S(1)}, u32[]{:S(2)}, u32[]{:S(2)}) %collective-permute-start.6) | collective-permute-done | bytes 1179680 | tf_op jit(solution)/shard_map/ppermute | solution.py:252
  19.5 0.9 constant_dynamic-slice_fusion
  20.3 4.9 %collective-permute-start.8 = (bf16[1152,256]{1,0:T(8,128)(2,1)}, bf16[1152,256]{1,0:T(8,128)(2,1)S(1)}, u32[]{:S(2)}, u32[]{:S(2)}) collective-permute-start(bf16[1152,256]{1,0:T(8,128)(2,1)} %constant_dynamic-slice_fusion), channel_id=1, source_target_pairs={{0,16},{1,49},{16,32},{17,1},{32,48},{33,17},{48,0},{49,33},{2,18}... | collective-permute-start | bytes 1769480 | tf_op jit(solution)/shard_map/ppermute | solution.py:254
  25.2 6.6 %collective-permute-start.7 = (bf16[2304,256]{1,0:T(8,128)(2,1)S(1)}, bf16[2304,256]{1,0:T(8,128)(2,1)}, u32[]{:S(2)}, u32[]{:S(2)}) collective-permute-start(bf16[2304,256]{1,0:T(8,128)(2,1)S(1)} %collective-permute-done.6.near_mine), channel_id=1, source_target_pairs={{0,1},{1,0},{2,3},{3,2},{4,5},{5,4},{6,7},{7,6},{8,9},{9,8},{10,11... | collective-permute-start | bytes 3538952 | tf_op jit(solution)/shard_map/ppermute | solution.py:255
  32.3 10.7 %collective-permute-start.9 = (bf16[1152,256]{1,0:T(8,128)(2,1)S(1)}, bf16[1152,256]{1,0:T(8,128)(2,1)S(1)}, u32[]{:S(2)}, u32[]{:S(2)}) collective-permute-start(bf16[1152,256]{1,0:T(8,128)(2,1)S(1)} %collective-permute-done.8.far_mine), channel_id=1, source_target_pairs={{0,1},{1,0},{2,3},{3,2},{4,5},{5,4},{6,7},{7,6},{8,9},{9,8},{10,11... | collective-permute-start | bytes 1769480 | tf_op jit(solution)/shard_map/ppermute | solution.py:256
  43.1 0.8 dynamic-slice_bitcast_fusion
  44.0 1.9 %collective-permute-start.4 = (bf16[96,640]{1,0:T(8,128)(2,1)S(1)}, bf16[96,640]{1,0:T(8,128)(2,1)S(1)}, u32[]{:S(2)}, u32[]{:S(2)}) collective-permute-start(bf16[96,640]{1,0:T(8,128)(2,1)S(1)} %pad_maximum_fusion.own), channel_id=1, source_target_pairs={{0,14},{1,15},{2,0},{3,1},{4,2},{5,3},{6,4},{7,5},{8,6},{9,7},{10,... | collective-permute-start | bytes 368648 | tf_op jit(solution)/shard_map/ppermute | solution.py:269
  45.9 1.9 %collective-permute-start.5 = (bf16[64,384]{1,0:T(8,128)(2,1)S(1)}, bf16[64,384]{1,0:T(8,128)(2,1)S(1)}, u32[]{:S(2)}, u32[]{:S(2)}) collective-permute-start(bf16[64,384]{1,0:T(8,128)(2,1)S(1)} %get-tuple-element.14), channel_id=1, source_target_pairs={{0,13},{1,14},{2,15},{3,0},{4,1},{5,2},{6,3},{7,4},{8,5},{9,6},{10... | collective-permute-start | bytes 147464 | tf_op jit(solution)/shard_map/ppermute | solution.py:271
  47.8 4.5 %collective-permute-start = (bf16[64,384]{1,0:T(8,128)(2,1)S(1)}, bf16[64,384]{1,0:T(8,128)(2,1)S(1)}, u32[]{:S(2)}, u32[]{:S(2)}) collective-permute-start(bf16[64,384]{1,0:T(8,128)(2,1)S(1)} %get-tuple-element.15), channel_id=1, source_target_pairs={{0,3},{1,4},{2,5},{3,6},{4,7},{5,8},{6,9},{7,10},{8,11},{9,12},{10... | collective-permute-start | bytes 147464 | tf_op jit(solution)/shard_map/ppermute | solution.py:270
  52.6 2.6 %collective-permute-done.m3a = bf16[64,384]{1,0:T(8,128)(2,1)S(1)} collective-permute-done((bf16[64,384]{1,0:T(8,128)(2,1)S(1)}, bf16[64,384]{1,0:T(8,128)(2,1)S(1)}, u32[]{:S(2)}, u32[]{:S(2)}) %collective-permute-start) | collective-permute-done | bytes 49184 | tf_op jit(solution)/shard_map/ppermute | solution.py:270
  55.2 2.0 %collective-permute-start.2 = (bf16[96,640]{1,0:T(8,128)(2,1)S(1)}, bf16[96,640]{1,0:T(8,128)(2,1)S(1)}, u32[]{:S(2)}, u32[]{:S(2)}) collective-permute-start(bf16[96,640]{1,0:T(8,128)(2,1)S(1)} %pad_maximum_fusion.own), channel_id=1, source_target_pairs={{0,1},{1,2},{2,3},{3,4},{4,5},{5,6},{6,7},{7,8},{8,9},{9,10},{10,1... | collective-permute-start | bytes 368648 | tf_op jit(solution)/shard_map/ppermute | solution.py:266
  57.3 1.9 %collective-permute-start.1 = (bf16[96,640]{1,0:T(8,128)(2,1)S(1)}, bf16[96,640]{1,0:T(8,128)(2,1)S(1)}, u32[]{:S(2)}, u32[]{:S(2)}) collective-permute-start(bf16[96,640]{1,0:T(8,128)(2,1)S(1)} %pad_maximum_fusion.own), channel_id=1, source_target_pairs={{0,2},{1,3},{2,4},{3,5},{4,6},{5,7},{6,8},{7,9},{8,10},{9,11},{10,... | collective-permute-start | bytes 368648 | tf_op jit(solution)/shard_map/ppermute | solution.py:268
  59.3 5.2 %collective-permute-done.1.m2a = bf16[96,640]{1,0:T(8,128)(2,1)S(1)} collective-permute-done((bf16[96,640]{1,0:T(8,128)(2,1)S(1)}, bf16[96,640]{1,0:T(8,128)(2,1)S(1)}, u32[]{:S(2)}, u32[]{:S(2)}) %collective-permute-start.1) | collective-permute-done | bytes 122912 | tf_op jit(solution)/shard_map/ppermute | solution.py:268
  64.5 14.8 %shard_map.59 = (bf16[4,320,256]{2,1,0:T(8,128)(2,1)S(1)}, f32[256,128]{1,0:T(8,128)S(1)}) custom-call(s32[2]{0:T(128)S(1)} %pad_add_fusion.ids_ref.core_ref, bf16[64,384]{1,0:T(8,128)(2,1)S(1)} %collective-permute-done.m3a, bf16[96,640]{1,0:T(8,128)(2,1)S(1)} %collective-permute-done.1.m2a, bf16[96,640]{1,0:T(8,128)(2,1)S(1)} %collective-permute-done.2.m1a, ...), custom_call_target="tpu_custom_call" | custom-call | flops 6000000000 | bytes 6000000 | tf_op jit(solution)/shard_map/pallas_call | solution.py:217
  79.3 13.6 %all_to_all.15.mine = bf16[4,320,256]{2,1,0:T(8,128)(2,1)S(1)} all-to-all(bf16[4,320,256]{2,1,0:T(8,128)(2,1)S(1)} %get-tuple-element.6), channel_id=1, replica_groups=mesh['dp'=8,'section'=4,'py'=8,'core'=2] {'section'}, dimensions={0} | all-to-all | bytes 1310720 | tf_op jit(solution)/shard_map/all_to_all | solution.py:275
  93.0 2.5 %collective-permute-start.10 = (bf16[4,224,256]{2,1,0:T(8,128)(2,1)S(1)}, bf16[4,224,256]{2,1,0:T(8,128)(2,1)S(1)}, u32[]{:S(2)}, u32[]{:S(2)}) collective-permute-start(bf16[4,224,256]{2,1,0:T(8,128)(2,1)S(1)} %slice.16), channel_id=1, source_target_pairs={{0,1},{1,0},{2,3},{3,2},{4,5},{5,4},{6,7},{7,6},{8,9},{9,8},{10,11... | collective-permute-start | bytes 1376264 | tf_op jit(solution)/shard_map/ppermute | solution.py:276
  95.5 1.4 collective-permute-done.10.other
  96.9 3.3 %shard_map.60 = (bf16[2560,128]{1,0:T(8,128)(2,1)S(1)}, bf16[4,96,256]{2,1,0:T(8,128)(2,1)}) custom-call(s32[2]{0:T(128)S(1)} %pad_add_fusion.ids_ref.core_ref, bf16[4,320,256]{2,1,0:T(8,128)(2,1)S(1)} %all_to_all.15.mine, bf16[4,224,256]{2,1,0:T(8,128)(2,1)S(1)} %collective-permute-done.10.other, f32[256,128]{1,0:T(8,128)S(1)} %get-tuple-element.7.offp), custom_call_target="tpu_custom_call" | custom-call | flops 1000000000 | bytes 2000000 | tf_op jit(solution)/shard_map/pallas_call | solution.py:279
  100.2 31.3 %all_to_all.16.x_ref = bf16[64,40,128]{2,1,0:T(8,128)(2,1)S(1)} all-to-all(bf16[64,40,128]{2,1,0:T(8,128)(2,1)S(1)} %bitcast.17), channel_id=1, replica_groups=mesh['dp'=8,'section'=4,'py'=8,'core'=2] {'dp','py'}, dimensions={0} | all-to-all | bytes 1310720 | tf_op jit(solution)/shard_map/all_to_all | solution.py:291
  131.6 25.5 %all_to_all.17 = bf16[64,40,128]{2,1,0:T(8,128)(2,1)S(1)} all-to-all(bf16[64,40,128]{2,1,0:T(8,128)(2,1)S(1)} %shard_map.61), channel_id=1, replica_groups=mesh['dp'=8,'section'=4,'py'=8,'core'=2] {'dp','py'}, dimensions={0} | all-to-all | bytes 1310720 | tf_op jit(solution)/shard_map/all_to_all | solution.py:295
  157.2 6.3 %collective-permute-start.11 = (bf16[2560,128]{1,0:T(8,128)(2,1)S(1)}, bf16[2560,128]{1,0:T(8,128)(2,1)S(1)}, u32[]{:S(2)}, u32[]{:S(2)}) collective-permute-start(bf16[2560,128]{1,0:T(8,128)(2,1)S(1)} %bitcast.15), channel_id=1, source_target_pairs={{0,1},{1,0},{2,3},{3,2},{4,5},{5,4},{6,7},{7,6},{8,9},{9,8},{10,11... | collective-permute-start | bytes 1966088 | tf_op jit(solution)/shard_map/ppermute | solution.py:296
  163.5 1.7 %collective-permute-done.11.other = bf16[2560,128]{1,0:T(8,128)(2,1)S(1)} collective-permute-done((bf16[2560,128]{1,0:T(8,128)(2,1)S(1)}, bf16[2560,128]{1,0:T(8,128)(2,1)S(1)}, u32[]{:S(2)}, u32[]{:S(2)}) %collective-permute-start.11) | collective-permute-done | bytes 655392 | tf_op jit(solution)/shard_map/ppermute | solution.py:296
  165.2 1.8 %shard_map.62 = bf16[2304,256]{1,0:T(8,128)(2,1)} custom-call(s32[2]{0:T(128)S(1)} %pad_add_fusion.ids_ref.core_ref, bf16[2560,128]{1,0:T(8,128)(2,1)S(1)} %bitcast.16, bf16[2560,128]{1,0:T(8,128)(2,1)S(1)} %collective-permute-done.11.other), custom_call_target="tpu_custom_call" | custom-call | bytes 2000000 | tf_op jit(solution)/shard_map/pallas_call | solution.py:297
  (25 shorter events, 1.0 us)
Async XLA Ops:
  0.6 42.5 %copy-start = (bf16[4,1,96,256]{3,2,1,0:T(8,128)(2,1)S(1)}, bf16[4,1,96,256]{3,2,1,0:T(8,128)(2,1)}, u32[]{:S(2)}) copy-start(bf16[4,1,96,256]{3,2,1,0:T(8,128)(2,1)} %param.4) | copy-start | bytes 589828
  0.6 63.8 %copy-start.1 = (bf16[1,2304,256]{2,1,0:T(8,128)(2,1)S(1)}, bf16[1,2304,256]{2,1,0:T(8,128)(2,1)}, u32[]{:S(2)}) copy-start(bf16[1,2304,256]{2,1,0:T(8,128)(2,1)} %param.6) | copy-start | bytes 3538948
  0.7 31.2 %copy-start.2 = (s32[9,96]{1,0:T(8,128)S(1)}, s32[9,96]{1,0:T(8,128)}, u32[]{:S(2)}) copy-start(s32[9,96]{1,0:T(8,128)} %param.7) | copy-start | bytes 10372
  0.7 18.8 %collective-permute-start.6 = (bf16[2304,256]{1,0:T(8,128)(2,1)}, bf16[2304,256]{1,0:T(8,128)(2,1)S(1)}, u32[]{:S(2)}, u32[]{:S(2)}) collective-permute-start(bf16[2304,256]{1,0:T(8,128)(2,1)} %bitcast.18), channel_id=1, source_target_pairs={{0,16},{1,49},{16,32},{17,1},{32,48},{33,17},{48,0},{49,33},{2,18}... | collective-permute-start | bytes 3538952 | tf_op jit(solution)/shard_map/ppermute | solution.py:252
  20.3 12.0 %collective-permute-start.8 = (bf16[1152,256]{1,0:T(8,128)(2,1)}, bf16[1152,256]{1,0:T(8,128)(2,1)S(1)}, u32[]{:S(2)}, u32[]{:S(2)}) collective-permute-start(bf16[1152,256]{1,0:T(8,128)(2,1)} %constant_dynamic-slice_fusion), channel_id=1, source_target_pairs={{0,16},{1,49},{16,32},{17,1},{32,48},{33,17},{48,0},{49,33},{2,18}... | collective-permute-start | bytes 1769480 | tf_op jit(solution)/shard_map/ppermute | solution.py:254
  25.2 39.3 %collective-permute-start.7 = (bf16[2304,256]{1,0:T(8,128)(2,1)S(1)}, bf16[2304,256]{1,0:T(8,128)(2,1)}, u32[]{:S(2)}, u32[]{:S(2)}) collective-permute-start(bf16[2304,256]{1,0:T(8,128)(2,1)S(1)} %collective-permute-done.6.near_mine), channel_id=1, source_target_pairs={{0,1},{1,0},{2,3},{3,2},{4,5},{5,4},{6,7},{7,6},{8,9},{9,8},{10,11... | collective-permute-start | bytes 3538952 | tf_op jit(solution)/shard_map/ppermute | solution.py:255
  32.3 32.1 %collective-permute-start.9 = (bf16[1152,256]{1,0:T(8,128)(2,1)S(1)}, bf16[1152,256]{1,0:T(8,128)(2,1)S(1)}, u32[]{:S(2)}, u32[]{:S(2)}) collective-permute-start(bf16[1152,256]{1,0:T(8,128)(2,1)S(1)} %collective-permute-done.8.far_mine), channel_id=1, source_target_pairs={{0,1},{1,0},{2,3},{3,2},{4,5},{5,4},{6,7},{7,6},{8,9},{9,8},{10,11... | collective-permute-start | bytes 1769480 | tf_op jit(solution)/shard_map/ppermute | solution.py:256
  44.0 13.3 %collective-permute-start.4 = (bf16[96,640]{1,0:T(8,128)(2,1)S(1)}, bf16[96,640]{1,0:T(8,128)(2,1)S(1)}, u32[]{:S(2)}, u32[]{:S(2)}) collective-permute-start(bf16[96,640]{1,0:T(8,128)(2,1)S(1)} %pad_maximum_fusion.own), channel_id=1, source_target_pairs={{0,14},{1,15},{2,0},{3,1},{4,2},{5,3},{6,4},{7,5},{8,6},{9,7},{10,... | collective-permute-start | bytes 368648 | tf_op jit(solution)/shard_map/ppermute | solution.py:269
  45.9 6.7 %collective-permute-start.5 = (bf16[64,384]{1,0:T(8,128)(2,1)S(1)}, bf16[64,384]{1,0:T(8,128)(2,1)S(1)}, u32[]{:S(2)}, u32[]{:S(2)}) collective-permute-start(bf16[64,384]{1,0:T(8,128)(2,1)S(1)} %get-tuple-element.14), channel_id=1, source_target_pairs={{0,13},{1,14},{2,15},{3,0},{4,1},{5,2},{6,3},{7,4},{8,5},{9,6},{10... | collective-permute-start | bytes 147464 | tf_op jit(solution)/shard_map/ppermute | solution.py:271
  47.8 7.4 %collective-permute-start = (bf16[64,384]{1,0:T(8,128)(2,1)S(1)}, bf16[64,384]{1,0:T(8,128)(2,1)S(1)}, u32[]{:S(2)}, u32[]{:S(2)}) collective-permute-start(bf16[64,384]{1,0:T(8,128)(2,1)S(1)} %get-tuple-element.15), channel_id=1, source_target_pairs={{0,3},{1,4},{2,5},{3,6},{4,7},{5,8},{6,9},{7,10},{8,11},{9,12},{10... | collective-permute-start | bytes 147464 | tf_op jit(solution)/shard_map/ppermute | solution.py:270
  52.6 6.7 %collective-permute-start.3 = (bf16[96,640]{1,0:T(8,128)(2,1)S(1)}, bf16[96,640]{1,0:T(8,128)(2,1)S(1)}, u32[]{:S(2)}, u32[]{:S(2)}) collective-permute-start(bf16[96,640]{1,0:T(8,128)(2,1)S(1)} %pad_maximum_fusion.own), channel_id=1, source_target_pairs={{0,15},{1,0},{2,1},{3,2},{4,3},{5,4},{6,5},{7,6},{8,7},{9,8},{10,9... | collective-permute-start | bytes 368648 | tf_op jit(solution)/shard_map/ppermute | solution.py:267
  55.2 4.0 %collective-permute-start.2 = (bf16[96,640]{1,0:T(8,128)(2,1)S(1)}, bf16[96,640]{1,0:T(8,128)(2,1)S(1)}, u32[]{:S(2)}, u32[]{:S(2)}) collective-permute-start(bf16[96,640]{1,0:T(8,128)(2,1)S(1)} %pad_maximum_fusion.own), channel_id=1, source_target_pairs={{0,1},{1,2},{2,3},{3,4},{4,5},{5,6},{6,7},{7,8},{8,9},{9,10},{10,1... | collective-permute-start | bytes 368648 | tf_op jit(solution)/shard_map/ppermute | solution.py:266
  57.3 7.2 %collective-permute-start.1 = (bf16[96,640]{1,0:T(8,128)(2,1)S(1)}, bf16[96,640]{1,0:T(8,128)(2,1)S(1)}, u32[]{:S(2)}, u32[]{:S(2)}) collective-permute-start(bf16[96,640]{1,0:T(8,128)(2,1)S(1)} %pad_maximum_fusion.own), channel_id=1, source_target_pairs={{0,2},{1,3},{2,4},{3,5},{4,6},{5,7},{6,8},{7,9},{8,10},{9,11},{10,... | collective-permute-start | bytes 368648 | tf_op jit(solution)/shard_map/ppermute | solution.py:268
  93.0 4.0 %collective-permute-start.10 = (bf16[4,224,256]{2,1,0:T(8,128)(2,1)S(1)}, bf16[4,224,256]{2,1,0:T(8,128)(2,1)S(1)}, u32[]{:S(2)}, u32[]{:S(2)}) collective-permute-start(bf16[4,224,256]{2,1,0:T(8,128)(2,1)S(1)} %slice.16), channel_id=1, source_target_pairs={{0,1},{1,0},{2,3},{3,2},{4,5},{5,4},{6,7},{7,6},{8,9},{9,8},{10,11... | collective-permute-start | bytes 1376264 | tf_op jit(solution)/shard_map/ppermute | solution.py:276
  157.2 8.1 %collective-permute-start.11 = (bf16[2560,128]{1,0:T(8,128)(2,1)S(1)}, bf16[2560,128]{1,0:T(8,128)(2,1)S(1)}, u32[]{:S(2)}, u32[]{:S(2)}) collective-permute-start(bf16[2560,128]{1,0:T(8,128)(2,1)S(1)} %bitcast.15), channel_id=1, source_target_pairs={{0,1},{1,0},{2,3},{3,2},{4,5},{5,4},{6,7},{7,6},{8,9},{9,8},{10,11... | collective-permute-start | bytes 1966088 | tf_op jit(solution)/shard_map/ppermute | solution.py:296

commit v4 on v3

--- a/solution.py
+++ b/solution.py
@@ -56,35 +56,20 @@
         one(t)
 
 
-def stack_kernel(ids_ref, m3a, m2a, m1a, own, m1b, m2b, m3b, w_own, near_mine, near_other, far_mine, far_other,
-                 out_ref, offp_ref, w_buf, h_buf, off_buf, s_buf, st_buf, gat, der, pre_buf, g_buf, sems):
-    core, section = ids_ref[0], ids_ref[1]
-    left, right = lax.rem(section + 3, LEVELS), lax.rem(section + 1, LEVELS)
-    far = w_buf.at[lax.rem(section + 2, LEVELS)]
-    row_mine = pl.multiple_of(core * HALF, HALF)
-    row_other = pl.multiple_of((1 - core) * HALF, HALF)
-    copies = []
-    for n, (src, dst) in enumerate((
-        (w_own, w_buf.at[section]),
-        (near_mine, w_buf.at[jnp.where(core == 0, left, right)]),
-        (near_other, w_buf.at[jnp.where(core == 0, right, left)]),
-        (far_mine, far.at[pl.ds(row_mine, HALF), :]),
-        (far_other, far.at[pl.ds(row_other, HALF), :]),
-    )):
-        copies.append(pltpu.make_async_copy(src, dst, sems.at[n]))
-        copies[-1].start()
-
-    h_buf[...] = jnp.zeros_like(h_buf)
-    off_buf[...] = jnp.zeros_like(off_buf)
-    pre_buf[...] = jnp.zeros_like(pre_buf)
-    g_buf[...] = jnp.zeros_like(g_buf)
+def prep_kernel(ids_ref, m3a, m2a, m1a, own, m1b, m2b, m3b, h_ref, g_ref, s_ref, st_ref, gat_ref, pair_ref, off_buf):
+    core = ids_ref[0]
+    h_ref[:PAD, :] = jnp.zeros((PAD, C), BF)
+    h_ref[ROWS - PAD:, :] = jnp.zeros((PAD, C), BF)
+    g_ref[...] = jnp.zeros_like(g_ref)
+    off_buf[:PAD, :] = jnp.zeros((PAD, 128), F32)
+    off_buf[ROWS - PAD:, :] = jnp.zeros((PAD, 128), F32)
     at = PAD
     for piece in (m3a, m2a, m1a, own, m1b, m2b, m3b):
         n = piece.shape[0]
-        h_buf[0, at:at + n, :] = piece[:, :C]
+        h_ref[at:at + n, :] = piece[:, :C]
         off_buf[at:at + n, :] = piece[:, C:C + 128].astype(F32)
         if piece.shape[1] > C + 128:
-            g_buf[at:at + n, :] = piece[:, C + 128:]
+            g_ref[at:at + n, :] = piece[:, C + 128:]
         at += n
 
     rel = (lax.broadcasted_iota(jnp.int32, (TILE, 128), 1)
@@ -94,7 +79,7 @@
         d = off_buf[pl.ds(pl.multiple_of(t * TILE + PAD, PAD), TILE), :]
         for k in range(1, TAPS):
             hit = rel == d[:, k:k + 1]
-            s_buf[t, (k - 1) * TILE:k * TILE, :] = jnp.where(hit, 1.0, 0.0).astype(BF)
+            s_ref[t, (k - 1) * TILE:k * TILE, :] = jnp.where(hit, 1.0, 0.0).astype(BF)
         return carry
 
     lax.fori_loop(0, FWD_TILES[0][1], build_s, 0)
@@ -103,26 +88,61 @@
         d = jnp.transpose(off_buf[pl.ds(pl.multiple_of(t * TILE, TILE), 128), :])
         for k in range(1, TAPS):
             hit = -rel == d[k:k + 1, :]
-            st_buf[t, (k - 1) * TILE:k * TILE, :] = jnp.where(hit, 1.0, 0.0).astype(BF)
+            st_ref[t, (k - 1) * TILE:k * TILE, :] = jnp.where(hit, 1.0, 0.0).astype(BF)
         return carry
 
     lax.fori_loop(BWD_TILES[3][0], BWD_TILES[3][1], build_st, 0)
-
+    expand_all(gat_ref, *FWD_TILES[0], h_ref, s_ref, 3)
+
+    start = pl.multiple_of(PAD + OWN - HALO - PIX * core, HALO)
+    offt = jnp.transpose(off_buf[pl.ds(start, 2 * PROWS), :])
+    apart = (lax.broadcasted_iota(jnp.int32, (2 * PIX, 2 * PROWS), 0)
+             - lax.broadcasted_iota(jnp.int32, (2 * PIX, 2 * PROWS), 1) + HALO).astype(F32)
+    for k in range(1, TAPS):
+        pair_ref[k - 1] = jnp.where(apart == offt[k:k + 1, :], 1.0, 0.0).astype(BF)
+
+
+def stack_kernel(ids_ref, h0, g_top, s_buf, st_buf, gat0, w_own, near1_mine, near1_other, near2_mine, near2_other,
+                 far_mine, far_other, out_ref, w_buf, h_buf, gat, der, pre_buf, g_buf, sems):
+    core, section = ids_ref[0], ids_ref[1]
+    left, right = lax.rem(section + 3, LEVELS), lax.rem(section + 1, LEVELS)
+    mine = w_buf.at[jnp.where(core == 0, left, right)]
+    other = w_buf.at[jnp.where(core == 0, right, left)]
+    far = w_buf.at[lax.rem(section + 2, LEVELS)]
+    here = pl.ds(pl.multiple_of(core * HALF, HALF), HALF)
+    there = pl.ds(pl.multiple_of((1 - core) * HALF, HALF), HALF)
+    copies = []
+    for n, (src, dst) in enumerate((
+        (w_own, w_buf.at[section]),
+        (near1_mine, mine.at[here, :]),
+        (near1_other, other.at[there, :]),
+        (near2_mine, mine.at[there, :]),
+        (near2_other, other.at[here, :]),
+        (far_mine, far.at[here, :]),
+        (far_other, far.at[there, :]),
+    )):
+        copies.append(pltpu.make_async_copy(src, dst, sems.at[n]))
+        copies[-1].start()
+    h_buf[...] = jnp.zeros_like(h_buf)
+    pre_buf[...] = jnp.zeros_like(pre_buf)
+    g_buf[...] = g_top[...]
     for copy in copies:
         copy.wait()
 
     for level in range(LEVELS):
         first, last = FWD_TILES[level]
 
-        expand_all(gat, first, last, h_buf.at[level], s_buf, 3)
+        src = h0 if level == 0 else h_buf.at[level - 1]
+        rows = gat0 if level == 0 else gat
+        if level:
+            expand_all(gat, first, last, src, s_buf, 3)
         lo, hi = first * TILE, last * TILE
-        act = jnp.dot(gat[lo:hi, :], w_buf[level], preferred_element_type=F32)
+        act = jnp.dot(rows[lo:hi, :], w_buf[level], preferred_element_type=F32)
         squash = jnp.tanh(act)
         der[level, lo:hi, :] = 1.0 - squash * squash
         if level + 1 < LEVELS:
-            h_buf[level + 1, PAD + lo:PAD + hi, :] = (
-                h_buf[level, PAD + lo:PAD + hi, :].astype(F32) + squash).astype(BF)
-        out_ref[level, :HROWS, :] = h_buf[level, PAD + OWN:PAD + OWN + PIX, :]
+            h_buf[level, PAD + lo:PAD + hi, :] = (src[PAD + lo:PAD + hi, :].astype(F32) + squash).astype(BF)
+        out_ref[level, :HROWS, :] = src[PAD + OWN:PAD + OWN + PIX, :]
 
     for level in range(LEVELS - 1, -1, -1):
         lo, hi = PRE_ROWS[level]
@@ -142,11 +162,8 @@
         out_ref[level, HROWS:HROWS + PROWS, :] = pre_buf[pl.ds(start, PROWS), :]
         out_ref[level, HROWS + PROWS:, :] = g_buf[PAD + OWN:PAD + OWN + PIX, :]
 
-    start = pl.multiple_of(PAD + OWN - HALO - PIX * core, HALO)
-    offp_ref[...] = off_buf[pl.ds(start, 2 * PROWS), :]
-
-
-def grad_kernel(core_ref, mine, other, offp, out_ref, gin_ref, st_buf, p_buf, h_buf, t_buf):
+
+def grad_kernel(core_ref, mine, other, hot, out_ref, gin_ref, p_buf, h_buf, t_buf):
     core = core_ref[0]
     micro = mine.shape[0]
     pair = 2 * PIX
@@ -160,17 +177,13 @@
                     p_buf[n * PROWS:(n + 1) * PROWS, m * 128:(m + 1) * 128] = (
                         ref[m, HROWS:HROWS + PROWS, c * 128:(c + 1) * 128])
                     h_buf[m * pair + n * PIX:m * pair + (n + 1) * PIX, :] = ref[m, :HROWS, :]
-    rel = (lax.broadcasted_iota(jnp.int32, (pair, 2 * PROWS), 0)
-           - lax.broadcasted_iota(jnp.int32, (pair, 2 * PROWS), 1) + HALO).astype(F32)
-    offt = jnp.transpose(offp[...])
     h_t = jnp.transpose(h_buf[...].astype(F32)).astype(BF)
     pre = p_buf[...]
     for k in range(TAPS):
         if k == 0:
             spread = pre[HALO:HALO + pair]
         else:
-            hit = jnp.where(rel == offt[k:k + 1, :], 1.0, 0.0).astype(BF)
-            spread = jnp.dot(hit, pre, preferred_element_type=F32).astype(BF)
+            spread = jnp.dot(hot[k - 1], pre, preferred_element_type=F32).astype(BF)
         for m in range(micro):
             t_buf[m * pair:(m + 1) * pair, :] = spread[:, m * 128:(m + 1) * 128]
         block = jnp.dot(h_t, t_buf[...], preferred_element_type=F32)
@@ -194,7 +207,7 @@
 
 VMEM = pl.BlockSpec(memory_space=pltpu.VMEM)
 SMEM = pl.BlockSpec(memory_space=pltpu.SMEM)
-HBM = pl.BlockSpec(memory_space=pltpu.HBM)
+ANY = pl.BlockSpec(memory_space=pl.ANY)
 INTERPRET = False
 
 
@@ -212,25 +225,40 @@
     )
 
 
+def prep_call(*operands):
+    tiles, hot = FWD_TILES[0][1], (TAPS - 1) * TILE
+    return call(
+        prep_kernel,
+        [
+            jax.ShapeDtypeStruct((ROWS, C), BF),
+            jax.ShapeDtypeStruct((ROWS, C), BF),
+            jax.ShapeDtypeStruct((tiles, hot, 2 * TILE), BF),
+            jax.ShapeDtypeStruct((BWD_TILES[3][1], hot, 2 * TILE), BF),
+            jax.ShapeDtypeStruct((tiles * TILE, TAPS * C), BF),
+            jax.ShapeDtypeStruct((TAPS - 1, 2 * PIX, 2 * PROWS), BF),
+        ],
+        [SMEM] + [VMEM] * 7,
+        [pltpu.VMEM((ROWS, 128), F32)],
+        flops=10**9, nbytes=6 * 10**6,
+    )(*operands)
+
+
 def stack_call(*operands):
     tiles = FWD_TILES[0][1]
     return call(
         stack_kernel,
-        [jax.ShapeDtypeStruct((LEVELS, MSG, C), BF), jax.ShapeDtypeStruct((2 * PROWS, 128), F32)],
-        [SMEM] + [VMEM] * 7 + [HBM] * 5,
+        jax.ShapeDtypeStruct((LEVELS, MSG, C), BF),
+        [SMEM] + [VMEM] * 5 + [ANY] * 7,
         [
             pltpu.VMEM((LEVELS, TAPS * C, C), BF),
-            pltpu.VMEM((LEVELS, ROWS, C), BF),
-            pltpu.VMEM((ROWS, 128), F32),
-            pltpu.VMEM((tiles, (TAPS - 1) * TILE, 2 * TILE), BF),
-            pltpu.VMEM((BWD_TILES[3][1], (TAPS - 1) * TILE, 2 * TILE), BF),
+            pltpu.VMEM((LEVELS - 1, ROWS, C), BF),
             pltpu.VMEM((tiles * TILE, TAPS * C), BF),
             pltpu.VMEM((LEVELS, tiles * TILE, C), F32),
             pltpu.VMEM((ROWS, C), BF),
             pltpu.VMEM((ROWS, C), BF),
-            pltpu.SemaphoreType.DMA((5,)),
+            pltpu.SemaphoreType.DMA((7,)),
         ],
-        flops=6 * 10**9, nbytes=6 * 10**6,
+        flops=5 * 10**9, nbytes=10 * 10**6,
     )(*operands)
 
 
@@ -249,11 +277,12 @@
 
     sections = lax.axis_size("section")
     ways = [(2 * i + c, 2 * ((i + (1, -1)[c]) % sections) + c) for i in range(sections) for c in range(2)]
-    near = lax.ppermute(weights[0], ("section", "core"), ways)
-    half = lax.dynamic_slice_in_dim(near, core * HALF, HALF, axis=0)
-    far = lax.ppermute(half, ("section", "core"), ways)
-    near_other = lax.ppermute(near, "core", shift(2, 1))
-    far_other = lax.ppermute(far, "core", shift(2, 1))
+    near1 = lax.ppermute(lax.dynamic_slice_in_dim(weights[0], core * HALF, HALF), ("section", "core"), ways)
+    near2 = lax.ppermute(lax.dynamic_slice_in_dim(weights[0], (1 - core) * HALF, HALF), ("section", "core"), ways)
+    far = lax.ppermute(near1, ("section", "core"), ways)
+    parts = []
+    for block in (near1, near2, far):
+        parts += [block, lax.ppermute(block, "core", shift(2, 1))]
 
     place = patch * PIX + jnp.arange(PIX, dtype=jnp.int32)
     offsets = jnp.mod(neighbours - place[None, :] + HALO, npix) - HALO
@@ -270,7 +299,8 @@
     m3a = send(own[PIX - edge:, :C + 128], perm=shift(patches, 3))
     m3b = send(own[:edge, :C + 128], perm=shift(patches, -3))
 
-    out, offp = stack_call(cores, m3a, m2a, m1a, own, m1b, m2b, m3b, weights[0], near, near_other, far, far_other)
+    *window, hot = prep_call(cores, m3a, m2a, m1a, own, m1b, m2b, m3b)
+    out = stack_call(cores, *window, weights[0], *parts)
 
     mine = lax.all_to_all(out, "section", 0, 0, tiled=True)
     other = lax.ppermute(mine[:, :HROWS + PROWS], "core", shift(2, 1))
@@ -281,13 +311,12 @@
         [jax.ShapeDtypeStruct((rows, 128), BF), jax.ShapeDtypeStruct((micro, PIX, C), BF)],
         [SMEM] + [VMEM] * 3,
         [
-            pltpu.VMEM((2 * PIX, 2 * PROWS), BF),
             pltpu.VMEM((2 * PROWS, micro * 128), BF),
             pltpu.VMEM((micro * 2 * PIX, C), BF),
             pltpu.VMEM((micro * 2 * PIX, 128), BF),
         ],
         flops=10**9, nbytes=2 * 10**6,
-    )(cores, mine, other, offp)
+    )(cores, mine, other, hot)
     pieces = lax.all_to_all(part.reshape((chips, rows // chips, 128)), ("dp", "py"), 0, 0, tiled=True)
     total = call(
         sum_kernel, jax.ShapeDtypeStruct(pieces.shape, BF), [VMEM], nbytes=10**6,

time: 168 us -> 169 us (level)
  waiting for transfers between devices: 24.9 us -> 16.9 us
  starting transfers between devices: 48.8 us -> 54.4 us
  Pallas kernels: 20 us -> 24.1 us
  blocking collectives: 70.4 us -> 68.3 us
    ppermute x4 -> x6, waiting for transfers between devices: 13.7 us -> 4.35 us  [the longest x1 4.33 us: step(): lax.ppermute(lax.dynamic_slice_in_dim(weights[0], core * HALF, HALF), ('s...]
    ppermute x1, waiting for transfers between devices: 0.01 us -> 4.76 us  [step(): m2b = send(own, perm=shift(patches, -2))]
    pallas_call x1 -> x2, Pallas kernels: 14.8 us -> 18.9 us  [the longest x1 13.9 us: stack_call(): call(stack_kernel, jax.ShapeDtypeStruct((LEVELS, MSG, C), BF), [SMEM] + [...]
    ppermute x1, starting transfers between devices: 0.01 us -> 3.32 us  [step(): m1b = send(own, perm=shift(patches, -1))]
    ppermute x1, starting transfers between devices: 1.92 us -> 4.85 us  [step(): m3b = send(own[:edge, :C + 128], perm=shift(patches, -3))]
    ppermute x1, waiting for transfers between devices: 2.63 us -> 0.01 us  [step(): m3a = send(own[PIX - edge:, :C + 128], perm=shift(patches, 3))]
    ppermute x1, starting transfers between devices: 4.54 us -> 1.92 us  [step(): m3a = send(own[PIX - edge:, :C + 128], perm=shift(patches, 3))]
    ppermute x4 -> x6, starting transfers between devices: 27.6 us -> 30.1 us  [the longest x3 17.4 us: step(): parts += [block, lax.ppermute(block, 'core', shift(2, 1))]]
  transfers between devices with their start and end apart: 12 -> 14, of which waited for: 7 -> 5; matrix products, arithmetic and copies ran while one was open for 1% -> 1% of each run, Pallas kernels for 0% -> 3%
where the time goes in v4:
time: 169 us; the launch traced here: 168 us
  blocking collectives  68.3 us (40%)
  starting transfers between devices  54.4 us (32%)
  Pallas kernels  24.1 us (14%)
  waiting for transfers between devices  16.9 us (10%)
  local copies, waits for them, and re-layouts  3.35 us (2%)
    all_to_all x1, blocking collectives, step(): lax.all_to_all(part.reshape((chips, rows // chips, 128)), ('dp', 'py'), 0...  30.4 us
    all_to_all x1, blocking collectives, step(): lax.all_to_all(total, ('dp', 'py'), 0, 0, tiled=True).reshape((rows, 128))  25.5 us
    ppermute x3, starting transfers between devices, step(): parts += [block, lax.ppermute(block, 'core', shift(2, 1))]  17.4 us
    pallas_call x1, Pallas kernels, stack_call(): call(stack_kernel, jax.ShapeDtypeStruct((LEVELS, MSG, C), BF), [SMEM] + [...  13.9 us
    all_to_all x1, blocking collectives, step(): mine = lax.all_to_all(out, 'section', 0, 0, tiled=True)  12.4 us
    ppermute x1, starting transfers between devices, step(): swapped = lax.ppermute(full, 'core', shift(2, 1))  6.34 us
    ppermute x1, starting transfers between devices, step(): lax.ppermute(lax.dynamic_slice_in_dim(weights[0], core * HALF, HALF), ('s...  5.2 us
    pallas_call x1, Pallas kernels, prep_call(): call(prep_kernel, [jax.ShapeDtypeStruct((ROWS, C), BF), jax.ShapeDtypeStr...  5.03 us
  transfers between devices with their start and end apart: 14, of which 5 were waited for; matrix products, arithmetic and copies ran while one was open for 1% of the time, Pallas kernels for 3%

profile of v4, /device:TPU:1, one launch (start us, length us, event | category | flops | bytes accessed | tf_op | source)
XLA Modules:
  0.0 168.1 jit_solution(6722376808527993692)
XLA Ops:
  2.0 5.2 %collective-permute-start.6 = (bf16[1152,256]{1,0:T(8,128)(2,1)S(1)}, bf16[1152,256]{1,0:T(8,128)(2,1)S(1)}, u32[]{:S(2)}, u32[]{:S(2)}) collective-permute-start(bf16[1152,256]{1,0:T(8,128)(2,1)S(1)} %get-tuple-element.23), channel_id=1, source_target_pairs={{0,16},{1,49},{16,32},{17,1},{32,48},{33,17},{48,0},{49,33},{2,18}... | collective-permute-start | bytes 1769480 | tf_op jit(solution)/shard_map/ppermute | solution.py:280
  7.2 2.5 %collective-permute-start.8 = (bf16[1152,256]{1,0:T(8,128)(2,1)S(1)}, bf16[1152,256]{1,0:T(8,128)(2,1)S(1)}, u32[]{:S(2)}, u32[]{:S(2)}) collective-permute-start(bf16[1152,256]{1,0:T(8,128)(2,1)S(1)} %get-tuple-element.22), channel_id=1, source_target_pairs={{0,16},{1,49},{16,32},{17,1},{32,48},{33,17},{48,0},{49,33},{2,18}... | collective-permute-start | bytes 1769480 | tf_op jit(solution)/shard_map/ppermute | solution.py:281
  9.7 4.3 %collective-permute-done.6.near1_mine = bf16[1152,256]{1,0:T(8,128)(2,1)S(1)} collective-permute-done((bf16[1152,256]{1,0:T(8,128)(2,1)S(1)}, bf16[1152,256]{1,0:T(8,128)(2,1)S(1)}, u32[]{:S(2)}, u32[]{:S(2)}) %collective-permute-start.6) | collective-permute-done | bytes 589856 | tf_op jit(solution)/shard_map/ppermute | solution.py:280
  14.0 5.0 %collective-permute-start.10 = (bf16[1152,256]{1,0:T(8,128)(2,1)S(1)}, bf16[1152,256]{1,0:T(8,128)(2,1)S(1)}, u32[]{:S(2)}, u32[]{:S(2)}) collective-permute-start(bf16[1152,256]{1,0:T(8,128)(2,1)S(1)} %collective-permute-done.6.near1_mine), channel_id=1, source_target_pairs={{0,16},{1,49},{16,32},{17,1},{32,48},{33,17},{48,0},{49,33},{2,18}... | collective-permute-start | bytes 1769480 | tf_op jit(solution)/shard_map/ppermute | solution.py:282
  19.3 6.6 %collective-permute-start.7 = (bf16[1152,256]{1,0:T(8,128)(2,1)S(1)}, bf16[1152,256]{1,0:T(8,128)(2,1)S(1)}, u32[]{:S(2)}, u32[]{:S(2)}) collective-permute-start(bf16[1152,256]{1,0:T(8,128)(2,1)S(1)} %collective-permute-done.6.near1_mine), channel_id=1, source_target_pairs={{0,1},{1,0},{2,3},{3,2},{4,5},{5,4},{6,7},{7,6},{8,9},{9,8},{10,11... | collective-permute-start | bytes 1769480 | tf_op jit(solution)/shard_map/ppermute | solution.py:285
  25.9 4.1 %collective-permute-start.9 = (bf16[1152,256]{1,0:T(8,128)(2,1)S(1)}, bf16[1152,256]{1,0:T(8,128)(2,1)S(1)}, u32[]{:S(2)}, u32[]{:S(2)}) collective-permute-start(bf16[1152,256]{1,0:T(8,128)(2,1)S(1)} %collective-permute-done.8.near2_mine), channel_id=1, source_target_pairs={{0,1},{1,0},{2,3},{3,2},{4,5},{5,4},{6,7},{7,6},{8,9},{9,8},{10,11... | collective-permute-start | bytes 1769480 | tf_op jit(solution)/shard_map/ppermute | solution.py:285
  30.1 6.6 %collective-permute-start.11 = (bf16[1152,256]{1,0:T(8,128)(2,1)S(1)}, bf16[1152,256]{1,0:T(8,128)(2,1)S(1)}, u32[]{:S(2)}, u32[]{:S(2)}) collective-permute-start(bf16[1152,256]{1,0:T(8,128)(2,1)S(1)} %collective-permute-done.10.far_mine), channel_id=1, source_target_pairs={{0,1},{1,0},{2,3},{3,2},{4,5},{5,4},{6,7},{7,6},{8,9},{9,8},{10,11... | collective-permute-start | bytes 1769480 | tf_op jit(solution)/shard_map/ppermute | solution.py:285
  36.8 1.9 %collective-permute-start = (bf16[64,384]{1,0:T(8,128)(2,1)S(1)}, bf16[64,384]{1,0:T(8,128)(2,1)S(1)}, u32[]{:S(2)}, u32[]{:S(2)}) collective-permute-start(bf16[64,384]{1,0:T(8,128)(2,1)S(1)} %get-tuple-element.25), channel_id=1, source_target_pairs={{0,3},{1,4},{2,5},{3,6},{4,7},{5,8},{6,9},{7,10},{8,11},{9,12},{10... | collective-permute-start | bytes 147464 | tf_op jit(solution)/shard_map/ppermute | solution.py:299
  38.7 4.9 %collective-permute-start.5 = (bf16[64,384]{1,0:T(8,128)(2,1)S(1)}, bf16[64,384]{1,0:T(8,128)(2,1)S(1)}, u32[]{:S(2)}, u32[]{:S(2)}) collective-permute-start(bf16[64,384]{1,0:T(8,128)(2,1)S(1)} %get-tuple-element.24), channel_id=1, source_target_pairs={{0,13},{1,14},{2,15},{3,0},{4,1},{5,2},{6,3},{7,4},{8,5},{9,6},{10... | collective-permute-start | bytes 147464 | tf_op jit(solution)/shard_map/ppermute | solution.py:300
  44.4 1.9 %collective-permute-start.1 = (bf16[96,640]{1,0:T(8,128)(2,1)S(1)}, bf16[96,640]{1,0:T(8,128)(2,1)S(1)}, u32[]{:S(2)}, u32[]{:S(2)}) collective-permute-start(bf16[96,640]{1,0:T(8,128)(2,1)S(1)} %pad_maximum_fusion.own), channel_id=1, source_target_pairs={{0,2},{1,3},{2,4},{3,5},{4,6},{5,7},{6,8},{7,9},{8,10},{9,11},{10,... | collective-permute-start | bytes 368648 | tf_op jit(solution)/shard_map/ppermute | solution.py:297
  46.6 4.6 %collective-permute-done.1.m2a = bf16[96,640]{1,0:T(8,128)(2,1)S(1)} collective-permute-done((bf16[96,640]{1,0:T(8,128)(2,1)S(1)}, bf16[96,640]{1,0:T(8,128)(2,1)S(1)}, u32[]{:S(2)}, u32[]{:S(2)}) %collective-permute-start.1) | collective-permute-done | bytes 122912 | tf_op jit(solution)/shard_map/ppermute | solution.py:297
  51.2 3.3 %collective-permute-start.3 = (bf16[96,640]{1,0:T(8,128)(2,1)S(1)}, bf16[96,640]{1,0:T(8,128)(2,1)S(1)}, u32[]{:S(2)}, u32[]{:S(2)}) collective-permute-start(bf16[96,640]{1,0:T(8,128)(2,1)S(1)} %pad_maximum_fusion.own), channel_id=1, source_target_pairs={{0,15},{1,0},{2,1},{3,2},{4,3},{5,4},{6,5},{7,6},{8,7},{9,8},{10,9... | collective-permute-start | bytes 368648 | tf_op jit(solution)/shard_map/ppermute | solution.py:296
  54.5 1.9 %collective-permute-start.4 = (bf16[96,640]{1,0:T(8,128)(2,1)S(1)}, bf16[96,640]{1,0:T(8,128)(2,1)S(1)}, u32[]{:S(2)}, u32[]{:S(2)}) collective-permute-start(bf16[96,640]{1,0:T(8,128)(2,1)S(1)} %pad_maximum_fusion.own), channel_id=1, source_target_pairs={{0,14},{1,15},{2,0},{3,1},{4,2},{5,3},{6,4},{7,5},{8,6},{9,7},{10,... | collective-permute-start | bytes 368648 | tf_op jit(solution)/shard_map/ppermute | solution.py:298
  56.5 4.8 %collective-permute-done.4.m2b = bf16[96,640]{1,0:T(8,128)(2,1)S(1)} collective-permute-done((bf16[96,640]{1,0:T(8,128)(2,1)S(1)}, bf16[96,640]{1,0:T(8,128)(2,1)S(1)}, u32[]{:S(2)}, u32[]{:S(2)}) %collective-permute-start.4) | collective-permute-done | bytes 122912 | tf_op jit(solution)/shard_map/ppermute | solution.py:298
  61.3 5.0 %shard_map.59 = (bf16[672,256]{1,0:T(8,128)(2,1)S(1)}, bf16[672,256]{1,0:T(8,128)(2,1)S(1)}, bf16[9,512,128]{2,1,0:T(8,128)(2,1)S(1)}, bf16[7,512,128]{2,1,0:T(8...) custom-call(s32[2]{0:T(128)S(1)} %pad_add_fusion.ids_ref.core_ref, ...), custom_call_target="tpu_custom_call" | custom-call | flops 1000000000 | bytes 6000000 | tf_op jit(solution)/shard_map/pallas_call | solution.py:230
  67.4 13.9 %shard_map.60 = bf16[4,320,256]{2,1,0:T(8,128)(2,1)S(1)} custom-call(s32[2]{0:T(128)S(1)} %pad_add_fusion.ids_ref.core_ref, bf16[672,256]{1,0:T(8,128)(2,1)S(1)} %get-tuple-element.10.h0, bf16[672,256]{1,0:T(8,128)(2,1)S(1)} %get-tuple-element.11.g_top, bf16[9,512,128]{2,1,0:T(8,128)(2,1)} %copy-done.1, bf16[7,512,128]{2,1,0:T(8,128)(2,1)S(1)} %get-tuple-element.13.st_buf, ...), custom_call_target="tpu_custom_call" | custom-call | flops 5000000000 | bytes 10000000 | tf_op jit(solution)/shard_map/pallas_call | solution.py:248
  81.3 12.4 %all_to_all.15.mine = bf16[4,320,256]{2,1,0:T(8,128)(2,1)S(1)} all-to-all(bf16[4,320,256]{2,1,0:T(8,128)(2,1)S(1)} %shard_map.60), channel_id=1, replica_groups=mesh['dp'=8,'section'=4,'py'=8,'core'=2] {'section'}, dimensions={0} | all-to-all | bytes 1310720 | tf_op jit(solution)/shard_map/all_to_all | solution.py:305
  93.7 3.8 %collective-permute-start.12 = (bf16[4,224,256]{2,1,0:T(8,128)(2,1)S(1)}, bf16[4,224,256]{2,1,0:T(8,128)(2,1)S(1)}, u32[]{:S(2)}, u32[]{:S(2)}) collective-permute-start(bf16[4,224,256]{2,1,0:T(8,128)(2,1)S(1)} %slice.16), channel_id=1, source_target_pairs={{0,1},{1,0},{2,3},{3,2},{4,5},{5,4},{6,7},{7,6},{8,9},{9,8},{10,11... | collective-permute-start | bytes 1376264 | tf_op jit(solution)/shard_map/ppermute | solution.py:306
  98.9 3.3 %shard_map.61 = (bf16[2560,128]{1,0:T(8,128)(2,1)S(1)}, bf16[4,96,256]{2,1,0:T(8,128)(2,1)}) custom-call(s32[2]{0:T(128)S(1)} %pad_add_fusion.ids_ref.core_ref, bf16[4,320,256]{2,1,0:T(8,128)(2,1)S(1)} %all_to_all.15.mine, bf16[4,224,256]{2,1,0:T(8,128)(2,1)S(1)} %collective-permute-done.12.other, bf16[8,192,256]{2,1,0:T(8,128)(2,1)S(1)} %get-tuple-element.15.hot), custom_call_target="tpu_custom_call" | custom-call | flops 1000000000 | bytes 2000000 | tf_op jit(solution)/shard_map/pallas_call | solution.py:309
  102.2 30.4 %all_to_all.16.x_ref = bf16[64,40,128]{2,1,0:T(8,128)(2,1)S(1)} all-to-all(bf16[64,40,128]{2,1,0:T(8,128)(2,1)S(1)} %bitcast.21), channel_id=1, replica_groups=mesh['dp'=8,'section'=4,'py'=8,'core'=2] {'dp','py'}, dimensions={0} | all-to-all | bytes 1310720 | tf_op jit(solution)/shard_map/all_to_all | solution.py:320
  132.7 25.5 %all_to_all.17 = bf16[64,40,128]{2,1,0:T(8,128)(2,1)S(1)} all-to-all(bf16[64,40,128]{2,1,0:T(8,128)(2,1)S(1)} %shard_map.62), channel_id=1, replica_groups=mesh['dp'=8,'section'=4,'py'=8,'core'=2] {'dp','py'}, dimensions={0} | all-to-all | bytes 1310720 | tf_op jit(solution)/shard_map/all_to_all | solution.py:324
  158.2 6.3 %collective-permute-start.13 = (bf16[2560,128]{1,0:T(8,128)(2,1)S(1)}, bf16[2560,128]{1,0:T(8,128)(2,1)S(1)}, u32[]{:S(2)}, u32[]{:S(2)}) collective-permute-start(bf16[2560,128]{1,0:T(8,128)(2,1)S(1)} %bitcast.19), channel_id=1, source_target_pairs={{0,1},{1,0},{2,3},{3,2},{4,5},{5,4},{6,7},{7,6},{8,9},{9,8},{10,11... | collective-permute-start | bytes 1966088 | tf_op jit(solution)/shard_map/ppermute | solution.py:325
  164.6 1.7 %collective-permute-done.13.other = bf16[2560,128]{1,0:T(8,128)(2,1)S(1)} collective-permute-done((bf16[2560,128]{1,0:T(8,128)(2,1)S(1)}, bf16[2560,128]{1,0:T(8,128)(2,1)S(1)}, u32[]{:S(2)}, u32[]{:S(2)}) %collective-permute-start.13) | collective-permute-done | bytes 655392 | tf_op jit(solution)/shard_map/ppermute | solution.py:325
  166.3 1.8 %shard_map.63 = bf16[2304,256]{1,0:T(8,128)(2,1)} custom-call(s32[2]{0:T(128)S(1)} %pad_add_fusion.ids_ref.core_ref, bf16[2560,128]{1,0:T(8,128)(2,1)S(1)} %bitcast.20, bf16[2560,128]{1,0:T(8,128)(2,1)S(1)} %collective-permute-done.13.other), custom_call_target="tpu_custom_call" | custom-call | bytes 2000000 | tf_op jit(solution)/shard_map/pallas_call | solution.py:326
  (30 shorter events, 5.3 us)
Async XLA Ops:
  0.6 18.6 %copy-start = (bf16[4,1,96,256]{3,2,1,0:T(8,128)(2,1)S(1)}, bf16[4,1,96,256]{3,2,1,0:T(8,128)(2,1)}, u32[]{:S(2)}) copy-start(bf16[4,1,96,256]{3,2,1,0:T(8,128)(2,1)} %param.4) | copy-start | bytes 589828
  0.7 18.4 %copy-start.2 = (s32[9,96]{1,0:T(8,128)S(1)}, s32[9,96]{1,0:T(8,128)}, u32[]{:S(2)}) copy-start(s32[9,96]{1,0:T(8,128)} %param.7) | copy-start | bytes 10372
  2.0 12.0 %collective-permute-start.6 = (bf16[1152,256]{1,0:T(8,128)(2,1)S(1)}, bf16[1152,256]{1,0:T(8,128)(2,1)S(1)}, u32[]{:S(2)}, u32[]{:S(2)}) collective-permute-start(bf16[1152,256]{1,0:T(8,128)(2,1)S(1)} %get-tuple-element.23), channel_id=1, source_target_pairs={{0,16},{1,49},{16,32},{17,1},{32,48},{33,17},{48,0},{49,33},{2,18}... | collective-permute-start | bytes 1769480 | tf_op jit(solution)/shard_map/ppermute | solution.py:280
  7.2 18.7 %collective-permute-start.8 = (bf16[1152,256]{1,0:T(8,128)(2,1)S(1)}, bf16[1152,256]{1,0:T(8,128)(2,1)S(1)}, u32[]{:S(2)}, u32[]{:S(2)}) collective-permute-start(bf16[1152,256]{1,0:T(8,128)(2,1)S(1)} %get-tuple-element.22), channel_id=1, source_target_pairs={{0,16},{1,49},{16,32},{17,1},{32,48},{33,17},{48,0},{49,33},{2,18}... | collective-permute-start | bytes 1769480 | tf_op jit(solution)/shard_map/ppermute | solution.py:281
  14.0 16.0 %collective-permute-start.10 = (bf16[1152,256]{1,0:T(8,128)(2,1)S(1)}, bf16[1152,256]{1,0:T(8,128)(2,1)S(1)}, u32[]{:S(2)}, u32[]{:S(2)}) collective-permute-start(bf16[1152,256]{1,0:T(8,128)(2,1)S(1)} %collective-permute-done.6.near1_mine), channel_id=1, source_target_pairs={{0,16},{1,49},{16,32},{17,1},{32,48},{33,17},{48,0},{49,33},{2,18}... | collective-permute-start | bytes 1769480 | tf_op jit(solution)/shard_map/ppermute | solution.py:282
  19.3 48.0 %collective-permute-start.7 = (bf16[1152,256]{1,0:T(8,128)(2,1)S(1)}, bf16[1152,256]{1,0:T(8,128)(2,1)S(1)}, u32[]{:S(2)}, u32[]{:S(2)}) collective-permute-start(bf16[1152,256]{1,0:T(8,128)(2,1)S(1)} %collective-permute-done.6.near1_mine), channel_id=1, source_target_pairs={{0,1},{1,0},{2,3},{3,2},{4,5},{5,4},{6,7},{7,6},{8,9},{9,8},{10,11... | collective-permute-start | bytes 1769480 | tf_op jit(solution)/shard_map/ppermute | solution.py:285
  25.9 41.4 %collective-permute-start.9 = (bf16[1152,256]{1,0:T(8,128)(2,1)S(1)}, bf16[1152,256]{1,0:T(8,128)(2,1)S(1)}, u32[]{:S(2)}, u32[]{:S(2)}) collective-permute-start(bf16[1152,256]{1,0:T(8,128)(2,1)S(1)} %collective-permute-done.8.near2_mine), channel_id=1, source_target_pairs={{0,1},{1,0},{2,3},{3,2},{4,5},{5,4},{6,7},{7,6},{8,9},{9,8},{10,11... | collective-permute-start | bytes 1769480 | tf_op jit(solution)/shard_map/ppermute | solution.py:285
  30.1 37.3 %collective-permute-start.11 = (bf16[1152,256]{1,0:T(8,128)(2,1)S(1)}, bf16[1152,256]{1,0:T(8,128)(2,1)S(1)}, u32[]{:S(2)}, u32[]{:S(2)}) collective-permute-start(bf16[1152,256]{1,0:T(8,128)(2,1)S(1)} %collective-permute-done.10.far_mine), channel_id=1, source_target_pairs={{0,1},{1,0},{2,3},{3,2},{4,5},{5,4},{6,7},{7,6},{8,9},{9,8},{10,11... | collective-permute-start | bytes 1769480 | tf_op jit(solution)/shard_map/ppermute | solution.py:285
  36.8 7.6 %collective-permute-start = (bf16[64,384]{1,0:T(8,128)(2,1)S(1)}, bf16[64,384]{1,0:T(8,128)(2,1)S(1)}, u32[]{:S(2)}, u32[]{:S(2)}) collective-permute-start(bf16[64,384]{1,0:T(8,128)(2,1)S(1)} %get-tuple-element.25), channel_id=1, source_target_pairs={{0,3},{1,4},{2,5},{3,6},{4,7},{5,8},{6,9},{7,10},{8,11},{9,12},{10... | collective-permute-start | bytes 147464 | tf_op jit(solution)/shard_map/ppermute | solution.py:299
  38.7 7.6 %collective-permute-start.5 = (bf16[64,384]{1,0:T(8,128)(2,1)S(1)}, bf16[64,384]{1,0:T(8,128)(2,1)S(1)}, u32[]{:S(2)}, u32[]{:S(2)}) collective-permute-start(bf16[64,384]{1,0:T(8,128)(2,1)S(1)} %get-tuple-element.24), channel_id=1, source_target_pairs={{0,13},{1,14},{2,15},{3,0},{4,1},{5,2},{6,3},{7,4},{8,5},{9,6},{10... | collective-permute-start | bytes 147464 | tf_op jit(solution)/shard_map/ppermute | solution.py:300
  44.4 6.8 %collective-permute-start.1 = (bf16[96,640]{1,0:T(8,128)(2,1)S(1)}, bf16[96,640]{1,0:T(8,128)(2,1)S(1)}, u32[]{:S(2)}, u32[]{:S(2)}) collective-permute-start(bf16[96,640]{1,0:T(8,128)(2,1)S(1)} %pad_maximum_fusion.own), channel_id=1, source_target_pairs={{0,2},{1,3},{2,4},{3,5},{4,6},{5,7},{6,8},{7,9},{8,10},{9,11},{10,... | collective-permute-start | bytes 368648 | tf_op jit(solution)/shard_map/ppermute | solution.py:297
  46.3 8.2 %collective-permute-start.2 = (bf16[96,640]{1,0:T(8,128)(2,1)S(1)}, bf16[96,640]{1,0:T(8,128)(2,1)S(1)}, u32[]{:S(2)}, u32[]{:S(2)}) collective-permute-start(bf16[96,640]{1,0:T(8,128)(2,1)S(1)} %pad_maximum_fusion.own), channel_id=1, source_target_pairs={{0,1},{1,2},{2,3},{3,4},{4,5},{5,6},{6,7},{7,8},{8,9},{9,10},{10,1... | collective-permute-start | bytes 368648 | tf_op jit(solution)/shard_map/ppermute | solution.py:295
  51.2 5.3 %collective-permute-start.3 = (bf16[96,640]{1,0:T(8,128)(2,1)S(1)}, bf16[96,640]{1,0:T(8,128)(2,1)S(1)}, u32[]{:S(2)}, u32[]{:S(2)}) collective-permute-start(bf16[96,640]{1,0:T(8,128)(2,1)S(1)} %pad_maximum_fusion.own), channel_id=1, source_target_pairs={{0,15},{1,0},{2,1},{3,2},{4,3},{5,4},{6,5},{7,6},{8,7},{9,8},{10,9... | collective-permute-start | bytes 368648 | tf_op jit(solution)/shard_map/ppermute | solution.py:296
  54.5 6.8 %collective-permute-start.4 = (bf16[96,640]{1,0:T(8,128)(2,1)S(1)}, bf16[96,640]{1,0:T(8,128)(2,1)S(1)}, u32[]{:S(2)}, u32[]{:S(2)}) collective-permute-start(bf16[96,640]{1,0:T(8,128)(2,1)S(1)} %pad_maximum_fusion.own), channel_id=1, source_target_pairs={{0,14},{1,15},{2,0},{3,1},{4,2},{5,3},{6,4},{7,5},{8,6},{9,7},{10,... | collective-permute-start | bytes 368648 | tf_op jit(solution)/shard_map/ppermute | solution.py:298
  66.3 1.0 copy-start.1
  93.7 5.2 %collective-permute-start.12 = (bf16[4,224,256]{2,1,0:T(8,128)(2,1)S(1)}, bf16[4,224,256]{2,1,0:T(8,128)(2,1)S(1)}, u32[]{:S(2)}, u32[]{:S(2)}) collective-permute-start(bf16[4,224,256]{2,1,0:T(8,128)(2,1)S(1)} %slice.16), channel_id=1, source_target_pairs={{0,1},{1,0},{2,3},{3,2},{4,5},{5,4},{6,7},{7,6},{8,9},{9,8},{10,11... | collective-permute-start | bytes 1376264 | tf_op jit(solution)/shard_map/ppermute | solution.py:306
  158.2 8.1 %collective-permute-start.13 = (bf16[2560,128]{1,0:T(8,128)(2,1)S(1)}, bf16[2560,128]{1,0:T(8,128)(2,1)S(1)}, u32[]{:S(2)}, u32[]{:S(2)}) collective-permute-start(bf16[2560,128]{1,0:T(8,128)(2,1)S(1)} %bitcast.19), channel_id=1, source_target_pairs={{0,1},{1,0},{2,3},{3,2},{4,5},{5,4},{6,7},{7,6},{8,9},{9,8},{10,11... | collective-permute-start | bytes 1966088 | tf_op jit(solution)/shard_map/ppermute | solution.py:325

commit v5 on v4

--- a/solution.py
+++ b/solution.py
@@ -102,22 +102,18 @@
         pair_ref[k - 1] = jnp.where(apart == offt[k:k + 1, :], 1.0, 0.0).astype(BF)
 
 
-def stack_kernel(ids_ref, h0, g_top, s_buf, st_buf, gat0, w_own, near1_mine, near1_other, near2_mine, near2_other,
-                 far_mine, far_other, out_ref, w_buf, h_buf, gat, der, pre_buf, g_buf, sems):
+def stack_kernel(ids_ref, h0, g_top, s_buf, st_buf, gat0, w_own, near_mine, near_other, far_mine, far_other,
+                 out_ref, w_buf, h_buf, gat, der, pre_buf, g_buf, sems):
     core, section = ids_ref[0], ids_ref[1]
     left, right = lax.rem(section + 3, LEVELS), lax.rem(section + 1, LEVELS)
-    mine = w_buf.at[jnp.where(core == 0, left, right)]
-    other = w_buf.at[jnp.where(core == 0, right, left)]
     far = w_buf.at[lax.rem(section + 2, LEVELS)]
     here = pl.ds(pl.multiple_of(core * HALF, HALF), HALF)
     there = pl.ds(pl.multiple_of((1 - core) * HALF, HALF), HALF)
     copies = []
     for n, (src, dst) in enumerate((
         (w_own, w_buf.at[section]),
-        (near1_mine, mine.at[here, :]),
-        (near1_other, other.at[there, :]),
-        (near2_mine, mine.at[there, :]),
-        (near2_other, other.at[here, :]),
+        (near_mine, w_buf.at[jnp.where(core == 0, left, right)]),
+        (near_other, w_buf.at[jnp.where(core == 0, right, left)]),
         (far_mine, far.at[here, :]),
         (far_other, far.at[there, :]),
     )):
@@ -221,7 +217,7 @@
         scratch_shapes=list(scratch),
         interpret=INTERPRET,
         cost_estimate=pl.CostEstimate(flops=flops, bytes_accessed=nbytes, transcendentals=0),
-        compiler_params=pltpu.CompilerParams(vmem_limit_bytes=48 << 20),
+        compiler_params=pltpu.CompilerParams(vmem_limit_bytes=28 << 20),
     )
 
 
@@ -248,7 +244,7 @@
     return call(
         stack_kernel,
         jax.ShapeDtypeStruct((LEVELS, MSG, C), BF),
-        [SMEM] + [VMEM] * 5 + [ANY] * 7,
+        [SMEM] + [VMEM] * 5 + [ANY] * 5,
         [
             pltpu.VMEM((LEVELS, TAPS * C, C), BF),
             pltpu.VMEM((LEVELS - 1, ROWS, C), BF),
@@ -256,7 +252,7 @@
             pltpu.VMEM((LEVELS, tiles * TILE, C), F32),
             pltpu.VMEM((ROWS, C), BF),
             pltpu.VMEM((ROWS, C), BF),
-            pltpu.SemaphoreType.DMA((7,)),
+            pltpu.SemaphoreType.DMA((5,)),
         ],
         flops=5 * 10**9, nbytes=10 * 10**6,
     )(*operands)
@@ -277,11 +273,11 @@
 
     sections = lax.axis_size("section")
     ways = [(2 * i + c, 2 * ((i + (1, -1)[c]) % sections) + c) for i in range(sections) for c in range(2)]
-    near1 = lax.ppermute(lax.dynamic_slice_in_dim(weights[0], core * HALF, HALF), ("section", "core"), ways)
-    near2 = lax.ppermute(lax.dynamic_slice_in_dim(weights[0], (1 - core) * HALF, HALF), ("section", "core"), ways)
-    far = lax.ppermute(near1, ("section", "core"), ways)
+    near = lax.ppermute(weights[0], ("section", "core"), ways)
+    half = lax.dynamic_slice_in_dim(near, core * HALF, HALF)
+    far = lax.ppermute(half, ("section", "core"), ways)
     parts = []
-    for block in (near1, near2, far):
+    for block in (near, far):
         parts += [block, lax.ppermute(block, "core", shift(2, 1))]
 
     place = patch * PIX + jnp.arange(PIX, dtype=jnp.int32)

time: 169 us -> 167 us (0.988)
  Pallas kernels: 24.1 us -> 21 us
  waiting for transfers between devices: 16.9 us -> 19.6 us
    ppermute x3 -> x2, waiting for transfers between devices: 4.34 us -> 13.7 us  [the longest x1 13.4 us: step(): near = lax.ppermute(weights[0], ('section', 'core'), ways)]
    ppermute x1, waiting for transfers between devices: 4.63 us -> 0.01 us  [step(): m2a = send(own, perm=shift(patches, 2))]
    ppermute x1, waiting for transfers between devices: 4.76 us -> 1.76 us  [step(): m2b = send(own, perm=shift(patches, -2))]
    ppermute x1, starting transfers between devices: 3.76 us -> 6.46 us  [step(): other = lax.ppermute(mine[:, :HROWS + PROWS], 'core', shift(2, 1))]
    ppermute x1, starting transfers between devices: 3.32 us -> 0.78 us  [step(): m1b = send(own, perm=shift(patches, -1))]
    ppermute x3 -> x2, starting transfers between devices: 12.7 us -> 10.2 us  [the longest x1 5.34 us: step(): near = lax.ppermute(weights[0], ('section', 'core'), ways)]
    ppermute x1, starting transfers between devices: 1.91 us -> 4.27 us  [step(): m2b = send(own, perm=shift(patches, -2))]
    all_to_all x1, blocking collectives: 12.4 us -> 10 us  [step(): mine = lax.all_to_all(out, 'section', 0, 0, tiled=True)]
  transfers between devices with their start and end apart: 14 -> 12, of which waited for: 5 -> 6; matrix products, arithmetic and copies ran while one was open for 1% -> 1% of each run, Pallas kernels for 3% -> 2%
where the time goes in v5:
time: 167 us; the launch traced here: 166 us
  blocking collectives  67.4 us (40%)
  starting transfers between devices  55.4 us (33%)
  Pallas kernels  21 us (13%)
  waiting for transfers between devices  19.6 us (12%)
  local copies, waits for them, and re-layouts  1.83 us (1%)
    all_to_all x1, blocking collectives, step(): lax.all_to_all(part.reshape((chips, rows // chips, 128)), ('dp', 'py'), 0...  31.8 us
    all_to_all x1, blocking collectives, step(): lax.all_to_all(total, ('dp', 'py'), 0, 0, tiled=True).reshape((rows, 128))  25.5 us
    ppermute x2, starting transfers between devices, step(): parts += [block, lax.ppermute(block, 'core', shift(2, 1))]  17.4 us
    ppermute x1, waiting for transfers between devices, step(): near = lax.ppermute(weights[0], ('section', 'core'), ways)  13.4 us
    pallas_call x1, Pallas kernels, stack_call(): call(stack_kernel, jax.ShapeDtypeStruct((LEVELS, MSG, C), BF), [SMEM] + [...  12.1 us
    all_to_all x1, blocking collectives, step(): mine = lax.all_to_all(out, 'section', 0, 0, tiled=True)  10 us
    ppermute x1, starting transfers between devices, step(): other = lax.ppermute(mine[:, :HROWS + PROWS], 'core', shift(2, 1))  6.46 us
    ppermute x1, starting transfers between devices, step(): swapped = lax.ppermute(full, 'core', shift(2, 1))  6.34 us
  transfers between devices with their start and end apart: 12, of which 6 were waited for; matrix products, arithmetic and copies ran while one was open for 1% of the time, Pallas kernels for 2%

profile of v5, /device:TPU:1, one launch (start us, length us, event | category | flops | bytes accessed | tf_op | source)
XLA Modules:
  0.0 166.2 jit_solution(3039349240921161882)
XLA Ops:
  0.7 5.3 %collective-permute-start.6 = (bf16[2304,256]{1,0:T(8,128)(2,1)}, bf16[2304,256]{1,0:T(8,128)(2,1)S(1)}, u32[]{:S(2)}, u32[]{:S(2)}) collective-permute-start(bf16[2304,256]{1,0:T(8,128)(2,1)} %bitcast.18), channel_id=1, source_target_pairs={{0,16},{1,49},{16,32},{17,1},{32,48},{33,17},{48,0},{49,33},{2,18}... | collective-permute-start | bytes 3538952 | tf_op jit(solution)/shard_map/ppermute | solution.py:276
  6.0 13.4 %collective-permute-done.6.near_mine = bf16[2304,256]{1,0:T(8,128)(2,1)S(1)} collective-permute-done((bf16[2304,256]{1,0:T(8,128)(2,1)}, bf16[2304,256]{1,0:T(8,128)(2,1)S(1)}, u32[]{:S(2)}, u32[]{:S(2)}) %collective-permute-start.6) | collective-permute-done | bytes 1179680 | tf_op jit(solution)/shard_map/ppermute | solution.py:276
  19.4 0.9 constant_dynamic-slice_fusion
  20.3 4.9 %collective-permute-start.8 = (bf16[1152,256]{1,0:T(8,128)(2,1)}, bf16[1152,256]{1,0:T(8,128)(2,1)S(1)}, u32[]{:S(2)}, u32[]{:S(2)}) collective-permute-start(bf16[1152,256]{1,0:T(8,128)(2,1)} %constant_dynamic-slice_fusion), channel_id=1, source_target_pairs={{0,16},{1,49},{16,32},{17,1},{32,48},{33,17},{48,0},{49,33},{2,18}... | collective-permute-start | bytes 1769480 | tf_op jit(solution)/shard_map/ppermute | solution.py:278
  25.2 6.6 %collective-permute-start.7 = (bf16[2304,256]{1,0:T(8,128)(2,1)S(1)}, bf16[2304,256]{1,0:T(8,128)(2,1)S(1)}, u32[]{:S(2)}, u32[]{:S(2)}) collective-permute-start(bf16[2304,256]{1,0:T(8,128)(2,1)S(1)} %collective-permute-done.6.near_mine), channel_id=1, source_target_pairs={{0,1},{1,0},{2,3},{3,2},{4,5},{5,4},{6,7},{7,6},{8,9},{9,8},{10,11... | collective-permute-start | bytes 3538952 | tf_op jit(solution)/shard_map/ppermute | solution.py:281
  32.3 10.7 %collective-permute-start.9 = (bf16[1152,256]{1,0:T(8,128)(2,1)S(1)}, bf16[1152,256]{1,0:T(8,128)(2,1)S(1)}, u32[]{:S(2)}, u32[]{:S(2)}) collective-permute-start(bf16[1152,256]{1,0:T(8,128)(2,1)S(1)} %collective-permute-done.8.far_mine), channel_id=1, source_target_pairs={{0,1},{1,0},{2,3},{3,2},{4,5},{5,4},{6,7},{7,6},{8,9},{9,8},{10,11... | collective-permute-start | bytes 1769480 | tf_op jit(solution)/shard_map/ppermute | solution.py:281
  43.9 1.9 %collective-permute-start.1 = (bf16[96,640]{1,0:T(8,128)(2,1)S(1)}, bf16[96,640]{1,0:T(8,128)(2,1)S(1)}, u32[]{:S(2)}, u32[]{:S(2)}) collective-permute-start(bf16[96,640]{1,0:T(8,128)(2,1)S(1)} %pad_maximum_fusion.own), channel_id=1, source_target_pairs={{0,2},{1,3},{2,4},{3,5},{4,6},{5,7},{6,8},{7,9},{8,10},{9,11},{10,... | collective-permute-start | bytes 368648 | tf_op jit(solution)/shard_map/ppermute | solution.py:293
  45.9 1.9 %collective-permute-start = (bf16[64,384]{1,0:T(8,128)(2,1)S(1)}, bf16[64,384]{1,0:T(8,128)(2,1)S(1)}, u32[]{:S(2)}, u32[]{:S(2)}) collective-permute-start(bf16[64,384]{1,0:T(8,128)(2,1)S(1)} %get-tuple-element.23), channel_id=1, source_target_pairs={{0,3},{1,4},{2,5},{3,6},{4,7},{5,8},{6,9},{7,10},{8,11},{9,12},{10... | collective-permute-start | bytes 147464 | tf_op jit(solution)/shard_map/ppermute | solution.py:295
  47.8 4.9 %collective-permute-start.5 = (bf16[64,384]{1,0:T(8,128)(2,1)S(1)}, bf16[64,384]{1,0:T(8,128)(2,1)S(1)}, u32[]{:S(2)}, u32[]{:S(2)}) collective-permute-start(bf16[64,384]{1,0:T(8,128)(2,1)S(1)} %get-tuple-element.22), channel_id=1, source_target_pairs={{0,13},{1,14},{2,15},{3,0},{4,1},{5,2},{6,3},{7,4},{8,5},{9,6},{10... | collective-permute-start | bytes 147464 | tf_op jit(solution)/shard_map/ppermute | solution.py:296
  52.7 1.0 collective-permute-done.m3a
  53.6 1.3 collective-permute-start.2
  55.7 4.3 %collective-permute-start.4 = (bf16[96,640]{1,0:T(8,128)(2,1)S(1)}, bf16[96,640]{1,0:T(8,128)(2,1)S(1)}, u32[]{:S(2)}, u32[]{:S(2)}) collective-permute-start(bf16[96,640]{1,0:T(8,128)(2,1)S(1)} %pad_maximum_fusion.own), channel_id=1, source_target_pairs={{0,14},{1,15},{2,0},{3,1},{4,2},{5,3},{6,4},{7,5},{8,6},{9,7},{10,... | collective-permute-start | bytes 368648 | tf_op jit(solution)/shard_map/ppermute | solution.py:294
  60.1 1.8 %collective-permute-done.4.m2b = bf16[96,640]{1,0:T(8,128)(2,1)S(1)} collective-permute-done((bf16[96,640]{1,0:T(8,128)(2,1)S(1)}, bf16[96,640]{1,0:T(8,128)(2,1)S(1)}, u32[]{:S(2)}, u32[]{:S(2)}) %collective-permute-start.4) | collective-permute-done | bytes 122912 | tf_op jit(solution)/shard_map/ppermute | solution.py:294
  61.8 3.7 %shard_map.59 = (bf16[672,256]{1,0:T(8,128)(2,1)S(1)}, bf16[672,256]{1,0:T(8,128)(2,1)S(1)}, bf16[9,512,128]{2,1,0:T(8,128)(2,1)S(1)}, bf16[7,512,128]{2,1,0:T(8...) custom-call(s32[2]{0:T(128)S(1)} %pad_add_fusion.ids_ref.core_ref, ...), custom_call_target="tpu_custom_call" | custom-call | flops 1000000000 | bytes 6000000 | tf_op jit(solution)/shard_map/pallas_call | solution.py:226
  65.6 12.1 %shard_map.60 = bf16[4,320,256]{2,1,0:T(8,128)(2,1)S(1)} custom-call(s32[2]{0:T(128)S(1)} %pad_add_fusion.ids_ref.core_ref, bf16[672,256]{1,0:T(8,128)(2,1)S(1)} %get-tuple-element.10.h0, bf16[672,256]{1,0:T(8,128)(2,1)S(1)} %get-tuple-element.11.g_top, bf16[9,512,128]{2,1,0:T(8,128)(2,1)S(1)} %get-tuple-element.12.s_buf, ...), custom_call_target="tpu_custom_call" | custom-call | flops 5000000000 | bytes 10000000 | tf_op jit(solution)/shard_map/pallas_call | solution.py:244
  77.7 10.0 %all_to_all.15.mine = bf16[4,320,256]{2,1,0:T(8,128)(2,1)S(1)} all-to-all(bf16[4,320,256]{2,1,0:T(8,128)(2,1)S(1)} %shard_map.60), channel_id=1, replica_groups=mesh['dp'=8,'section'=4,'py'=8,'core'=2] {'section'}, dimensions={0} | all-to-all | bytes 1310720 | tf_op jit(solution)/shard_map/all_to_all | solution.py:301
  87.8 6.5 %collective-permute-start.10 = (bf16[4,224,256]{2,1,0:T(8,128)(2,1)S(1)}, bf16[4,224,256]{2,1,0:T(8,128)(2,1)S(1)}, u32[]{:S(2)}, u32[]{:S(2)}) collective-permute-start(bf16[4,224,256]{2,1,0:T(8,128)(2,1)S(1)} %slice.16), channel_id=1, source_target_pairs={{0,1},{1,0},{2,3},{3,2},{4,5},{5,4},{6,7},{7,6},{8,9},{9,8},{10,11... | collective-permute-start | bytes 1376264 | tf_op jit(solution)/shard_map/ppermute | solution.py:302
  94.3 1.4 collective-permute-done.10.other
  95.7 3.3 %shard_map.61 = (bf16[2560,128]{1,0:T(8,128)(2,1)S(1)}, bf16[4,96,256]{2,1,0:T(8,128)(2,1)}) custom-call(s32[2]{0:T(128)S(1)} %pad_add_fusion.ids_ref.core_ref, bf16[4,320,256]{2,1,0:T(8,128)(2,1)S(1)} %all_to_all.15.mine, bf16[4,224,256]{2,1,0:T(8,128)(2,1)S(1)} %collective-permute-done.10.other, bf16[8,192,256]{2,1,0:T(8,128)(2,1)S(1)} %get-tuple-element.15.hot), custom_call_target="tpu_custom_call" | custom-call | flops 1000000000 | bytes 2000000 | tf_op jit(solution)/shard_map/pallas_call | solution.py:305
  99.0 31.8 %all_to_all.16.x_ref = bf16[64,40,128]{2,1,0:T(8,128)(2,1)S(1)} all-to-all(bf16[64,40,128]{2,1,0:T(8,128)(2,1)S(1)} %bitcast.17), channel_id=1, replica_groups=mesh['dp'=8,'section'=4,'py'=8,'core'=2] {'dp','py'}, dimensions={0} | all-to-all | bytes 1310720 | tf_op jit(solution)/shard_map/all_to_all | solution.py:316
  130.9 25.5 %all_to_all.17 = bf16[64,40,128]{2,1,0:T(8,128)(2,1)S(1)} all-to-all(bf16[64,40,128]{2,1,0:T(8,128)(2,1)S(1)} %shard_map.62), channel_id=1, replica_groups=mesh['dp'=8,'section'=4,'py'=8,'core'=2] {'dp','py'}, dimensions={0} | all-to-all | bytes 1310720 | tf_op jit(solution)/shard_map/all_to_all | solution.py:320
  156.4 6.3 %collective-permute-start.11 = (bf16[2560,128]{1,0:T(8,128)(2,1)S(1)}, bf16[2560,128]{1,0:T(8,128)(2,1)S(1)}, u32[]{:S(2)}, u32[]{:S(2)}) collective-permute-start(bf16[2560,128]{1,0:T(8,128)(2,1)S(1)} %bitcast.15), channel_id=1, source_target_pairs={{0,1},{1,0},{2,3},{3,2},{4,5},{5,4},{6,7},{7,6},{8,9},{9,8},{10,11... | collective-permute-start | bytes 1966088 | tf_op jit(solution)/shard_map/ppermute | solution.py:321
  162.8 1.7 %collective-permute-done.11.other = bf16[2560,128]{1,0:T(8,128)(2,1)S(1)} collective-permute-done((bf16[2560,128]{1,0:T(8,128)(2,1)S(1)}, bf16[2560,128]{1,0:T(8,128)(2,1)S(1)}, u32[]{:S(2)}, u32[]{:S(2)}) %collective-permute-start.11) | collective-permute-done | bytes 655392 | tf_op jit(solution)/shard_map/ppermute | solution.py:321
  164.5 1.8 %shard_map.63 = bf16[2304,256]{1,0:T(8,128)(2,1)} custom-call(s32[2]{0:T(128)S(1)} %pad_add_fusion.ids_ref.core_ref, bf16[2560,128]{1,0:T(8,128)(2,1)S(1)} %bitcast.16, bf16[2560,128]{1,0:T(8,128)(2,1)S(1)} %collective-permute-done.11.other), custom_call_target="tpu_custom_call" | custom-call | bytes 2000000 | tf_op jit(solution)/shard_map/pallas_call | solution.py:322
  (26 shorter events, 2.3 us)
Async XLA Ops:
  0.6 31.4 %copy-start = (bf16[4,1,96,256]{3,2,1,0:T(8,128)(2,1)S(1)}, bf16[4,1,96,256]{3,2,1,0:T(8,128)(2,1)}, u32[]{:S(2)}) copy-start(bf16[4,1,96,256]{3,2,1,0:T(8,128)(2,1)} %param.4) | copy-start | bytes 589828
  0.6 31.2 %copy-start.2 = (s32[9,96]{1,0:T(8,128)S(1)}, s32[9,96]{1,0:T(8,128)}, u32[]{:S(2)}) copy-start(s32[9,96]{1,0:T(8,128)} %param.7) | copy-start | bytes 10372
  0.7 18.8 %collective-permute-start.6 = (bf16[2304,256]{1,0:T(8,128)(2,1)}, bf16[2304,256]{1,0:T(8,128)(2,1)S(1)}, u32[]{:S(2)}, u32[]{:S(2)}) collective-permute-start(bf16[2304,256]{1,0:T(8,128)(2,1)} %bitcast.18), channel_id=1, source_target_pairs={{0,16},{1,49},{16,32},{17,1},{32,48},{33,17},{48,0},{49,33},{2,18}... | collective-permute-start | bytes 3538952 | tf_op jit(solution)/shard_map/ppermute | solution.py:276
  20.3 12.0 %collective-permute-start.8 = (bf16[1152,256]{1,0:T(8,128)(2,1)}, bf16[1152,256]{1,0:T(8,128)(2,1)S(1)}, u32[]{:S(2)}, u32[]{:S(2)}) collective-permute-start(bf16[1152,256]{1,0:T(8,128)(2,1)} %constant_dynamic-slice_fusion), channel_id=1, source_target_pairs={{0,16},{1,49},{16,32},{17,1},{32,48},{33,17},{48,0},{49,33},{2,18}... | collective-permute-start | bytes 1769480 | tf_op jit(solution)/shard_map/ppermute | solution.py:278
  25.2 40.4 %collective-permute-start.7 = (bf16[2304,256]{1,0:T(8,128)(2,1)S(1)}, bf16[2304,256]{1,0:T(8,128)(2,1)S(1)}, u32[]{:S(2)}, u32[]{:S(2)}) collective-permute-start(bf16[2304,256]{1,0:T(8,128)(2,1)S(1)} %collective-permute-done.6.near_mine), channel_id=1, source_target_pairs={{0,1},{1,0},{2,3},{3,2},{4,5},{5,4},{6,7},{7,6},{8,9},{9,8},{10,11... | collective-permute-start | bytes 3538952 | tf_op jit(solution)/shard_map/ppermute | solution.py:281
  32.3 33.2 %collective-permute-start.9 = (bf16[1152,256]{1,0:T(8,128)(2,1)S(1)}, bf16[1152,256]{1,0:T(8,128)(2,1)S(1)}, u32[]{:S(2)}, u32[]{:S(2)}) collective-permute-start(bf16[1152,256]{1,0:T(8,128)(2,1)S(1)} %collective-permute-done.8.far_mine), channel_id=1, source_target_pairs={{0,1},{1,0},{2,3},{3,2},{4,5},{5,4},{6,7},{7,6},{8,9},{9,8},{10,11... | collective-permute-start | bytes 1769480 | tf_op jit(solution)/shard_map/ppermute | solution.py:281
  43.9 11.8 %collective-permute-start.1 = (bf16[96,640]{1,0:T(8,128)(2,1)S(1)}, bf16[96,640]{1,0:T(8,128)(2,1)S(1)}, u32[]{:S(2)}, u32[]{:S(2)}) collective-permute-start(bf16[96,640]{1,0:T(8,128)(2,1)S(1)} %pad_maximum_fusion.own), channel_id=1, source_target_pairs={{0,2},{1,3},{2,4},{3,5},{4,6},{5,7},{6,8},{7,9},{8,10},{9,11},{10,... | collective-permute-start | bytes 368648 | tf_op jit(solution)/shard_map/ppermute | solution.py:293
  45.9 7.8 %collective-permute-start = (bf16[64,384]{1,0:T(8,128)(2,1)S(1)}, bf16[64,384]{1,0:T(8,128)(2,1)S(1)}, u32[]{:S(2)}, u32[]{:S(2)}) collective-permute-start(bf16[64,384]{1,0:T(8,128)(2,1)S(1)} %get-tuple-element.23), channel_id=1, source_target_pairs={{0,3},{1,4},{2,5},{3,6},{4,7},{5,8},{6,9},{7,10},{8,11},{9,12},{10... | collective-permute-start | bytes 147464 | tf_op jit(solution)/shard_map/ppermute | solution.py:295
  47.8 7.1 %collective-permute-start.5 = (bf16[64,384]{1,0:T(8,128)(2,1)S(1)}, bf16[64,384]{1,0:T(8,128)(2,1)S(1)}, u32[]{:S(2)}, u32[]{:S(2)}) collective-permute-start(bf16[64,384]{1,0:T(8,128)(2,1)S(1)} %get-tuple-element.22), channel_id=1, source_target_pairs={{0,13},{1,14},{2,15},{3,0},{4,1},{5,2},{6,3},{7,4},{8,5},{9,6},{10... | collective-permute-start | bytes 147464 | tf_op jit(solution)/shard_map/ppermute | solution.py:296
  53.6 6.4 %collective-permute-start.2 = (bf16[96,640]{1,0:T(8,128)(2,1)S(1)}, bf16[96,640]{1,0:T(8,128)(2,1)S(1)}, u32[]{:S(2)}, u32[]{:S(2)}) collective-permute-start(bf16[96,640]{1,0:T(8,128)(2,1)S(1)} %pad_maximum_fusion.own), channel_id=1, source_target_pairs={{0,1},{1,2},{2,3},{3,4},{4,5},{5,6},{6,7},{7,8},{8,9},{9,10},{10,1... | collective-permute-start | bytes 368648 | tf_op jit(solution)/shard_map/ppermute | solution.py:291
  54.9 5.1 %collective-permute-start.3 = (bf16[96,640]{1,0:T(8,128)(2,1)S(1)}, bf16[96,640]{1,0:T(8,128)(2,1)S(1)}, u32[]{:S(2)}, u32[]{:S(2)}) collective-permute-start(bf16[96,640]{1,0:T(8,128)(2,1)S(1)} %pad_maximum_fusion.own), channel_id=1, source_target_pairs={{0,15},{1,0},{2,1},{3,2},{4,3},{5,4},{6,5},{7,6},{8,7},{9,8},{10,9... | collective-permute-start | bytes 368648 | tf_op jit(solution)/shard_map/ppermute | solution.py:292
  55.7 6.1 %collective-permute-start.4 = (bf16[96,640]{1,0:T(8,128)(2,1)S(1)}, bf16[96,640]{1,0:T(8,128)(2,1)S(1)}, u32[]{:S(2)}, u32[]{:S(2)}) collective-permute-start(bf16[96,640]{1,0:T(8,128)(2,1)S(1)} %pad_maximum_fusion.own), channel_id=1, source_target_pairs={{0,14},{1,15},{2,0},{3,1},{4,2},{5,3},{6,4},{7,5},{8,6},{9,7},{10,... | collective-permute-start | bytes 368648 | tf_op jit(solution)/shard_map/ppermute | solution.py:294
  60.1 5.5 %copy-start.1 = (bf16[1,2304,256]{2,1,0:T(8,128)(2,1)S(1)}, bf16[1,2304,256]{2,1,0:T(8,128)(2,1)}, u32[]{:S(2)}) copy-start(bf16[1,2304,256]{2,1,0:T(8,128)(2,1)} %param.6) | copy-start | bytes 3538948
  87.8 7.9 %collective-permute-start.10 = (bf16[4,224,256]{2,1,0:T(8,128)(2,1)S(1)}, bf16[4,224,256]{2,1,0:T(8,128)(2,1)S(1)}, u32[]{:S(2)}, u32[]{:S(2)}) collective-permute-start(bf16[4,224,256]{2,1,0:T(8,128)(2,1)S(1)} %slice.16), channel_id=1, source_target_pairs={{0,1},{1,0},{2,3},{3,2},{4,5},{5,4},{6,7},{7,6},{8,9},{9,8},{10,11... | collective-permute-start | bytes 1376264 | tf_op jit(solution)/shard_map/ppermute | solution.py:302
  156.4 8.1 %collective-permute-start.11 = (bf16[2560,128]{1,0:T(8,128)(2,1)S(1)}, bf16[2560,128]{1,0:T(8,128)(2,1)S(1)}, u32[]{:S(2)}, u32[]{:S(2)}) collective-permute-start(bf16[2560,128]{1,0:T(8,128)(2,1)S(1)} %bitcast.15), channel_id=1, source_target_pairs={{0,1},{1,0},{2,3},{3,2},{4,5},{5,4},{6,7},{7,6},{8,9},{9,8},{10,11... | collective-permute-start | bytes 1966088 | tf_op jit(solution)/shard_map/ppermute | solution.py:321

commit v6 on v5

--- a/solution.py
+++ b/solution.py
@@ -27,6 +27,8 @@
 FWD_TILES = ((0, 9), (1, 9), (1, 8), (2, 8))
 PRE_ROWS = ((224, 384), (192, 416), (160, 448), (128, 480))
 BWD_TILES = ((4, 6), (3, 6), (3, 7), (2, 7))
+EDGE = 2 * HALO
+OFF = 16
 OWN = REACH
 HROWS, PROWS, GROWS = PIX, PIX + HALO, PIX
 MSG = HROWS + PROWS + GROWS
@@ -56,20 +58,69 @@
         one(t)
 
 
-def prep_kernel(ids_ref, m3a, m2a, m1a, own, m1b, m2b, m3b, h_ref, g_ref, s_ref, st_ref, gat_ref, pair_ref, off_buf):
-    core = ids_ref[0]
+def pack_kernel(npix, ids_ref, maps, upstream, neighbours, own, to2a, to2b, to3a, to3b, off_buf):
+    start, top = maps[0, 0], upstream[0, 0]
+    place = ids_ref[2] * PIX + lax.broadcasted_iota(jnp.int32, (TAPS, PIX), 1)
+    offsets = neighbours[...] - place + HALO
+    offsets = jnp.where(offsets < 0, offsets + npix, offsets)
+    offsets = jnp.where(offsets >= npix, offsets - npix, offsets) - HALO
+    off_buf[...] = jnp.zeros_like(off_buf)
+    off_buf[:TAPS, :PIX] = offsets.astype(F32)
+    tail = off_buf[...].astype(BF)
+    for ref, rows in ((own, (start, top)), (to2a, (start, top[PIX - HALO:])), (to2b, (start, top[:HALO])),
+                      (to3a, (start[PIX - EDGE:],)), (to3b, (start[:EDGE],))):
+        at = 0
+        for value in (*rows, tail):
+            ref[at:at + value.shape[0], :] = value
+            at += value.shape[0]
+
+
+def pack_call(ids, maps, upstream, neighbours):
+    npix = PIX * lax.axis_size("py") * lax.axis_size("core")
+    mine = pl.BlockSpec((1, 1, PIX, C), lambda i, ids: (ids[1], 0, 0, 0))
+    rows = [2 * PIX + OFF, PIX + HALO + OFF, PIX + HALO + OFF, EDGE + OFF, EDGE + OFF]
+    return pl.pallas_call(
+        functools.partial(pack_kernel, npix),
+        grid_spec=pltpu.PrefetchScalarGridSpec(
+            num_scalar_prefetch=1,
+            grid=(1,),
+            in_specs=[mine, mine, pl.BlockSpec((TAPS, PIX), lambda i, ids: (0, 0))],
+            out_specs=[pl.BlockSpec((n, C), lambda i, ids: (0, 0)) for n in rows],
+            scratch_shapes=[pltpu.VMEM((OFF, C), F32)],
+        ),
+        out_shape=[jax.ShapeDtypeStruct((n, C), BF) for n in rows],
+        interpret=INTERPRET,
+        cost_estimate=pl.CostEstimate(flops=0, bytes_accessed=10**6, transcendentals=0),
+    )(ids, maps, upstream, neighbours)
+
+
+def prep_kernel(ids_ref, m3a, m2a, m1a, own, m1b, m2b, m3b, w_own, near_mine, near_other,
+                h_ref, g_ref, s_ref, st_ref, gat_ref, pair_ref, w_ref, off_buf, sems):
+    core, section = ids_ref[0], ids_ref[1]
+    left, right = lax.rem(section + 3, LEVELS), lax.rem(section + 1, LEVELS)
+    copies = []
+    for n, (src, level) in enumerate((
+        (w_own, section),
+        (near_mine, jnp.where(core == 0, left, right)),
+        (near_other, jnp.where(core == 0, right, left)),
+    )):
+        copies.append(pltpu.make_async_copy(src, w_ref.at[level], sems.at[n]))
+        copies[-1].start()
     h_ref[:PAD, :] = jnp.zeros((PAD, C), BF)
     h_ref[ROWS - PAD:, :] = jnp.zeros((PAD, C), BF)
     g_ref[...] = jnp.zeros_like(g_ref)
     off_buf[:PAD, :] = jnp.zeros((PAD, 128), F32)
     off_buf[ROWS - PAD:, :] = jnp.zeros((PAD, 128), F32)
     at = PAD
-    for piece in (m3a, m2a, m1a, own, m1b, m2b, m3b):
-        n = piece.shape[0]
-        h_ref[at:at + n, :] = piece[:, :C]
-        off_buf[at:at + n, :] = piece[:, C:C + 128].astype(F32)
-        if piece.shape[1] > C + 128:
-            g_ref[at:at + n, :] = piece[:, C + 128:]
+    shapes = ((EDGE, PIX - EDGE, 0, 0), (PIX, 0, HALO, PIX - HALO), (PIX, 0, PIX, 0), (PIX, 0, PIX, 0),
+              (PIX, 0, PIX, 0), (PIX, 0, HALO, 0), (EDGE, 0, 0, 0))
+    for piece, (n, first, n_top, first_top) in zip((m3a, m2a, m1a, own, m1b, m2b, m3b), shapes):
+        h_ref[at:at + n, :] = piece[:n, :]
+        if n_top:
+            place = at + first_top
+            g_ref[place:place + n_top, :] = piece[n:n + n_top, :]
+        off_t = jnp.transpose(piece[n + n_top:, :128].astype(F32))
+        off_buf[at:at + n, :OFF] = off_t[first:first + n]
         at += n
 
     rel = (lax.broadcasted_iota(jnp.int32, (TILE, 128), 1)
@@ -100,24 +151,18 @@
              - lax.broadcasted_iota(jnp.int32, (2 * PIX, 2 * PROWS), 1) + HALO).astype(F32)
     for k in range(1, TAPS):
         pair_ref[k - 1] = jnp.where(apart == offt[k:k + 1, :], 1.0, 0.0).astype(BF)
-
-
-def stack_kernel(ids_ref, h0, g_top, s_buf, st_buf, gat0, w_own, near_mine, near_other, far_mine, far_other,
+    for copy in copies:
+        copy.wait()
+
+
+def stack_kernel(ids_ref, h0, g_top, s_buf, st_buf, gat0, w_in, far_mine, far_other,
                  out_ref, w_buf, h_buf, gat, der, pre_buf, g_buf, sems):
     core, section = ids_ref[0], ids_ref[1]
-    left, right = lax.rem(section + 3, LEVELS), lax.rem(section + 1, LEVELS)
-    far = w_buf.at[lax.rem(section + 2, LEVELS)]
-    here = pl.ds(pl.multiple_of(core * HALF, HALF), HALF)
-    there = pl.ds(pl.multiple_of((1 - core) * HALF, HALF), HALF)
+    del w_in
     copies = []
-    for n, (src, dst) in enumerate((
-        (w_own, w_buf.at[section]),
-        (near_mine, w_buf.at[jnp.where(core == 0, left, right)]),
-        (near_other, w_buf.at[jnp.where(core == 0, right, left)]),
-        (far_mine, far.at[here, :]),
-        (far_other, far.at[there, :]),
-    )):
-        copies.append(pltpu.make_async_copy(src, dst, sems.at[n]))
+    for n, (src, half) in enumerate(((far_mine, core), (far_other, 1 - core))):
+        rows = pl.ds(pl.multiple_of(half * HALF, HALF), HALF)
+        copies.append(pltpu.make_async_copy(src, w_buf.at[lax.rem(section + 2, LEVELS), rows, :], sems.at[n]))
         copies[-1].start()
     h_buf[...] = jnp.zeros_like(h_buf)
     pre_buf[...] = jnp.zeros_like(pre_buf)
@@ -207,7 +252,7 @@
 INTERPRET = False
 
 
-def call(kernel, out_shape, in_specs, scratch=(), flops=0, nbytes=0):
+def call(kernel, out_shape, in_specs, scratch=(), flops=0, nbytes=0, aliases=None):
     many = isinstance(out_shape, (tuple, list))
     return pl.pallas_call(
         kernel,
@@ -216,6 +261,7 @@
         out_specs=[VMEM] * len(out_shape) if many else VMEM,
         scratch_shapes=list(scratch),
         interpret=INTERPRET,
+        input_output_aliases=aliases or {},
         cost_estimate=pl.CostEstimate(flops=flops, bytes_accessed=nbytes, transcendentals=0),
         compiler_params=pltpu.CompilerParams(vmem_limit_bytes=28 << 20),
     )
@@ -232,10 +278,11 @@
             jax.ShapeDtypeStruct((BWD_TILES[3][1], hot, 2 * TILE), BF),
             jax.ShapeDtypeStruct((tiles * TILE, TAPS * C), BF),
             jax.ShapeDtypeStruct((TAPS - 1, 2 * PIX, 2 * PROWS), BF),
+            jax.ShapeDtypeStruct((LEVELS, TAPS * C, C), BF),
         ],
-        [SMEM] + [VMEM] * 7,
-        [pltpu.VMEM((ROWS, 128), F32)],
-        flops=10**9, nbytes=6 * 10**6,
+        [SMEM] + [VMEM] * 7 + [ANY] * 3,
+        [pltpu.VMEM((ROWS, 128), F32), pltpu.SemaphoreType.DMA((3,))],
+        flops=10**9, nbytes=12 * 10**6,
     )(*operands)
 
 
@@ -243,18 +290,17 @@
     tiles = FWD_TILES[0][1]
     return call(
         stack_kernel,
-        jax.ShapeDtypeStruct((LEVELS, MSG, C), BF),
-        [SMEM] + [VMEM] * 5 + [ANY] * 5,
+        [jax.ShapeDtypeStruct((LEVELS, MSG, C), BF), jax.ShapeDtypeStruct((LEVELS, TAPS * C, C), BF)],
+        [SMEM] + [VMEM] * 6 + [ANY] * 2,
         [
-            pltpu.VMEM((LEVELS, TAPS * C, C), BF),
             pltpu.VMEM((LEVELS - 1, ROWS, C), BF),
             pltpu.VMEM((tiles * TILE, TAPS * C), BF),
             pltpu.VMEM((LEVELS, tiles * TILE, C), F32),
             pltpu.VMEM((ROWS, C), BF),
             pltpu.VMEM((ROWS, C), BF),
-            pltpu.SemaphoreType.DMA((5,)),
+            pltpu.SemaphoreType.DMA((2,)),
         ],
-        flops=5 * 10**9, nbytes=10 * 10**6,
+        flops=5 * 10**9, nbytes=10 * 10**6, aliases={6: 1},
     )(*operands)
 
 
@@ -268,35 +314,28 @@
     core = lax.axis_index("core")
     patches = lax.axis_size("py") * lax.axis_size("core")
     patch = lax.axis_index("py") * lax.axis_size("core") + core
-    npix = PIX * patches
-    cores = jnp.stack([core, section]).astype(jnp.int32)
+    cores = jnp.stack([core, section, patch]).astype(jnp.int32)
 
     sections = lax.axis_size("section")
     ways = [(2 * i + c, 2 * ((i + (1, -1)[c]) % sections) + c) for i in range(sections) for c in range(2)]
     near = lax.ppermute(weights[0], ("section", "core"), ways)
     half = lax.dynamic_slice_in_dim(near, core * HALF, HALF)
     far = lax.ppermute(half, ("section", "core"), ways)
-    parts = []
-    for block in (near, far):
-        parts += [block, lax.ppermute(block, "core", shift(2, 1))]
-
-    place = patch * PIX + jnp.arange(PIX, dtype=jnp.int32)
-    offsets = jnp.mod(neighbours - place[None, :] + HALO, npix) - HALO
-    offsets = jnp.pad(offsets.astype(BF).T, ((0, 0), (0, 128 - TAPS)))
-    start = lax.dynamic_index_in_dim(maps, section, 0, keepdims=False)[0]
-    top = lax.dynamic_index_in_dim(upstream, section, 0, keepdims=False)[0]
-    own = jnp.concatenate([start, offsets, top], axis=1)
-    edge = 2 * HALO
+    near_other = lax.ppermute(near, "core", shift(2, 1))
+    far_other = lax.ppermute(far, "core", shift(2, 1))
+
+    own, to2a, to2b, to3a, to3b = pack_call(cores, maps, upstream, neighbours)
     send = functools.partial(lax.ppermute, axis_name=("py", "core"))
     m1a = send(own, perm=shift(patches, 1))
     m1b = send(own, perm=shift(patches, -1))
-    m2a = send(own, perm=shift(patches, 2))
-    m2b = send(own, perm=shift(patches, -2))
-    m3a = send(own[PIX - edge:, :C + 128], perm=shift(patches, 3))
-    m3b = send(own[:edge, :C + 128], perm=shift(patches, -3))
-
-    *window, hot = prep_call(cores, m3a, m2a, m1a, own, m1b, m2b, m3b)
-    out = stack_call(cores, *window, weights[0], *parts)
+    m2a = send(to2a, perm=shift(patches, 2))
+    m2b = send(to2b, perm=shift(patches, -2))
+    m3a = send(to3a, perm=shift(patches, 3))
+    m3b = send(to3b, perm=shift(patches, -3))
+
+    h0, g_top, s_hot, st_hot, gat0, hot, w_all = prep_call(
+        cores, m3a, m2a, m1a, own, m1b, m2b, m3b, weights[0], near, near_other)
+    out, _ = stack_call(cores, h0, g_top, s_hot, st_hot, gat0, w_all, far, far_other)
 
     mine = lax.all_to_all(out, "section", 0, 0, tiled=True)
     other = lax.ppermute(mine[:, :HROWS + PROWS], "core", shift(2, 1))
@@ -319,8 +358,14 @@
     )(pieces)
     full = lax.all_to_all(total, ("dp", "py"), 0, 0, tiled=True).reshape((rows, 128))
     swapped = lax.ppermute(full, "core", shift(2, 1))
-    summed = call(
-        join_kernel, jax.ShapeDtypeStruct((TAPS * C, C), BF), [SMEM, VMEM, VMEM], nbytes=2 * 10**6,
+    block = pl.BlockSpec((C, 128), lambda i: (i, 0))
+    summed = pl.pallas_call(
+        join_kernel,
+        grid=(TAPS,),
+        out_shape=jax.ShapeDtypeStruct((TAPS * C, C), BF),
+        in_specs=[SMEM, block, block],
+        out_specs=pl.BlockSpec((C, C), lambda i: (i, 0)),
+        interpret=INTERPRET,
     )(cores, full, swapped)
     return (gin[None, :, None], summed[None])
 

time: 167 us -> 177 us (1.060)
  starting transfers between devices: 55.4 us -> 46.8 us
  waiting for transfers between devices: 19.6 us -> 28 us
  Pallas kernels: 21 us -> 28.2 us
  blocking collectives: 67.4 us -> 69.6 us
    ppermute x1, waiting for transfers between devices: 0.27 us -> 9.1 us  [step(): far = lax.ppermute(half, ('section', 'core'), ways)]
    pallas_call x2 -> x3, Pallas kernels: 13.9 us -> 20.3 us  [the longest x1 12.3 us: stack_call(): call(stack_kernel, [jax.ShapeDtypeStruct((LEVELS, MSG, C), BF), jax.Shape...]
    ppermute x6, starting transfers between devices: 30.3 us -> 26.8 us  [the longest x1 9.6 us: step(): near_other = lax.ppermute(near, 'core', shift(2, 1))]
    ppermute x1, starting transfers between devices: 4.91 us -> 1.92 us  [step(): far = lax.ppermute(half, ('section', 'core'), ways)]
    ppermute x1, starting transfers between devices: 6.46 us -> 3.91 us  [step(): other = lax.ppermute(mine[:, :HROWS + PROWS], 'core', shift(2, 1))]
    unnamed x6 -> x10, local copies, waits for them, and re-layouts: 0.02 us -> 2.38 us
    all_to_all x1, blocking collectives: 10 us -> 12.2 us  [step(): mine = lax.all_to_all(out, 'section', 0, 0, tiled=True)]
  transfers between devices with their start and end apart: 12 -> 12, of which waited for: 6 -> 6; matrix products, arithmetic and copies ran while one was open for 1% -> 0% of each run, Pallas kernels for 2% -> 4%
where the time goes in v6:
time: 177 us
  blocking collectives  69.6 us (39%)
  starting transfers between devices  46.8 us (26%)
  Pallas kernels  28.2 us (16%)
  waiting for transfers between devices  28 us (16%)
  local copies, waits for them, and re-layouts  2.45 us (1%)
    all_to_all x1, blocking collectives, step(): lax.all_to_all(part.reshape((chips, rows // chips, 128)), ('dp', 'py'), 0...  31.9 us
    all_to_all x1, blocking collectives, step(): lax.all_to_all(total, ('dp', 'py'), 0, 0, tiled=True).reshape((rows, 128))  25.5 us
    ppermute x1, waiting for transfers between devices, step(): near = lax.ppermute(weights[0], ('section', 'core'), ways)  13.4 us
    pallas_call x1, Pallas kernels, stack_call(): call(stack_kernel, [jax.ShapeDtypeStruct((LEVELS, MSG, C), BF), jax.Shape...  12.3 us
    all_to_all x1, blocking collectives, step(): mine = lax.all_to_all(out, 'section', 0, 0, tiled=True)  12.2 us
    ppermute x1, starting transfers between devices, step(): near_other = lax.ppermute(near, 'core', shift(2, 1))  9.6 us
    ppermute x1, waiting for transfers between devices, step(): far = lax.ppermute(half, ('section', 'core'), ways)  9.1 us
    ppermute x1, starting transfers between devices, step(): swapped = lax.ppermute(full, 'core', shift(2, 1))  6.34 us
  transfers between devices with their start and end apart: 12, of which 6 were waited for; matrix products, arithmetic and copies ran while one was open for 0% of the time, Pallas kernels for 4%

profile of v6, /device:TPU:1, one launch (start us, length us, event | category | flops | bytes accessed | tf_op | source)
XLA Modules:
  0.0 176.5 jit_solution(16490318281914189316)
XLA Ops:
  0.6 5.3 %collective-permute-start.6 = (bf16[2304,256]{1,0:T(8,128)(2,1)}, bf16[2304,256]{1,0:T(8,128)(2,1)S(1)}, u32[]{:S(2)}, u32[]{:S(2)}) collective-permute-start(bf16[2304,256]{1,0:T(8,128)(2,1)} %bitcast.10), channel_id=1, source_target_pairs={{0,16},{1,49},{16,32},{17,1},{32,48},{33,17},{48,0},{49,33},{2,18}... | collective-permute-start | bytes 3538952 | tf_op jit(solution)/shard_map/ppermute | solution.py:321
  6.0 13.4 %collective-permute-done.6.near_mine = bf16[2304,256]{1,0:T(8,128)(2,1)S(1)} collective-permute-done((bf16[2304,256]{1,0:T(8,128)(2,1)}, bf16[2304,256]{1,0:T(8,128)(2,1)S(1)}, u32[]{:S(2)}, u32[]{:S(2)}) %collective-permute-start.6) | collective-permute-done | bytes 1179680 | tf_op jit(solution)/shard_map/ppermute | solution.py:321
  19.4 9.6 %collective-permute-start.7 = (bf16[2304,256]{1,0:T(8,128)(2,1)S(1)}, bf16[2304,256]{1,0:T(8,128)(2,1)S(1)}, u32[]{:S(2)}, u32[]{:S(2)}) collective-permute-start(bf16[2304,256]{1,0:T(8,128)(2,1)S(1)} %collective-permute-done.6.near_mine), channel_id=1, source_target_pairs={{0,1},{1,0},{2,3},{3,2},{4,5},{5,4},{6,7},{7,6},{8,9},{9,8},{10,11... | collective-permute-start | bytes 3538952 | tf_op jit(solution)/shard_map/ppermute | solution.py:324
  29.1 1.9 %collective-permute-start.8 = (bf16[1152,256]{1,0:T(8,128)(2,1)S(1)}, bf16[1152,256]{1,0:T(8,128)(2,1)}, u32[]{:S(2)}, u32[]{:S(2)}) collective-permute-start(bf16[1152,256]{1,0:T(8,128)(2,1)S(1)} %constant_dynamic-slice_fusion), channel_id=1, source_target_pairs={{0,16},{1,49},{16,32},{17,1},{32,48},{33,17},{48,0},{49,33},{2,18}... | collective-permute-start | bytes 1769480 | tf_op jit(solution)/shard_map/ppermute | solution.py:323
  31.0 9.1 %collective-permute-done.8.far_mine = bf16[1152,256]{1,0:T(8,128)(2,1)} collective-permute-done((bf16[1152,256]{1,0:T(8,128)(2,1)S(1)}, bf16[1152,256]{1,0:T(8,128)(2,1)}, u32[]{:S(2)}, u32[]{:S(2)}) %collective-permute-start.8) | collective-permute-done | bytes 589856 | tf_op jit(solution)/shard_map/ppermute | solution.py:323
  40.1 4.0 %collective-permute-start.9 = (bf16[1152,256]{1,0:T(8,128)(2,1)}, bf16[1152,256]{1,0:T(8,128)(2,1)}, u32[]{:S(2)}, u32[]{:S(2)}) collective-permute-start(bf16[1152,256]{1,0:T(8,128)(2,1)} %collective-permute-done.8.far_mine), channel_id=1, source_target_pairs={{0,1},{1,0},{2,3},{3,2},{4,5},{5,4},{6,7},{7,6},{8,9},{9,8},{10,11... | collective-permute-start | bytes 1769480 | tf_op jit(solution)/shard_map/ppermute | solution.py:325
  44.7 2.2 %shard_map.59 = (bf16[208,256]{1,0:T(8,128)(2,1)}, bf16[144,256]{1,0:T(8,128)(2,1)}, bf16[144,256]{1,0:T(8,128)(2,1)}, bf16[80,256]{1,0:T(8,128)(2,1)}, bf16[80,256]{1,0:T(8,128)(2,1)}) custom-call(s32[3]{0:T(128)} %pad_add_fusion.ids_ref.core_ref, bf16[4,1,96,256]{3,2,1,0:T(8,128)(2,1)} %maps.1, bf16[4,1,96,256]{3,2,1,0:T(8,128)(2,1)} %upstream.1, ...), custom_call_target="tpu_custom_call" | custom-call | bytes 1000000 | tf_op jit(solution)/shard_map/pallas_call | solution.py:82
  47.0 1.9 %collective-permute-start = (bf16[80,256]{1,0:T(8,128)(2,1)}, bf16[80,256]{1,0:T(8,128)(2,1)S(1)}, u32[]{:S(2)}, u32[]{:S(2)}) collective-permute-start(bf16[80,256]{1,0:T(8,128)(2,1)} %get-tuple-element.17), channel_id=1, source_target_pairs={{0,3},{1,4},{2,5},{3,6},{4,7},{5,8},{6,9},{7,10},{8,11},{9,12},{10... | collective-permute-start | bytes 122888 | tf_op jit(solution)/shard_map/ppermute | solution.py:333
  48.9 1.9 %collective-permute-start.1 = (bf16[144,256]{1,0:T(8,128)(2,1)}, bf16[144,256]{1,0:T(8,128)(2,1)S(1)}, u32[]{:S(2)}, u32[]{:S(2)}) collective-permute-start(bf16[144,256]{1,0:T(8,128)(2,1)} %get-tuple-element.18), channel_id=1, source_target_pairs={{0,2},{1,3},{2,4},{3,5},{4,6},{5,7},{6,8},{7,9},{8,10},{9,11},{10,... | collective-permute-start | bytes 221192 | tf_op jit(solution)/shard_map/ppermute | solution.py:331
  50.8 4.9 %collective-permute-start.5 = (bf16[80,256]{1,0:T(8,128)(2,1)}, bf16[80,256]{1,0:T(8,128)(2,1)S(1)}, u32[]{:S(2)}, u32[]{:S(2)}) collective-permute-start(bf16[80,256]{1,0:T(8,128)(2,1)} %get-tuple-element.21), channel_id=1, source_target_pairs={{0,13},{1,14},{2,15},{3,0},{4,1},{5,2},{6,3},{7,4},{8,5},{9,6},{10... | collective-permute-start | bytes 122888 | tf_op jit(solution)/shard_map/ppermute | solution.py:334
  57.2 1.6 collective-permute-start.2
  58.8 4.5 %collective-permute-start.4 = (bf16[144,256]{1,0:T(8,128)(2,1)}, bf16[144,256]{1,0:T(8,128)(2,1)S(1)}, u32[]{:S(2)}, u32[]{:S(2)}) collective-permute-start(bf16[144,256]{1,0:T(8,128)(2,1)} %get-tuple-element.20), channel_id=1, source_target_pairs={{0,14},{1,15},{2,0},{3,1},{4,2},{5,3},{6,4},{7,5},{8,6},{9,7},{10,... | collective-permute-start | bytes 221192 | tf_op jit(solution)/shard_map/ppermute | solution.py:332
  63.3 1.7 collective-permute-done.4.m2b
  66.6 4.6 %shard_map.60 = (bf16[672,256]{1,0:T(8,128)(2,1)S(1)}, bf16[672,256]{1,0:T(8,128)(2,1)S(1)}, bf16[9,512,128]{2,1,0:T(8,128)(2,1)S(1)}, bf16[7,512,128]{2,1,0:T(8...) custom-call(s32[3]{0:T(128)S(1)} %copy-done.2, ...), custom_call_target="tpu_custom_call" | custom-call | flops 1000000000 | bytes 12000000 | tf_op jit(solution)/shard_map/pallas_call | solution.py:272
  71.2 12.3 %shard_map.61 = (bf16[4,320,256]{2,1,0:T(8,128)(2,1)S(1)}, bf16[4,2304,256]{2,1,0:T(8,128)(2,1)S(1)}) custom-call(s32[3]{0:T(128)S(1)} %copy-done.2, bf16[672,256]{1,0:T(8,128)(2,1)S(1)} %get-tuple-element.22.h0, bf16[672,256]{1,0:T(8,128)(2,1)S(1)} %get-tuple-element.23.g_top, ...), custom_call_target="tpu_custom_call", output_to_operand_aliasing={{1}: (6, {})} | custom-call | flops 5000000000 | bytes 10000000 | tf_op jit(solution)/shard_map/pallas_call | solution.py:291
  83.4 12.2 %all_to_all.15.mine = bf16[4,320,256]{2,1,0:T(8,128)(2,1)S(1)} all-to-all(bf16[4,320,256]{2,1,0:T(8,128)(2,1)S(1)} %get-tuple-element.28), channel_id=1, replica_groups=mesh['dp'=8,'section'=4,'py'=8,'core'=2] {'section'}, dimensions={0} | all-to-all | bytes 1310720 | tf_op jit(solution)/shard_map/all_to_all | solution.py:340
  95.7 3.9 %collective-permute-start.10 = (bf16[4,224,256]{2,1,0:T(8,128)(2,1)S(1)}, bf16[4,224,256]{2,1,0:T(8,128)(2,1)S(1)}, u32[]{:S(2)}, u32[]{:S(2)}) collective-permute-start(bf16[4,224,256]{2,1,0:T(8,128)(2,1)S(1)} %slice.4), channel_id=1, source_target_pairs={{0,1},{1,0},{2,3},{3,2},{4,5},{5,4},{6,7},{7,6},{8,9},{9,8},{10,11... | collective-permute-start | bytes 1376264 | tf_op jit(solution)/shard_map/ppermute | solution.py:341
  99.6 1.4 collective-permute-done.10.other
  101.0 3.3 %shard_map.62 = (bf16[2560,128]{1,0:T(8,128)(2,1)S(1)}, bf16[4,96,256]{2,1,0:T(8,128)(2,1)}) custom-call(s32[3]{0:T(128)S(1)} %copy-done.2, bf16[4,320,256]{2,1,0:T(8,128)(2,1)S(1)} %all_to_all.15.mine, bf16[4,224,256]{2,1,0:T(8,128)(2,1)S(1)} %collective-permute-done.10.other, bf16[8,192,256]{2,1,0:T(8,128)(2,1)S(1)} %get-tuple-element.29.hot), custom_call_target="tpu_custom_call" | custom-call | flops 1000000000 | bytes 2000000 | tf_op jit(solution)/shard_map/pallas_call | solution.py:344
  104.3 31.9 %all_to_all.16.x_ref = bf16[64,40,128]{2,1,0:T(8,128)(2,1)S(1)} all-to-all(bf16[64,40,128]{2,1,0:T(8,128)(2,1)S(1)} %bitcast.12), channel_id=1, replica_groups=mesh['dp'=8,'section'=4,'py'=8,'core'=2] {'dp','py'}, dimensions={0} | all-to-all | bytes 1310720 | tf_op jit(solution)/shard_map/all_to_all | solution.py:355
  136.3 25.5 %all_to_all.17 = bf16[64,40,128]{2,1,0:T(8,128)(2,1)S(1)} all-to-all(bf16[64,40,128]{2,1,0:T(8,128)(2,1)S(1)} %shard_map.63), channel_id=1, replica_groups=mesh['dp'=8,'section'=4,'py'=8,'core'=2] {'dp','py'}, dimensions={0} | all-to-all | bytes 1310720 | tf_op jit(solution)/shard_map/all_to_all | solution.py:359
  161.9 6.3 %collective-permute-start.11 = (bf16[2560,128]{1,0:T(8,128)(2,1)S(1)}, bf16[2560,128]{1,0:T(8,128)(2,1)S(1)}, u32[]{:S(2)}, u32[]{:S(2)}) collective-permute-start(bf16[2560,128]{1,0:T(8,128)(2,1)S(1)} %bitcast.13), channel_id=1, source_target_pairs={{0,1},{1,0},{2,3},{3,2},{4,5},{5,4},{6,7},{7,6},{8,9},{9,8},{10,11... | collective-permute-start | bytes 1966088 | tf_op jit(solution)/shard_map/ppermute | solution.py:360
  168.2 1.7 collective-permute-done.11.other
  170.8 5.8 %shard_map.64 = bf16[2304,256]{1,0:T(8,128)(2,1)} custom-call(s32[3]{0:T(128)} %pad_add_fusion.ids_ref.core_ref, bf16[2560,128]{1,0:T(8,128)(2,1)} %bitcast.14, bf16[2560,128]{1,0:T(8,128)(2,1)} %copy-done.4), custom_call_target="tpu_custom_call" | custom-call | tf_op jit(solution)/shard_map/pallas_call | solution.py:362
  (22 shorter events, 4.8 us)
Async XLA Ops:
  0.6 64.4 %copy-start = (bf16[1,2304,256]{2,1,0:T(8,128)(2,1)S(1)}, bf16[1,2304,256]{2,1,0:T(8,128)(2,1)}, u32[]{:S(2)}) copy-start(bf16[1,2304,256]{2,1,0:T(8,128)(2,1)} %param.6) | copy-start | bytes 3538948
  0.6 18.8 %collective-permute-start.6 = (bf16[2304,256]{1,0:T(8,128)(2,1)}, bf16[2304,256]{1,0:T(8,128)(2,1)S(1)}, u32[]{:S(2)}, u32[]{:S(2)}) collective-permute-start(bf16[2304,256]{1,0:T(8,128)(2,1)} %bitcast.10), channel_id=1, source_target_pairs={{0,16},{1,49},{16,32},{17,1},{32,48},{33,17},{48,0},{49,33},{2,18}... | collective-permute-start | bytes 3538952 | tf_op jit(solution)/shard_map/ppermute | solution.py:321
  19.4 45.6 %collective-permute-start.7 = (bf16[2304,256]{1,0:T(8,128)(2,1)S(1)}, bf16[2304,256]{1,0:T(8,128)(2,1)S(1)}, u32[]{:S(2)}, u32[]{:S(2)}) collective-permute-start(bf16[2304,256]{1,0:T(8,128)(2,1)S(1)} %collective-permute-done.6.near_mine), channel_id=1, source_target_pairs={{0,1},{1,0},{2,3},{3,2},{4,5},{5,4},{6,7},{7,6},{8,9},{9,8},{10,11... | collective-permute-start | bytes 3538952 | tf_op jit(solution)/shard_map/ppermute | solution.py:324
  29.1 11.0 %collective-permute-start.8 = (bf16[1152,256]{1,0:T(8,128)(2,1)S(1)}, bf16[1152,256]{1,0:T(8,128)(2,1)}, u32[]{:S(2)}, u32[]{:S(2)}) collective-permute-start(bf16[1152,256]{1,0:T(8,128)(2,1)S(1)} %constant_dynamic-slice_fusion), channel_id=1, source_target_pairs={{0,16},{1,49},{16,32},{17,1},{32,48},{33,17},{48,0},{49,33},{2,18}... | collective-permute-start | bytes 1769480 | tf_op jit(solution)/shard_map/ppermute | solution.py:323
  40.1 31.0 %collective-permute-start.9 = (bf16[1152,256]{1,0:T(8,128)(2,1)}, bf16[1152,256]{1,0:T(8,128)(2,1)}, u32[]{:S(2)}, u32[]{:S(2)}) collective-permute-start(bf16[1152,256]{1,0:T(8,128)(2,1)} %collective-permute-done.8.far_mine), channel_id=1, source_target_pairs={{0,1},{1,0},{2,3},{3,2},{4,5},{5,4},{6,7},{7,6},{8,9},{9,8},{10,11... | collective-permute-start | bytes 1769480 | tf_op jit(solution)/shard_map/ppermute | solution.py:325
  47.0 8.7 %collective-permute-start = (bf16[80,256]{1,0:T(8,128)(2,1)}, bf16[80,256]{1,0:T(8,128)(2,1)S(1)}, u32[]{:S(2)}, u32[]{:S(2)}) collective-permute-start(bf16[80,256]{1,0:T(8,128)(2,1)} %get-tuple-element.17), channel_id=1, source_target_pairs={{0,3},{1,4},{2,5},{3,6},{4,7},{5,8},{6,9},{7,10},{8,11},{9,12},{10... | collective-permute-start | bytes 122888 | tf_op jit(solution)/shard_map/ppermute | solution.py:333
  48.9 9.9 %collective-permute-start.1 = (bf16[144,256]{1,0:T(8,128)(2,1)}, bf16[144,256]{1,0:T(8,128)(2,1)S(1)}, u32[]{:S(2)}, u32[]{:S(2)}) collective-permute-start(bf16[144,256]{1,0:T(8,128)(2,1)} %get-tuple-element.18), channel_id=1, source_target_pairs={{0,2},{1,3},{2,4},{3,5},{4,6},{5,7},{6,8},{7,9},{8,10},{9,11},{10,... | collective-permute-start | bytes 221192 | tf_op jit(solution)/shard_map/ppermute | solution.py:331
  50.8 6.4 %collective-permute-start.5 = (bf16[80,256]{1,0:T(8,128)(2,1)}, bf16[80,256]{1,0:T(8,128)(2,1)S(1)}, u32[]{:S(2)}, u32[]{:S(2)}) collective-permute-start(bf16[80,256]{1,0:T(8,128)(2,1)} %get-tuple-element.21), channel_id=1, source_target_pairs={{0,13},{1,14},{2,15},{3,0},{4,1},{5,2},{6,3},{7,4},{8,5},{9,6},{10... | collective-permute-start | bytes 122888 | tf_op jit(solution)/shard_map/ppermute | solution.py:334
  55.7 9.4 %collective-permute-start.3 = (bf16[208,256]{1,0:T(8,128)(2,1)}, bf16[208,256]{1,0:T(8,128)(2,1)S(1)}, u32[]{:S(2)}, u32[]{:S(2)}) collective-permute-start(bf16[208,256]{1,0:T(8,128)(2,1)} %get-tuple-element.19.own), channel_id=1, source_target_pairs={{0,15},{1,0},{2,1},{3,2},{4,3},{5,4},{6,5},{7,6},{8,7},{9,8},{10,9... | collective-permute-start | bytes 319496 | tf_op jit(solution)/shard_map/ppermute | solution.py:330
  57.2 7.8 %collective-permute-start.2 = (bf16[208,256]{1,0:T(8,128)(2,1)}, bf16[208,256]{1,0:T(8,128)(2,1)S(1)}, u32[]{:S(2)}, u32[]{:S(2)}) collective-permute-start(bf16[208,256]{1,0:T(8,128)(2,1)} %get-tuple-element.19.own), channel_id=1, source_target_pairs={{0,1},{1,2},{2,3},{3,4},{4,5},{5,6},{6,7},{7,8},{8,9},{9,10},{10,1... | collective-permute-start | bytes 319496 | tf_op jit(solution)/shard_map/ppermute | solution.py:329
  58.8 6.2 %collective-permute-start.4 = (bf16[144,256]{1,0:T(8,128)(2,1)}, bf16[144,256]{1,0:T(8,128)(2,1)S(1)}, u32[]{:S(2)}, u32[]{:S(2)}) collective-permute-start(bf16[144,256]{1,0:T(8,128)(2,1)} %get-tuple-element.20), channel_id=1, source_target_pairs={{0,14},{1,15},{2,0},{3,1},{4,2},{5,3},{6,4},{7,5},{8,6},{9,7},{10,... | collective-permute-start | bytes 221192 | tf_op jit(solution)/shard_map/ppermute | solution.py:332
  65.0 0.9 copy-start.1
  65.9 0.6 copy-start.2
  95.7 5.3 %collective-permute-start.10 = (bf16[4,224,256]{2,1,0:T(8,128)(2,1)S(1)}, bf16[4,224,256]{2,1,0:T(8,128)(2,1)S(1)}, u32[]{:S(2)}, u32[]{:S(2)}) collective-permute-start(bf16[4,224,256]{2,1,0:T(8,128)(2,1)S(1)} %slice.4), channel_id=1, source_target_pairs={{0,1},{1,0},{2,3},{3,2},{4,5},{5,4},{6,7},{7,6},{8,9},{9,8},{10,11... | collective-permute-start | bytes 1376264 | tf_op jit(solution)/shard_map/ppermute | solution.py:341
  161.9 8.1 %copy-start.3 = (bf16[64,40,128]{2,1,0:T(8,128)(2,1)}, bf16[64,40,128]{2,1,0:T(8,128)(2,1)S(1)}, u32[]{:S(2)}) copy-start(bf16[64,40,128]{2,1,0:T(8,128)(2,1)S(1)} %all_to_all.17) | copy-start | bytes 1966084
  161.9 8.1 %collective-permute-start.11 = (bf16[2560,128]{1,0:T(8,128)(2,1)S(1)}, bf16[2560,128]{1,0:T(8,128)(2,1)S(1)}, u32[]{:S(2)}, u32[]{:S(2)}) collective-permute-start(bf16[2560,128]{1,0:T(8,128)(2,1)S(1)} %bitcast.13), channel_id=1, source_target_pairs={{0,1},{1,0},{2,3},{3,2},{4,5},{5,4},{6,7},{7,6},{8,9},{9,8},{10,11... | collective-permute-start | bytes 1966088 | tf_op jit(solution)/shard_map/ppermute | solution.py:360
  169.9 0.9 copy-start.4

commit v7 on v6

--- a/solution.py
+++ b/solution.py
@@ -24,8 +24,10 @@
 F32 = jnp.float32
 NT = (((1,), (1,)), ((), ()))
 
+FWD_ROWS = ((32, 576), (64, 544), (96, 512), (128, 480))
 FWD_TILES = ((0, 9), (1, 9), (1, 8), (2, 8))
 PRE_ROWS = ((224, 384), (192, 416), (160, 448), (128, 480))
+BWD_ROWS = ((256, 352), (224, 384), (192, 416), (160, 448))
 BWD_TILES = ((4, 6), (3, 6), (3, 7), (2, 7))
 EDGE = 2 * HALO
 OFF = 16
@@ -94,7 +96,7 @@
     )(ids, maps, upstream, neighbours)
 
 
-def prep_kernel(ids_ref, m3a, m2a, m1a, own, m1b, m2b, m3b, w_own, near_mine, near_other,
+def prep_kernel(ids_ref, m3a, m2a, m1a, own, m1b, m2b, m3b, w_own, near_mine,
                 h_ref, g_ref, s_ref, st_ref, gat_ref, pair_ref, w_ref, off_buf, sems):
     core, section = ids_ref[0], ids_ref[1]
     left, right = lax.rem(section + 3, LEVELS), lax.rem(section + 1, LEVELS)
@@ -102,7 +104,6 @@
     for n, (src, level) in enumerate((
         (w_own, section),
         (near_mine, jnp.where(core == 0, left, right)),
-        (near_other, jnp.where(core == 0, right, left)),
     )):
         copies.append(pltpu.make_async_copy(src, w_ref.at[level], sems.at[n]))
         copies[-1].start()
@@ -155,14 +156,18 @@
         copy.wait()
 
 
-def stack_kernel(ids_ref, h0, g_top, s_buf, st_buf, gat0, w_in, far_mine, far_other,
+def stack_kernel(ids_ref, h0, g_top, s_buf, st_buf, gat0, w_in, near_other, far_mine, far_other,
                  out_ref, w_buf, h_buf, gat, der, pre_buf, g_buf, sems):
     core, section = ids_ref[0], ids_ref[1]
     del w_in
+    far = w_buf.at[lax.rem(section + 2, LEVELS)]
     copies = []
-    for n, (src, half) in enumerate(((far_mine, core), (far_other, 1 - core))):
-        rows = pl.ds(pl.multiple_of(half * HALF, HALF), HALF)
-        copies.append(pltpu.make_async_copy(src, w_buf.at[lax.rem(section + 2, LEVELS), rows, :], sems.at[n]))
+    for n, (src, dst) in enumerate((
+        (near_other, w_buf.at[lax.rem(section + 1 + 2 * core, LEVELS)]),
+        (far_mine, far.at[pl.ds(pl.multiple_of(core * HALF, HALF), HALF), :]),
+        (far_other, far.at[pl.ds(pl.multiple_of((1 - core) * HALF, HALF), HALF), :]),
+    )):
+        copies.append(pltpu.make_async_copy(src, dst, sems.at[n]))
         copies[-1].start()
     h_buf[...] = jnp.zeros_like(h_buf)
     pre_buf[...] = jnp.zeros_like(pre_buf)
@@ -177,7 +182,7 @@
         rows = gat0 if level == 0 else gat
         if level:
             expand_all(gat, first, last, src, s_buf, 3)
-        lo, hi = first * TILE, last * TILE
+        lo, hi = FWD_ROWS[level]
         act = jnp.dot(rows[lo:hi, :], w_buf[level], preferred_element_type=F32)
         squash = jnp.tanh(act)
         der[level, lo:hi, :] = 1.0 - squash * squash
@@ -192,7 +197,7 @@
         first, last = BWD_TILES[level]
 
         expand_all(gat, first, last, pre_buf, st_buf, 3)
-        lo, hi = first * TILE, last * TILE
+        lo, hi = BWD_ROWS[level]
         total = g_buf[PAD + lo:PAD + hi, :].astype(F32)
         for k in range(TAPS):
             total = total + lax.dot_general(gat[lo:hi, k * C:(k + 1) * C],
@@ -226,9 +231,12 @@
         else:
             spread = jnp.dot(hot[k - 1], pre, preferred_element_type=F32).astype(BF)
         for m in range(micro):
-            t_buf[m * pair:(m + 1) * pair, :] = spread[:, m * 128:(m + 1) * 128]
-        block = jnp.dot(h_t, t_buf[...], preferred_element_type=F32)
-        out_ref[k * C:(k + 1) * C, :] = block.astype(BF)
+            t_buf[m * pair:(m + 1) * pair, k * 128:(k + 1) * 128] = spread[:, m * 128:(m + 1) * 128]
+        if k % 2 or k == TAPS - 1:
+            low = k - k % 2 if k < TAPS - 1 else k
+            block = jnp.dot(h_t, t_buf[:, low * 128:(k + 1) * 128], preferred_element_type=F32).astype(BF)
+            for j in range(low, k + 1):
+                out_ref[j * C:(j + 1) * C, :] = block[:, (j - low) * 128:(j - low + 1) * 128]
     out_ref[TAPS * C:, :] = jnp.zeros((out_ref.shape[0] - TAPS * C, 128), BF)
 
 
@@ -280,8 +288,8 @@
             jax.ShapeDtypeStruct((TAPS - 1, 2 * PIX, 2 * PROWS), BF),
             jax.ShapeDtypeStruct((LEVELS, TAPS * C, C), BF),
         ],
-        [SMEM] + [VMEM] * 7 + [ANY] * 3,
-        [pltpu.VMEM((ROWS, 128), F32), pltpu.SemaphoreType.DMA((3,))],
+        [SMEM] + [VMEM] * 7 + [ANY] * 2,
+        [pltpu.VMEM((ROWS, 128), F32), pltpu.SemaphoreType.DMA((2,))],
         flops=10**9, nbytes=12 * 10**6,
     )(*operands)
 
@@ -291,14 +299,14 @@
     return call(
         stack_kernel,
         [jax.ShapeDtypeStruct((LEVELS, MSG, C), BF), jax.ShapeDtypeStruct((LEVELS, TAPS * C, C), BF)],
-        [SMEM] + [VMEM] * 6 + [ANY] * 2,
+        [SMEM] + [VMEM] * 6 + [ANY] * 3,
         [
             pltpu.VMEM((LEVELS - 1, ROWS, C), BF),
             pltpu.VMEM((tiles * TILE, TAPS * C), BF),
             pltpu.VMEM((LEVELS, tiles * TILE, C), F32),
             pltpu.VMEM((ROWS, C), BF),
             pltpu.VMEM((ROWS, C), BF),
-            pltpu.SemaphoreType.DMA((2,)),
+            pltpu.SemaphoreType.DMA((3,)),
         ],
         flops=5 * 10**9, nbytes=10 * 10**6, aliases={6: 1},
     )(*operands)
@@ -326,16 +334,13 @@
 
     own, to2a, to2b, to3a, to3b = pack_call(cores, maps, upstream, neighbours)
     send = functools.partial(lax.ppermute, axis_name=("py", "core"))
-    m1a = send(own, perm=shift(patches, 1))
-    m1b = send(own, perm=shift(patches, -1))
-    m2a = send(to2a, perm=shift(patches, 2))
-    m2b = send(to2b, perm=shift(patches, -2))
-    m3a = send(to3a, perm=shift(patches, 3))
-    m3b = send(to3b, perm=shift(patches, -3))
-
+    sends = []
+    for block, by in ((to2b, -2), (own, -1), (own, 1), (to2a, 2), (to3b, -3), (to3a, 3)):
+        sends.append(send(block, perm=shift(patches, by)))
+    m2b, m1b, m1a, m2a, m3b, m3a = sends
     h0, g_top, s_hot, st_hot, gat0, hot, w_all = prep_call(
-        cores, m3a, m2a, m1a, own, m1b, m2b, m3b, weights[0], near, near_other)
-    out, _ = stack_call(cores, h0, g_top, s_hot, st_hot, gat0, w_all, far, far_other)
+        cores, m3a, m2a, m1a, own, m1b, m2b, m3b, weights[0], near)
+    out, _ = stack_call(cores, h0, g_top, s_hot, st_hot, gat0, w_all, near_other, far, far_other)
 
     mine = lax.all_to_all(out, "section", 0, 0, tiled=True)
     other = lax.ppermute(mine[:, :HROWS + PROWS], "core", shift(2, 1))
@@ -348,7 +353,7 @@
         [
             pltpu.VMEM((2 * PROWS, micro * 128), BF),
             pltpu.VMEM((micro * 2 * PIX, C), BF),
-            pltpu.VMEM((micro * 2 * PIX, 128), BF),
+            pltpu.VMEM((micro * 2 * PIX, TAPS * 128), BF),
         ],
         flops=10**9, nbytes=2 * 10**6,
     )(cores, mine, other, hot)
@@ -358,14 +363,8 @@
     )(pieces)
     full = lax.all_to_all(total, ("dp", "py"), 0, 0, tiled=True).reshape((rows, 128))
     swapped = lax.ppermute(full, "core", shift(2, 1))
-    block = pl.BlockSpec((C, 128), lambda i: (i, 0))
-    summed = pl.pallas_call(
-        join_kernel,
-        grid=(TAPS,),
-        out_shape=jax.ShapeDtypeStruct((TAPS * C, C), BF),
-        in_specs=[SMEM, block, block],
-        out_specs=pl.BlockSpec((C, C), lambda i: (i, 0)),
-        interpret=INTERPRET,
+    summed = call(
+        join_kernel, jax.ShapeDtypeStruct((TAPS * C, C), BF), [SMEM, VMEM, VMEM], nbytes=2 * 10**6,
     )(cores, full, swapped)
     return (gin[None, :, None], summed[None])
 

time: 177 us -> 169 us (0.955)
  waiting for transfers between devices: 28 us -> 19.1 us
  starting transfers between devices: 46.8 us -> 53.8 us
  Pallas kernels: 28.2 us -> 22.5 us
    ppermute x1, waiting for transfers between devices: 9.1 us -> 0.19 us  [step(): far = lax.ppermute(half, ('section', 'core'), ways)]
    ppermute x1, starting transfers between devices: 3.98 us -> 11 us  [step(): far_other = lax.ppermute(far, 'core', shift(2, 1))]
    pallas_call x1, Pallas kernels: 5.76 us -> 1.77 us  [step(): call(join_kernel, jax.ShapeDtypeStruct((TAPS * C, C), BF), [SMEM, VMEM, V...]
    ppermute x1, starting transfers between devices: 1.92 us -> 4.92 us  [step(): far = lax.ppermute(half, ('section', 'core'), ways)]
    ppermute x1, starting transfers between devices: 9.6 us -> 6.61 us  [step(): near_other = lax.ppermute(near, 'core', shift(2, 1))]
where the time goes in v7:
time: 169 us; the launch traced here: 168 us
  blocking collectives  69.6 us (41%)
  starting transfers between devices  53.8 us (32%)
  Pallas kernels  22.5 us (13%)
  waiting for transfers between devices  19.1 us (11%)
    all_to_all x1, blocking collectives, step(): lax.all_to_all(part.reshape((chips, rows // chips, 128)), ('dp', 'py'), 0...  31.9 us
    all_to_all x1, blocking collectives, step(): lax.all_to_all(total, ('dp', 'py'), 0, 0, tiled=True).reshape((rows, 128))  25.5 us
    ppermute x6, starting transfers between devices, step(): sends.append(send(block, perm=shift(patches, by)))  15.7 us
    ppermute x1, waiting for transfers between devices, step(): near = lax.ppermute(weights[0], ('section', 'core'), ways)  13.4 us
    all_to_all x1, blocking collectives, step(): mine = lax.all_to_all(out, 'section', 0, 0, tiled=True)  12.2 us
    pallas_call x1, Pallas kernels, stack_call(): call(stack_kernel, [jax.ShapeDtypeStruct((LEVELS, MSG, C), BF), jax.Shape...  12.2 us
    ppermute x1, starting transfers between devices, step(): far_other = lax.ppermute(far, 'core', shift(2, 1))  11 us
    ppermute x1, starting transfers between devices, step(): near_other = lax.ppermute(near, 'core', shift(2, 1))  6.61 us
  transfers between devices with their start and end apart: 12, of which 6 were waited for; matrix products, arithmetic and copies ran while one was open for 0% of the time, Pallas kernels for 4%

profile of v7, /device:TPU:1, one launch (start us, length us, event | category | flops | bytes accessed | tf_op | source)
XLA Modules:
  0.0 168.1 jit_solution(16979126396473417241)
XLA Ops:
  0.6 5.3 %collective-permute-start.6 = (bf16[2304,256]{1,0:T(8,128)(2,1)}, bf16[2304,256]{1,0:T(8,128)(2,1)S(1)}, u32[]{:S(2)}, u32[]{:S(2)}) collective-permute-start(bf16[2304,256]{1,0:T(8,128)(2,1)} %bitcast.13), channel_id=1, source_target_pairs={{0,16},{1,49},{16,32},{17,1},{32,48},{33,17},{48,0},{49,33},{2,18}... | collective-permute-start | bytes 3538952 | tf_op jit(solution)/shard_map/ppermute | solution.py:329
  6.0 13.4 %collective-permute-done.6.near_mine = bf16[2304,256]{1,0:T(8,128)(2,1)S(1)} collective-permute-done((bf16[2304,256]{1,0:T(8,128)(2,1)}, bf16[2304,256]{1,0:T(8,128)(2,1)S(1)}, u32[]{:S(2)}, u32[]{:S(2)}) %collective-permute-start.6) | collective-permute-done | bytes 1179680 | tf_op jit(solution)/shard_map/ppermute | solution.py:329
  19.5 4.9 %collective-permute-start.8 = (bf16[1152,256]{1,0:T(8,128)(2,1)S(1)}, bf16[1152,256]{1,0:T(8,128)(2,1)}, u32[]{:S(2)}, u32[]{:S(2)}) collective-permute-start(bf16[1152,256]{1,0:T(8,128)(2,1)S(1)} %constant_dynamic-slice_fusion), channel_id=1, source_target_pairs={{0,16},{1,49},{16,32},{17,1},{32,48},{33,17},{48,0},{49,33},{2,18}... | collective-permute-start | bytes 1769480 | tf_op jit(solution)/shard_map/ppermute | solution.py:331
  24.4 6.6 %collective-permute-start.7 = (bf16[2304,256]{1,0:T(8,128)(2,1)S(1)}, bf16[2304,256]{1,0:T(8,128)(2,1)S(1)}, u32[]{:S(2)}, u32[]{:S(2)}) collective-permute-start(bf16[2304,256]{1,0:T(8,128)(2,1)S(1)} %collective-permute-done.6.near_mine), channel_id=1, source_target_pairs={{0,1},{1,0},{2,3},{3,2},{4,5},{5,4},{6,7},{7,6},{8,9},{9,8},{10,11... | collective-permute-start | bytes 3538952 | tf_op jit(solution)/shard_map/ppermute | solution.py:332
  31.2 11.0 %collective-permute-start.9 = (bf16[1152,256]{1,0:T(8,128)(2,1)}, bf16[1152,256]{1,0:T(8,128)(2,1)}, u32[]{:S(2)}, u32[]{:S(2)}) collective-permute-start(bf16[1152,256]{1,0:T(8,128)(2,1)} %collective-permute-done.8.far_mine), channel_id=1, source_target_pairs={{0,1},{1,0},{2,3},{3,2},{4,5},{5,4},{6,7},{7,6},{8,9},{9,8},{10,11... | collective-permute-start | bytes 1769480 | tf_op jit(solution)/shard_map/ppermute | solution.py:333
  42.8 2.2 %shard_map.59 = (bf16[208,256]{1,0:T(8,128)(2,1)}, bf16[144,256]{1,0:T(8,128)(2,1)}, bf16[144,256]{1,0:T(8,128)(2,1)}, bf16[80,256]{1,0:T(8,128)(2,1)}, bf16[80,256]{1,0:T(8,128)(2,1)}) custom-call(s32[3]{0:T(128)} %pad_add_fusion.ids_ref.core_ref, bf16[4,1,96,256]{3,2,1,0:T(8,128)(2,1)} %maps.1, bf16[4,1,96,256]{3,2,1,0:T(8,128)(2,1)} %upstream.1, ...), custom_call_target="tpu_custom_call" | custom-call | bytes 1000000 | tf_op jit(solution)/shard_map/pallas_call | solution.py:84
  45.1 1.9 %collective-permute-start = (bf16[80,256]{1,0:T(8,128)(2,1)}, bf16[80,256]{1,0:T(8,128)(2,1)S(1)}, u32[]{:S(2)}, u32[]{:S(2)}) collective-permute-start(bf16[80,256]{1,0:T(8,128)(2,1)} %get-tuple-element.17), channel_id=1, source_target_pairs={{0,3},{1,4},{2,5},{3,6},{4,7},{5,8},{6,9},{7,10},{8,11},{9,12},{10... | collective-permute-start | bytes 122888 | tf_op jit(solution)/shard_map/ppermute | solution.py:339
  47.0 1.9 %collective-permute-start.1 = (bf16[144,256]{1,0:T(8,128)(2,1)}, bf16[144,256]{1,0:T(8,128)(2,1)S(1)}, u32[]{:S(2)}, u32[]{:S(2)}) collective-permute-start(bf16[144,256]{1,0:T(8,128)(2,1)} %get-tuple-element.18), channel_id=1, source_target_pairs={{0,2},{1,3},{2,4},{3,5},{4,6},{5,7},{6,8},{7,9},{8,10},{9,11},{10,... | collective-permute-start | bytes 221192 | tf_op jit(solution)/shard_map/ppermute | solution.py:339
  48.9 4.9 %collective-permute-start.5 = (bf16[80,256]{1,0:T(8,128)(2,1)}, bf16[80,256]{1,0:T(8,128)(2,1)S(1)}, u32[]{:S(2)}, u32[]{:S(2)}) collective-permute-start(bf16[80,256]{1,0:T(8,128)(2,1)} %get-tuple-element.21), channel_id=1, source_target_pairs={{0,13},{1,14},{2,15},{3,0},{4,1},{5,2},{6,3},{7,4},{8,5},{9,6},{10... | collective-permute-start | bytes 122888 | tf_op jit(solution)/shard_map/ppermute | solution.py:339
  53.8 0.9 collective-permute-start.3
  55.3 1.6 collective-permute-start.2
  56.9 4.5 %collective-permute-start.4 = (bf16[144,256]{1,0:T(8,128)(2,1)}, bf16[144,256]{1,0:T(8,128)(2,1)S(1)}, u32[]{:S(2)}, u32[]{:S(2)}) collective-permute-start(bf16[144,256]{1,0:T(8,128)(2,1)} %get-tuple-element.20), channel_id=1, source_target_pairs={{0,14},{1,15},{2,0},{3,1},{4,2},{5,3},{6,4},{7,5},{8,6},{9,7},{10,... | collective-permute-start | bytes 221192 | tf_op jit(solution)/shard_map/ppermute | solution.py:339
  61.4 1.7 %collective-permute-done.4.m2b = bf16[144,256]{1,0:T(8,128)(2,1)S(1)} collective-permute-done((bf16[144,256]{1,0:T(8,128)(2,1)}, bf16[144,256]{1,0:T(8,128)(2,1)S(1)}, u32[]{:S(2)}, u32[]{:S(2)}) %collective-permute-start.4) | collective-permute-done | bytes 73760 | tf_op jit(solution)/shard_map/ppermute | solution.py:339
  64.7 4.3 %shard_map.60 = (bf16[672,256]{1,0:T(8,128)(2,1)S(1)}, bf16[672,256]{1,0:T(8,128)(2,1)S(1)}, bf16[9,512,128]{2,1,0:T(8,128)(2,1)S(1)}, bf16[7,512,128]{2,1,0:T(8...) custom-call(s32[3]{0:T(128)S(1)} %copy-done, ...), custom_call_target="tpu_custom_call" | custom-call | flops 1000000000 | bytes 12000000 | tf_op jit(solution)/shard_map/pallas_call | solution.py:280
  69.0 12.2 %shard_map.61 = (bf16[4,320,256]{2,1,0:T(8,128)(2,1)S(1)}, bf16[4,2304,256]{2,1,0:T(8,128)(2,1)S(1)}) custom-call(s32[3]{0:T(128)S(1)} %copy-done, bf16[672,256]{1,0:T(8,128)(2,1)S(1)} %get-tuple-element.22.h0, bf16[672,256]{1,0:T(8,128)(2,1)S(1)} %get-tuple-element.23.g_top, ...), custom_call_target="tpu_custom_call", output_to_operand_aliasing={{1}: (6, {})} | custom-call | flops 5000000000 | bytes 10000000 | tf_op jit(solution)/shard_map/pallas_call | solution.py:299
  81.2 12.2 %all_to_all.15.mine = bf16[4,320,256]{2,1,0:T(8,128)(2,1)S(1)} all-to-all(bf16[4,320,256]{2,1,0:T(8,128)(2,1)S(1)} %get-tuple-element.28), channel_id=1, replica_groups=mesh['dp'=8,'section'=4,'py'=8,'core'=2] {'section'}, dimensions={0} | all-to-all | bytes 1310720 | tf_op jit(solution)/shard_map/all_to_all | solution.py:345
  93.5 3.9 %collective-permute-start.10 = (bf16[4,224,256]{2,1,0:T(8,128)(2,1)S(1)}, bf16[4,224,256]{2,1,0:T(8,128)(2,1)S(1)}, u32[]{:S(2)}, u32[]{:S(2)}) collective-permute-start(bf16[4,224,256]{2,1,0:T(8,128)(2,1)S(1)} %slice.4), channel_id=1, source_target_pairs={{0,1},{1,0},{2,3},{3,2},{4,5},{5,4},{6,7},{7,6},{8,9},{9,8},{10,11... | collective-permute-start | bytes 1376264 | tf_op jit(solution)/shard_map/ppermute | solution.py:346
  97.4 1.4 collective-permute-done.10.other
  98.9 1.9 %shard_map.62 = (bf16[2560,128]{1,0:T(8,128)(2,1)S(1)}, bf16[4,96,256]{2,1,0:T(8,128)(2,1)}) custom-call(s32[3]{0:T(128)S(1)} %copy-done, bf16[4,320,256]{2,1,0:T(8,128)(2,1)S(1)} %all_to_all.15.mine, bf16[4,224,256]{2,1,0:T(8,128)(2,1)S(1)} %collective-permute-done.10.other, bf16[8,192,256]{2,1,0:T(8,128)(2,1)S(1)} %get-tuple-element.29.hot), custom_call_target="tpu_custom_call" | custom-call | flops 1000000000 | bytes 2000000 | tf_op jit(solution)/shard_map/pallas_call | solution.py:349
  100.7 31.9 %all_to_all.16.x_ref = bf16[64,40,128]{2,1,0:T(8,128)(2,1)S(1)} all-to-all(bf16[64,40,128]{2,1,0:T(8,128)(2,1)S(1)} %bitcast.12), channel_id=1, replica_groups=mesh['dp'=8,'section'=4,'py'=8,'core'=2] {'dp','py'}, dimensions={0} | all-to-all | bytes 1310720 | tf_op jit(solution)/shard_map/all_to_all | solution.py:360
  132.7 25.5 %all_to_all.17 = bf16[64,40,128]{2,1,0:T(8,128)(2,1)S(1)} all-to-all(bf16[64,40,128]{2,1,0:T(8,128)(2,1)S(1)} %shard_map.63), channel_id=1, replica_groups=mesh['dp'=8,'section'=4,'py'=8,'core'=2] {'dp','py'}, dimensions={0} | all-to-all | bytes 1310720 | tf_op jit(solution)/shard_map/all_to_all | solution.py:364
  158.3 6.3 %collective-permute-start.11 = (bf16[2560,128]{1,0:T(8,128)(2,1)S(1)}, bf16[2560,128]{1,0:T(8,128)(2,1)S(1)}, u32[]{:S(2)}, u32[]{:S(2)}) collective-permute-start(bf16[2560,128]{1,0:T(8,128)(2,1)S(1)} %bitcast.10), channel_id=1, source_target_pairs={{0,1},{1,0},{2,3},{3,2},{4,5},{5,4},{6,7},{7,6},{8,9},{9,8},{10,11... | collective-permute-start | bytes 1966088 | tf_op jit(solution)/shard_map/ppermute | solution.py:365
  164.6 1.7 %collective-permute-done.11.other = bf16[2560,128]{1,0:T(8,128)(2,1)S(1)} collective-permute-done((bf16[2560,128]{1,0:T(8,128)(2,1)S(1)}, bf16[2560,128]{1,0:T(8,128)(2,1)S(1)}, u32[]{:S(2)}, u32[]{:S(2)}) %collective-permute-start.11) | collective-permute-done | bytes 655392 | tf_op jit(solution)/shard_map/ppermute | solution.py:365
  166.3 1.8 %shard_map.64 = bf16[2304,256]{1,0:T(8,128)(2,1)} custom-call(s32[3]{0:T(128)S(1)} %copy-done.1, bf16[2560,128]{1,0:T(8,128)(2,1)S(1)} %bitcast.11, bf16[2560,128]{1,0:T(8,128)(2,1)S(1)} %collective-permute-done.11.other), custom_call_target="tpu_custom_call" | custom-call | bytes 2000000 | tf_op jit(solution)/shard_map/pallas_call | solution.py:366
  (20 shorter events, 3.3 us)
Async XLA Ops:
  0.6 62.5 %copy-start.2 = (bf16[1,2304,256]{2,1,0:T(8,128)(2,1)S(1)}, bf16[1,2304,256]{2,1,0:T(8,128)(2,1)}, u32[]{:S(2)}) copy-start(bf16[1,2304,256]{2,1,0:T(8,128)(2,1)} %param.6) | copy-start | bytes 3538948
  0.6 18.8 %collective-permute-start.6 = (bf16[2304,256]{1,0:T(8,128)(2,1)}, bf16[2304,256]{1,0:T(8,128)(2,1)S(1)}, u32[]{:S(2)}, u32[]{:S(2)}) collective-permute-start(bf16[2304,256]{1,0:T(8,128)(2,1)} %bitcast.13), channel_id=1, source_target_pairs={{0,16},{1,49},{16,32},{17,1},{32,48},{33,17},{48,0},{49,33},{2,18}... | collective-permute-start | bytes 3538952 | tf_op jit(solution)/shard_map/ppermute | solution.py:329
  19.5 11.7 %collective-permute-start.8 = (bf16[1152,256]{1,0:T(8,128)(2,1)S(1)}, bf16[1152,256]{1,0:T(8,128)(2,1)}, u32[]{:S(2)}, u32[]{:S(2)}) collective-permute-start(bf16[1152,256]{1,0:T(8,128)(2,1)S(1)} %constant_dynamic-slice_fusion), channel_id=1, source_target_pairs={{0,16},{1,49},{16,32},{17,1},{32,48},{33,17},{48,0},{49,33},{2,18}... | collective-permute-start | bytes 1769480 | tf_op jit(solution)/shard_map/ppermute | solution.py:331
  24.4 44.6 %collective-permute-start.7 = (bf16[2304,256]{1,0:T(8,128)(2,1)S(1)}, bf16[2304,256]{1,0:T(8,128)(2,1)S(1)}, u32[]{:S(2)}, u32[]{:S(2)}) collective-permute-start(bf16[2304,256]{1,0:T(8,128)(2,1)S(1)} %collective-permute-done.6.near_mine), channel_id=1, source_target_pairs={{0,1},{1,0},{2,3},{3,2},{4,5},{5,4},{6,7},{7,6},{8,9},{9,8},{10,11... | collective-permute-start | bytes 3538952 | tf_op jit(solution)/shard_map/ppermute | solution.py:332
  31.2 37.8 %collective-permute-start.9 = (bf16[1152,256]{1,0:T(8,128)(2,1)}, bf16[1152,256]{1,0:T(8,128)(2,1)}, u32[]{:S(2)}, u32[]{:S(2)}) collective-permute-start(bf16[1152,256]{1,0:T(8,128)(2,1)} %collective-permute-done.8.far_mine), channel_id=1, source_target_pairs={{0,1},{1,0},{2,3},{3,2},{4,5},{5,4},{6,7},{7,6},{8,9},{9,8},{10,11... | collective-permute-start | bytes 1769480 | tf_op jit(solution)/shard_map/ppermute | solution.py:333
  45.1 8.7 %collective-permute-start = (bf16[80,256]{1,0:T(8,128)(2,1)}, bf16[80,256]{1,0:T(8,128)(2,1)S(1)}, u32[]{:S(2)}, u32[]{:S(2)}) collective-permute-start(bf16[80,256]{1,0:T(8,128)(2,1)} %get-tuple-element.17), channel_id=1, source_target_pairs={{0,3},{1,4},{2,5},{3,6},{4,7},{5,8},{6,9},{7,10},{8,11},{9,12},{10... | collective-permute-start | bytes 122888 | tf_op jit(solution)/shard_map/ppermute | solution.py:339
  47.0 9.9 %collective-permute-start.1 = (bf16[144,256]{1,0:T(8,128)(2,1)}, bf16[144,256]{1,0:T(8,128)(2,1)S(1)}, u32[]{:S(2)}, u32[]{:S(2)}) collective-permute-start(bf16[144,256]{1,0:T(8,128)(2,1)} %get-tuple-element.18), channel_id=1, source_target_pairs={{0,2},{1,3},{2,4},{3,5},{4,6},{5,7},{6,8},{7,9},{8,10},{9,11},{10,... | collective-permute-start | bytes 221192 | tf_op jit(solution)/shard_map/ppermute | solution.py:339
  48.9 6.4 %collective-permute-start.5 = (bf16[80,256]{1,0:T(8,128)(2,1)}, bf16[80,256]{1,0:T(8,128)(2,1)S(1)}, u32[]{:S(2)}, u32[]{:S(2)}) collective-permute-start(bf16[80,256]{1,0:T(8,128)(2,1)} %get-tuple-element.21), channel_id=1, source_target_pairs={{0,13},{1,14},{2,15},{3,0},{4,1},{5,2},{6,3},{7,4},{8,5},{9,6},{10... | collective-permute-start | bytes 122888 | tf_op jit(solution)/shard_map/ppermute | solution.py:339
  53.8 9.4 %collective-permute-start.3 = (bf16[208,256]{1,0:T(8,128)(2,1)}, bf16[208,256]{1,0:T(8,128)(2,1)S(1)}, u32[]{:S(2)}, u32[]{:S(2)}) collective-permute-start(bf16[208,256]{1,0:T(8,128)(2,1)} %get-tuple-element.19.own), channel_id=1, source_target_pairs={{0,15},{1,0},{2,1},{3,2},{4,3},{5,4},{6,5},{7,6},{8,7},{9,8},{10,9... | collective-permute-start | bytes 319496 | tf_op jit(solution)/shard_map/ppermute | solution.py:339
  55.3 7.8 %collective-permute-start.2 = (bf16[208,256]{1,0:T(8,128)(2,1)}, bf16[208,256]{1,0:T(8,128)(2,1)S(1)}, u32[]{:S(2)}, u32[]{:S(2)}) collective-permute-start(bf16[208,256]{1,0:T(8,128)(2,1)} %get-tuple-element.19.own), channel_id=1, source_target_pairs={{0,1},{1,2},{2,3},{3,4},{4,5},{5,6},{6,7},{7,8},{8,9},{9,10},{10,1... | collective-permute-start | bytes 319496 | tf_op jit(solution)/shard_map/ppermute | solution.py:339
  56.9 6.2 %collective-permute-start.4 = (bf16[144,256]{1,0:T(8,128)(2,1)}, bf16[144,256]{1,0:T(8,128)(2,1)S(1)}, u32[]{:S(2)}, u32[]{:S(2)}) collective-permute-start(bf16[144,256]{1,0:T(8,128)(2,1)} %get-tuple-element.20), channel_id=1, source_target_pairs={{0,14},{1,15},{2,0},{3,1},{4,2},{5,3},{6,4},{7,5},{8,6},{9,7},{10,... | collective-permute-start | bytes 221192 | tf_op jit(solution)/shard_map/ppermute | solution.py:339
  63.1 0.7 copy-start
  63.8 0.9 copy-start.3
  93.5 5.4 %collective-permute-start.10 = (bf16[4,224,256]{2,1,0:T(8,128)(2,1)S(1)}, bf16[4,224,256]{2,1,0:T(8,128)(2,1)S(1)}, u32[]{:S(2)}, u32[]{:S(2)}) collective-permute-start(bf16[4,224,256]{2,1,0:T(8,128)(2,1)S(1)} %slice.4), channel_id=1, source_target_pairs={{0,1},{1,0},{2,3},{3,2},{4,5},{5,4},{6,7},{7,6},{8,9},{9,8},{10,11... | collective-permute-start | bytes 1376264 | tf_op jit(solution)/shard_map/ppermute | solution.py:346
  132.6 33.7 %copy-start.1 = (s32[3]{0:T(128)S(1)}, s32[3]{0:T(128)}, u32[]{:S(2)}) copy-start(s32[3]{0:T(128)} %pad_add_fusion.ids_ref.core_ref) | copy-start | bytes 40
  158.3 8.1 %collective-permute-start.11 = (bf16[2560,128]{1,0:T(8,128)(2,1)S(1)}, bf16[2560,128]{1,0:T(8,128)(2,1)S(1)}, u32[]{:S(2)}, u32[]{:S(2)}) collective-permute-start(bf16[2560,128]{1,0:T(8,128)(2,1)S(1)} %bitcast.10), channel_id=1, source_target_pairs={{0,1},{1,0},{2,3},{3,2},{4,5},{5,4},{6,7},{7,6},{8,9},{9,8},{10,11... | collective-permute-start | bytes 1966088 | tf_op jit(solution)/shard_map/ppermute | solution.py:365
